TPU v7x, 32 devices: a whole 2x2x4 slice. The times are simulated.
32 devices in a mesh: groups: 2 (over y), tensor: 8 (over z, core), rows: 2 (over x).
Axes of the slice: x: 2, y: 2, z: 4, core: 2. Of those that a mesh axis runs over, the one named last changes fastest.
Arguments:
- queries: bfloat16 [2048, 8192], P(('groups', 'tensor'), 'rows'), parts along dimension 0, may hold values from -32 to 32
- keyvals: bfloat16 [16384, 2048], P(('groups', 'tensor'), 'rows'), parts along dimension 0, may hold values from -6 to 6
- attending: int32 [128, 4], P(('groups', 'tensor')), parts along dimension 0, may hold values from 0 to 7, all different within a row; in each aligned block of 8 rows (0 to 7, 8 to 15, ...) at most 8 rows name the same one
- block_fill: int32 [128], P(('groups', 'tensor')), parts along dimension 0, may hold values from 1 to 128
- out_weight: bfloat16 [8192, 8192], P('rows', 'tensor'), may hold values from -0.0625 to 0.0625
Outputs:
- projected: bfloat16 [2048, 8192], P(('groups', 'rows'), 'tensor'), parts along dimension 0
There are 2 independent parts, one for each index of `groups`. A program takes and returns all parts, laid end to end along the dimension named above; an argument that names none is the same for every part. Nothing has to cross between parts.
Inputs may be any that keep to these rules, and one draw needn't show every extreme that they name: `attending`: each row names 4 different query blocks; among the 8 rows of one index of tensor no query block is named more than 8 times, and every query block is named by some row.
All inputs are finite; a program needn't handle non-finite values.
Results may differ from a plain program's by a relative error of at most 0.0052.
Values may be sent and summed in bfloat16 or wider, within the bound.
No kernel may reach another device: no remote copies, remote signals or barrier semaphores. Data moves between devices by JAX's collectives and lax.ppermute only.
A program may use at most 128 MiB of HBM per device.

v0:
```python
import functools
import math

import jax
import jax.numpy as jnp
from jax import lax
from jax.experimental import pallas as pl
from jax.experimental.pallas import tpu as pltpu
from jax.sharding import PartitionSpec as P


HEAD_WIDTH = 128
BLOCK_TOKENS = 128
masked_low = -1e30
exp2_scale = math.log2(math.e) / math.sqrt(HEAD_WIDTH)
key_group = 4
meta_rows = 16
share = 16


slab_rows = 512


def head_scores(q_heads, key_heads):
    scores = jnp.einsum("hrd,hkd->hrk", q_heads, key_heads, preferred_element_type=jnp.float32)
    return scores * (1.0 / math.sqrt(HEAD_WIDTH))


def fold_keys(q_heads, key_heads, value_heads, visible):
    head_count = key_heads.shape[0]
    row_count = q_heads.shape[1]
    key_count = key_heads.shape[1]
    slab_size = math.gcd(key_count, slab_rows)
    slab_count = key_count // slab_size
    keys_split = jnp.transpose(
        key_heads.reshape(head_count, slab_count, slab_size, HEAD_WIDTH), (1, 0, 2, 3)
    )
    values_split = jnp.transpose(
        value_heads.reshape(head_count, slab_count, slab_size, HEAD_WIDTH), (1, 0, 2, 3)
    )
    visible_split = visible.reshape(slab_count, slab_size)

    def find_top(current, pieces):
        scores = head_scores(q_heads, pieces[0])
        return (
            jnp.maximum(
                current, jnp.max(jnp.where(pieces[1][None, None, :], scores, masked_low), axis=2)
            ),
            None,
        )

    highest, unused = lax.scan(
        find_top,
        jnp.full((head_count, row_count), masked_low, jnp.float32),
        (keys_split, visible_split),
    )

    def accumulate(current, pieces):
        totals, summed = current
        scores = head_scores(q_heads, pieces[0])
        probs = jnp.where(pieces[2][None, None, :], jnp.exp(scores - highest[..., None]), 0.0)
        totals = totals + jnp.sum(probs, axis=2)
        summed = summed + jnp.einsum(
            "hrk,hkd->hrd",
            probs.astype(jnp.bfloat16),
            pieces[1],
            preferred_element_type=jnp.float32,
        )
        return ((totals, summed), None)

    start_state = (
        jnp.zeros((head_count, row_count), jnp.float32),
        jnp.zeros((head_count, row_count, HEAD_WIDTH), jnp.float32),
    )
    final_state, unused = lax.scan(
        accumulate, start_state, (keys_split, values_split, visible_split)
    )
    return final_state[1] / final_state[0][..., None]


def split_heads(kv_rows):
    key_count = kv_rows.shape[0]
    head_count = kv_rows.shape[1] // (2 * HEAD_WIDTH)
    reshaped_tensor = kv_rows.reshape(key_count, head_count, 2, HEAD_WIDTH)
    return (
        jnp.transpose(reshaped_tensor[:, :, 0, :], (1, 0, 2)),
        jnp.transpose(reshaped_tensor[:, :, 1, :], (1, 0, 2)),
    )


def gathered_shards(queries, keyvals, attending, block_fill, out_weight):
    q_len = queries.shape[0]
    head_count = keyvals.shape[1] // (2 * HEAD_WIDTH)
    query_group_width = queries.shape[1] // (HEAD_WIDTH * head_count)
    row_count = q_len * query_group_width
    positions = jnp.arange(BLOCK_TOKENS, dtype=jnp.int32)
    token_ok = positions[None, :] < block_fill[:, None]
    q_heads = jnp.transpose(
        queries.reshape(q_len, head_count, query_group_width, HEAD_WIDTH), (1, 0, 2, 3)
    ).reshape(head_count, row_count, HEAD_WIDTH)
    powers = jnp.sum(jnp.power(2, attending), axis=1).astype(jnp.int32)
    visible_bits = jnp.where(token_ok, powers[:, None], 0).reshape(keyvals.shape[0])
    my_bit = jnp.power(2, lax.axis_index("tensor"))
    all_rows, all_bits = (
        lax.all_gather(keyvals, "tensor", axis=0, tiled=True),
        lax.all_gather(visible_bits, "tensor", axis=0, tiled=True),
    )
    visible = all_bits // my_bit % 2 == 1
    key_heads, value_heads = split_heads(all_rows)
    merged = fold_keys(q_heads, key_heads, value_heads, visible)
    attended_output = jnp.transpose(
        merged.reshape(head_count, q_len, query_group_width, HEAD_WIDTH), (1, 0, 2, 3)
    )
    attended_output = attended_output.reshape(
        q_len, head_count * query_group_width * HEAD_WIDTH
    ).astype(jnp.bfloat16)
    terms = jnp.dot(
        lax.all_gather(attended_output, "tensor", axis=0, tiled=True),
        out_weight,
        preferred_element_type=jnp.float32,
    )
    return lax.psum_scatter(terms, "rows", scatter_dimension=0, tiled=True).astype(jnp.bfloat16)


def attend_kernel(first, last, heads, held, tab, cnt, qb, qk, qp, *refs):
    q_refs, (kv_a, kv_b, *refs) = refs[:4], refs[4:]
    if held:
        acc_in, top_in, *refs = refs
    if last:
        o_ref, kv, s_all, tops, q_rows, sems, acc = refs
    else:
        acc_out, top_out, kv, s_all, tops, q_rows, sems = refs
        acc = acc_out.at[0]
    step = pl.program_id(0)
    width = HEAD_WIDTH
    half = kv_a.shape[0]

    @pl.when(step == 0)
    def _():
        copies = [
            pltpu.make_async_copy(source, kv.at[pl.ds(half * i, half)], sems.at[i])
            for i, source in enumerate((kv_a, kv_b))
        ]
        for copy in copies:
            copy.start()
        for copy in copies:
            copy.wait()

    for which, q_ref in enumerate(q_refs):

        @pl.when(qp[step] == which)
        def _():
            for h in range(heads):
                q_rows[h * BLOCK_TOKENS : (h + 1) * BLOCK_TOKENS] = q_ref[
                    0, :, h * width : (h + 1) * width
                ]

    block = qb[step]
    groups = (cnt[block] + (key_group - 1)) // key_group
    tops[...] = jnp.full_like(tops, masked_low)
    lane = lax.broadcasted_iota(jnp.int32, (1, BLOCK_TOKENS), 1)

    def find(j, carry):
        top = tops[...]
        for p in range(0, key_group, 2):
            entries = [tab[block, j * key_group + p + i] for i in range(2)]
            keys = jnp.concatenate([kv[e // 256, :, :width] for e in entries], axis=0)
            hidden = jnp.concatenate(
                [jnp.where(lane < e % 256, 0.0, masked_low) for e in entries], axis=1
            )
            scores = lax.dot_general(
                q_rows[...], keys, (((1,), (1,)), ((), ())), preferred_element_type=jnp.float32
            )
            scores = scores + hidden
            s_all[j, :, p * BLOCK_TOKENS : (p + 2) * BLOCK_TOKENS] = scores
            top = jnp.maximum(top, jnp.maximum(scores[:, :width], scores[:, width:]))
        tops[...] = top
        return carry

    lax.fori_loop(0, groups, find, 0)
    top = jnp.max(tops[...], axis=1, keepdims=True) * exp2_scale
    top = jnp.broadcast_to(top, tops.shape)
    if first:
        acc[...] = jnp.zeros(acc.shape, jnp.float32)
    else:
        before = top_in[0]
        top = jnp.maximum(top, before)
        fade = jnp.exp2(before - top)
        acc[:, :width] = acc_in[0, :, :width] * fade
        acc[:, width:] = acc_in[0, :, width:] * fade
    tops[...] = top
    if not last:
        top_out[0] = top

    def gather(j, carry):
        entries = [tab[block, j * key_group + p] for p in range(key_group)]
        values = jnp.concatenate([kv[e // 256, :, width:] for e in entries], axis=0)
        values = jnp.concatenate([values, jnp.ones_like(values)], axis=1)
        probs = jnp.concatenate(
            [
                jnp.exp2(
                    s_all[j, :, p * BLOCK_TOKENS : (p + 1) * BLOCK_TOKENS] * exp2_scale - tops[...]
                ).astype(jnp.bfloat16)
                for p in range(key_group)
            ],
            axis=1,
        )
        acc[...] += jnp.dot(probs, values, preferred_element_type=jnp.float32)
        return carry

    lax.fori_loop(0, groups, gather, 0)
    if last:
        for h in range(heads):
            rows = slice(h * BLOCK_TOKENS, (h + 1) * BLOCK_TOKENS)
            o_ref[:, h * width : (h + 1) * width] = (acc[rows, :width] / acc[rows, width:]).astype(
                o_ref.dtype
            )


def attend(lists, at, q_four, kv_own, kv_swap, state=(), first=False, last=False):
    tab, cnt = lists
    qb, qk, qp = at
    count = qb.shape[0]
    width = q_four[0].shape[2]
    heads = width // HEAD_WIDTH
    rows = heads * BLOCK_TOKENS
    blocks = tab.shape[1]
    everyone = cnt.shape[0]
    q_spec = pl.BlockSpec((1, BLOCK_TOKENS, width), lambda i, tab, cnt, qb, qk, qp: (qk[i], 0, 0))
    acc_spec = pl.BlockSpec((1, rows, 2 * HEAD_WIDTH), lambda i, tab, cnt, qb, qk, qp: (qb[i], 0, 0))
    top_spec = pl.BlockSpec((1, rows, HEAD_WIDTH), lambda i, tab, cnt, qb, qk, qp: (qb[i], 0, 0))
    scratch = [
        pltpu.VMEM((blocks, BLOCK_TOKENS, 2 * HEAD_WIDTH), jnp.bfloat16),
        pltpu.VMEM((blocks // key_group, rows, key_group * BLOCK_TOKENS), jnp.float32),
        pltpu.VMEM((rows, HEAD_WIDTH), jnp.float32),
        pltpu.VMEM((rows, HEAD_WIDTH), jnp.bfloat16),
        pltpu.SemaphoreType.DMA((2,)),
    ]
    state_specs = [acc_spec, top_spec]
    if first:
        state_specs = [pl.BlockSpec(memory_space=pl.ANY)] * 2
    if last:
        out_shape = jax.ShapeDtypeStruct((count * BLOCK_TOKENS, width), jnp.bfloat16)
        out_specs = pl.BlockSpec((BLOCK_TOKENS, width), lambda i, *_: (i, 0))
        scratch.append(pltpu.VMEM((rows, 2 * HEAD_WIDTH), jnp.float32))
        aliases = {}
    else:
        out_shape = (
            jax.ShapeDtypeStruct((everyone, rows, 2 * HEAD_WIDTH), jnp.float32),
            jax.ShapeDtypeStruct((everyone, rows, HEAD_WIDTH), jnp.float32),
        )
        out_specs = (acc_spec, top_spec)
        aliases = {11 + i: i for i in range(len(state))}
    shape = (kv_own.shape[0] // BLOCK_TOKENS, BLOCK_TOKENS, kv_own.shape[1])
    work = count * blocks // 2 * rows * BLOCK_TOKENS
    return pl.pallas_call(
        functools.partial(attend_kernel, first, last, heads, bool(state)),
        out_shape=out_shape,
        grid_spec=pltpu.PrefetchScalarGridSpec(
            num_scalar_prefetch=5,
            grid=(count,),
            in_specs=[q_spec] * 4
            + [pl.BlockSpec(memory_space=pl.ANY)] * 2
            + state_specs[: len(state)],
            out_specs=out_specs,
            scratch_shapes=scratch,
        ),
        input_output_aliases=aliases,
        compiler_params=pltpu.CompilerParams(vmem_limit_bytes=60 << 20),
        cost_estimate=pl.CostEstimate(
            flops=work * 4 * HEAD_WIDTH * 4, bytes_accessed=work // 8, transcendentals=work
        ),
        name="attend",
    )(
        tab,
        cnt,
        qb,
        qk,
        qp,
        *q_four,
        kv_own.reshape(shape),
        kv_swap.reshape(shape),
        *state,
    )


def project_kernel(at, middle, mine, near, in_a, in_b, out_a, out_b, w_own, w_swap, *refs):
    own_ref, other_ref, one, two, sems = refs
    column = pl.program_id(0)

    @pl.when(column == 0)
    def _():
        for flag, pair in ((1, (in_a, in_b)), (0, (out_a, out_b))):

            @pl.when(middle[0] == flag)
            def _():
                copies = [
                    pltpu.make_async_copy(pair[0], one, sems.at[0]),
                    pltpu.make_async_copy(pair[1], two, sems.at[1]),
                ]
                for copy in copies:
                    copy.start()
                for copy in copies:
                    copy.wait()

    for w_ref, o_ref in ((w_swap, other_ref), (w_own, own_ref)):
        total = None
        for i, part in enumerate((mine, near, one, two)):
            term = jnp.dot(part[...], w_ref[at[i]], preferred_element_type=jnp.float32)
            total = term if total is None else total + term
        o_ref[...] = total.astype(o_ref.dtype)


def project(at, middle, parts, w_own, w_swap):
    rows, depth = parts[0].shape
    chips, _, columns = w_own.shape
    tile = 256
    whole = pl.BlockSpec((rows, depth), lambda j, *_: (0, 0))
    strip = pl.BlockSpec((rows, tile), lambda j, *_: (0, j))
    result = jax.ShapeDtypeStruct((rows, columns), jnp.bfloat16)
    return pl.pallas_call(
        project_kernel,
        out_shape=(jax.ShapeDtypeStruct((rows, columns), jnp.float32), result),
        grid_spec=pltpu.PrefetchScalarGridSpec(
            num_scalar_prefetch=2,
            grid=(columns // tile,),
            in_specs=[whole, whole]
            + [pl.BlockSpec(memory_space=pl.ANY)] * 4
            + [
                pl.BlockSpec((chips, depth, tile), lambda j, at, middle: (0, at[chips], j)),
                pl.BlockSpec((chips, depth, tile), lambda j, *_: (0, 0, j)),
            ],
            out_specs=(strip, strip),
            scratch_shapes=[
                pltpu.VMEM((rows, depth), jnp.bfloat16),
                pltpu.VMEM((rows, depth), jnp.bfloat16),
                pltpu.SemaphoreType.DMA((2,)),
            ],
        ),
        compiler_params=pltpu.CompilerParams(vmem_limit_bytes=60 << 20),
        cost_estimate=pl.CostEstimate(
            flops=2 * rows * 4 * depth * 2 * columns,
            bytes_accessed=2 * (8 * depth * columns + 6 * rows * depth + 3 * rows * columns),
            transcendentals=0,
        ),
        name="project",
    )(at, middle, *parts, w_own, w_swap)


def apart(k):
    return [(i, i ^ k) for i in range(8)]


def key_lists(meta, blocks):
    chips = meta.shape[0]
    naming = meta[:, :, : 8 * 4].reshape(chips, share, 4)
    fill = meta[:, :, 8 * 4 : 8 * 5].reshape(chips, share)
    wanted = jnp.arange(blocks, dtype=jnp.int32)[None, :, None, None]
    listed = jnp.any(naming[:, None] == wanted, axis=3)
    ones = listed.astype(jnp.int32)
    place = jnp.arange(share, dtype=jnp.int32)
    before = jnp.sum(jnp.where(place[None, :] < place[:, None], ones[:, :, None, :], 0), axis=3)
    entry = place * 256 + fill
    tab = jnp.sum(
        jnp.where(
            listed[..., None] & (before[..., None] == place),
            entry[:, None, :, None],
            0,
        ),
        axis=2,
    )
    return tab, jnp.sum(ones, axis=2)


def permute(array, perm, axis="tensor"):
    return lax.ppermute(array, axis, perm)


def exchanged_shards(queries, keyvals, attending, block_fill, out_weight):
    t = lax.axis_index("tensor")
    z, core = t // 2, t % 2
    row = lax.axis_index("rows")
    chips = 4
    q_len = queries.shape[0]
    wide = queries.shape[1] // chips
    depth = wide // 2
    pair = 2 * HEAD_WIDTH

    def swap(array):
        return permute(array, apart(1))

    meta = jnp.concatenate([attending.reshape(-1), block_fill]).astype(jnp.bfloat16)
    meta = jnp.pad(meta[None, :], ((0, meta_rows - 1), (0, depth - meta.shape[0])))
    meta = jnp.concatenate([meta, meta], axis=1)

    def q_for(chip):
        own = lax.dynamic_slice(queries, (0, chip * wide), (q_len, wide))
        return jnp.concatenate([own, meta], axis=0)

    def kv_for(chip):
        return lax.dynamic_slice(keyvals, (0, chip * pair), (keyvals.shape[0], pair))

    def columns_of(arrays, which):
        size = (q_len + meta_rows, depth)
        return jnp.stack([lax.dynamic_slice(a, (0, which * depth), size) for a in arrays])

    q_come = [q_for(z)]
    for k in range(1, chips):
        q_come.append(permute(q_for(z ^ k), apart(2 * k)))
    kv_own = [kv_for(z)]
    for k in range(1, chips):
        kv_own.append(permute(kv_for(z ^ k), apart(2 * k)))
    kv_swap = [swap(kv_own[k]) for k in range(chips)]

    near_own = columns_of(q_come[:2], core)
    near_swap = swap(columns_of(q_come[:2], 1 - core))
    far_own = columns_of(q_come[2:], core)
    far_swap = swap(columns_of(q_come[2:], 1 - core))
    q_four = [near_own, near_swap, far_own, far_swap]

    def lists_of(own, other):
        notes = jnp.stack([own[:, q_len, :64], other[:, q_len, :64]], axis=1)
        tab, cnt = key_lists(notes.astype(jnp.int32), 2 * chips)
        return [(tab[i], cnt[i]) for i in range(2)]

    lists = lists_of(near_own, near_swap)
    lists, far_notes = lax.optimization_barrier((lists, (far_own, far_swap)))
    lists = lists + lists_of(*far_notes)

    def places(blocks):
        blocks = blocks.astype(jnp.int32)
        k = (blocks // 2) ^ z
        which = 2 * (k // 2) + ((blocks % 2) ^ core)
        return blocks, (k % 2).astype(jnp.int32), which.astype(jnp.int32)

    four = jnp.arange(4, dtype=jnp.int32)
    near = places(4 * (z // 2) + four)
    far = places(4 * (1 - z // 2) + four)
    everything = places(jnp.arange(2 * chips, dtype=jnp.int32))
    q_near = q_four[:2] * 2
    state = attend(lists[0], near, q_near, kv_own[0], kv_swap[0], first=True)
    state = attend(lists[0], far, q_four, kv_own[0], kv_swap[0], state, first=True)
    state = attend(lists[1], everything, q_four, kv_own[1], kv_swap[1], state)
    state = attend(lists[2], everything, q_four, kv_own[2], kv_swap[2], state)

    w_split = out_weight.reshape(chips, 2, depth, out_weight.shape[1])
    w_swap = swap(lax.dynamic_index_in_dim(w_split, 1 - core, 1, keepdims=False))
    w_own = out_weight.reshape(chips, wide, out_weight.shape[1])
    far_chip = jnp.where(z < 2, 2, 1)
    chip_of = jnp.stack([z, z ^ 1, far_chip, far_chip ^ 1])
    at = jnp.concatenate([chip_of, core[None]]).astype(jnp.int32)
    middle = ((z == 1) | (z == 2)).astype(jnp.int32).reshape(1)
    across = [(2, 4), (3, 5), (4, 2), (5, 3)]
    outward = [(2, 0), (3, 1), (4, 6), (5, 7)]
    last = chips - 1

    def chunk(chip):
        pieces = places(2 * chip + jnp.arange(2, dtype=jnp.int32))
        mine = attend(lists[last], pieces, q_four, kv_own[last], kv_swap[last], state, last=True)
        beside = permute(mine, apart(2))
        in_a = permute(mine, across)
        in_b = permute(beside, across)
        out_a = permute(in_a, outward)
        out_b = permute(in_b, outward)
        own, other = project(at, middle, (mine, beside, in_a, in_b, out_a, out_b), w_own, w_swap)
        return own, swap(other)

    theirs = []
    for i in range(2):
        own, come = chunk(2 * (1 - row) + i)
        term = (own + come.astype(jnp.float32)).astype(jnp.bfloat16)
        theirs.append(permute(term, [(0, 1), (1, 0)], "rows"))
    ours = []
    for i in range(2):
        own, come = chunk(2 * row + i)
        ours.append(own + come.astype(jnp.float32) + theirs[i].astype(jnp.float32))
    return jnp.concatenate(ours, axis=0).astype(jnp.bfloat16)


def solution(mesh):
    tensor, rows = mesh.shape["tensor"], mesh.shape["rows"]

    def splits(queries, keyvals):
        return (
            tensor == 8
            and rows == 2
            and keyvals.shape[1] == 4 * 2 * HEAD_WIDTH
            and queries.shape[0] == BLOCK_TOKENS
            and keyvals.shape[0] == 8 * BLOCK_TOKENS
        )

    def shards(queries, keyvals, attending, block_fill, out_weight):
        form = exchanged_shards if splits(queries, keyvals) else gathered_shards
        return form(queries, keyvals, attending, block_fill, out_weight)

    return jax.shard_map(
        shards,
        mesh=mesh,
        in_specs=(
            P(("groups", "tensor"), "rows"),
            P(("groups", "tensor"), "rows"),
            P(("groups", "tensor"), None),
            P(("groups", "tensor")),
            P("rows", "tensor"),
        ),
        out_specs=P(("groups", "rows"), "tensor"),
        check_vma=False,
    )
```

profile of v0, /device:TPU:0, one launch (start us, length us, event | category | flops | bytes accessed | tf_op | source)
XLA Modules:
  0.0 275.6 jit_solution(1186394707410503733)
XLA Ops:
  4.0 4.1 %collective-permute-start.2 = (bf16[144,1024]{1,0:T(8,128)(2,1)}, bf16[144,1024]{1,0:T(8,128)(2,1)}, u32[]{:S(2)}, u32[]{:S(2)}) collective-permute-start(bf16[144,1024]{1,0:T(8,128)(2,1)} %get-tuple-element.65), channel_id=1, source_target_pairs={{0,8},{2,10},{4,12},{6,14},{8,0},{10,2},{12,4},{14,6},{1,9},{3,11}... | collective-permute-start | bytes 884744 | tf_op jit(solution)/shard_map/ppermute | solution.py:376
  8.1 1.3 collective-permute-start.3
  10.9 1.8 collective-permute-start.9
  20.1 4.6 %dynamic-slice_bitcast_fusion = bf16[4,512,1024]{2,1,0:T(8,128)(2,1)} fusion(bf16[4,2,512,1024]{3,2,1,0:T(8,128)(2,1)} %bitcast.56, s32[]{:T(128)S(6)} %select_n.217), kind=kLoop, calls=%fused_computation | loop fusion | bytes 8388612 | tf_op jit(solution)/shard_map/jit(dynamic_index_in_dim)/squeeze | solution.py:447
  24.8 6.3 %collective-permute-done = bf16[144,1024]{1,0:T(8,128)(2,1)} collective-permute-done((bf16[144,1024]{1,0:T(8,128)(2,1)}, bf16[144,1024]{1,0:T(8,128)(2,1)}, u32[]{:S(2)}, u32[]{:S(2)}) %collective-permute-start) | collective-permute-done | bytes 294944 | tf_op jit(solution)/shard_map/ppermute | solution.py:376
  31.1 1.6 collective-permute-start.7
  34.5 1.9 collective-permute-start.5
  41.4 5.3 %collective-permute-done.9 = bf16[1024,256]{1,0:T(8,128)(2,1)} collective-permute-done((bf16[1024,256]{1,0:T(8,128)(2,1)}, bf16[1024,256]{1,0:T(8,128)(2,1)}, u32[]{:S(2)}, u32[]{:S(2)}) %collective-permute-start.9) | collective-permute-done | bytes 524320 | tf_op jit(solution)/shard_map/ppermute | solution.py:376
  46.7 22.9 %collective-permute-done.7 = bf16[1024,256]{1,0:T(8,128)(2,1)} collective-permute-done((bf16[1024,256]{1,0:T(8,128)(2,1)}, bf16[1024,256]{1,0:T(8,128)(2,1)}, u32[]{:S(2)}, u32[]{:S(2)}) %collective-permute-start.7) | collective-permute-done | bytes 524320 | tf_op jit(solution)/shard_map/ppermute | solution.py:376
  71.9 12.0 %attend.8 = (f32[8,512,256]{2,1,0:T(8,128)}, f32[8,512,128]{2,1,0:T(8,128)}) custom-call(s32[8,16]{1,0:T(8,128)} %get-tuple-element.31.tab, s32[8]{0:T(128)} %get-tuple-element.32.cnt, s32[4]{0:T(128)} %iota_add_fusion.3.qb, s32[4]{0:T(128)} %get-tuple-element.83.qk, s32[4]{0:T(128)} %get-tuple-element.84.qp, ...), custom_call_target="tpu_custom_call" | custom-call | flops 4294967296 | bytes 262144 | tf_op jit(solution)/shard_map/attend/pallas_call | solution.py:256
  84.5 10.7 %attend.9 = (f32[8,512,256]{2,1,0:T(8,128)}, f32[8,512,128]{2,1,0:T(8,128)}) custom-call(s32[8,16]{1,0:T(8,128)} %get-tuple-element.31.tab, s32[8]{0:T(128)} %get-tuple-element.32.cnt, s32[4]{0:T(128)} %iota_add_fusion.4.qb, s32[4]{0:T(128)} %get-tuple-element.85.qk, s32[4]{0:T(128)} %get-tuple-element.86.qp, ...), custom_call_target="tpu_custom_call", output_to_operand_aliasing={{0}: (11, {}), {1}: (12, {})} | custom-call | flops 4294967296 | bytes 262144 | tf_op jit(solution)/shard_map/attend/pallas_call | solution.py:256
  95.7 19.3 %attend.10 = (f32[8,512,256]{2,1,0:T(8,128)}, f32[8,512,128]{2,1,0:T(8,128)}) custom-call(s32[8,16]{1,0:T(8,128)} %get-tuple-element.29.tab, s32[8]{0:T(128)} %get-tuple-element.30.cnt, s32[8]{0:T(128)} %iota.52.qb, s32[8]{0:T(128)} %get-tuple-element.87.qk, s32[8]{0:T(128)} %get-tuple-element.88.qp, ...), custom_call_target="tpu_custom_call", output_to_operand_aliasing={{0}: (11, {}), {1}: (12, {})} | custom-call | flops 8589934592 | bytes 524288 | tf_op jit(solution)/shard_map/attend/pallas_call | solution.py:256
  115.8 19.1 %attend.11 = (f32[8,512,256]{2,1,0:T(8,128)}, f32[8,512,128]{2,1,0:T(8,128)}) custom-call(s32[8,16]{1,0:T(8,128)} %get-tuple-element.69.tab, s32[8]{0:T(128)} %get-tuple-element.73.cnt, s32[8]{0:T(128)} %iota.50.qb, s32[8]{0:T(128)} %get-tuple-element.87.qk, s32[8]{0:T(128)} %get-tuple-element.88.qp, ...), custom_call_target="tpu_custom_call", output_to_operand_aliasing={{0}: (11, {}), {1}: (12, {})} | custom-call | flops 8589934592 | bytes 524288 | tf_op jit(solution)/shard_map/attend/pallas_call | solution.py:256
  135.8 6.7 %attend.12.mine = bf16[256,512]{1,0:T(8,128)(2,1)} custom-call(s32[8,16]{1,0:T(8,128)} %get-tuple-element.70.tab, s32[8]{0:T(128)} %get-tuple-element.74.cnt, s32[2]{0:T(128)} %iota_add_fusion.5.qb, s32[2]{0:T(128)} %get-tuple-element.89.qk, s32[2]{0:T(128)} %get-tuple-element.90.qp, bf16[2,144,512]{2,1,0:T(8,128)(2,1)} %pad_maximum_fusion.1.refs_0_.refs_2_, ...), custom_call_target="tpu_custom_call" | custom-call | flops 2147483648 | bytes 131072 | tf_op jit(solution)/shard_map/attend/pallas_call | solution.py:256
  142.5 10.6 %collective-permute-start.12 = (bf16[256,512]{1,0:T(8,128)(2,1)}, bf16[256,512]{1,0:T(8,128)(2,1)S(1)}, u32[]{:S(2)}, u32[]{:S(2)}) collective-permute-start(bf16[256,512]{1,0:T(8,128)(2,1)} %attend.12.mine), channel_id=1, source_target_pairs={{0,4},{2,6},{4,0},{6,2},{8,12},{10,14},{12,8},{14,10},{1,5},{3,7},... | collective-permute-start | bytes 786440 | tf_op jit(solution)/shard_map/ppermute | solution.py:376
  153.8 6.7 %attend.13.mine = bf16[256,512]{1,0:T(8,128)(2,1)} custom-call(s32[8,16]{1,0:T(8,128)} %get-tuple-element.70.tab, s32[8]{0:T(128)} %get-tuple-element.74.cnt, s32[2]{0:T(128)} %iota_add_fusion.2.qb, s32[2]{0:T(128)} %get-tuple-element.81.qk, s32[2]{0:T(128)} %get-tuple-element.82.qp, bf16[2,144,512]{2,1,0:T(8,128)(2,1)} %pad_maximum_fusion.1.refs_0_.refs_2_, ...), custom_call_target="tpu_custom_call" | custom-call | flops 2147483648 | bytes 131072 | tf_op jit(solution)/shard_map/attend/pallas_call | solution.py:256
  160.5 4.7 %collective-permute-start.19 = (bf16[256,512]{1,0:T(8,128)(2,1)}, bf16[256,512]{1,0:T(8,128)(2,1)S(1)}, u32[]{:S(2)}, u32[]{:S(2)}) collective-permute-start(bf16[256,512]{1,0:T(8,128)(2,1)} %attend.13.mine), channel_id=1, source_target_pairs={{0,4},{2,6},{4,0},{6,2},{8,12},{10,14},{12,8},{14,10},{1,5},{3,7},... | collective-permute-start | bytes 786440 | tf_op jit(solution)/shard_map/ppermute | solution.py:376
  166.0 9.3 %attend.14.mine = bf16[256,512]{1,0:T(8,128)(2,1)} custom-call(s32[8,16]{1,0:T(8,128)} %get-tuple-element.70.tab, s32[8]{0:T(128)} %get-tuple-element.74.cnt, s32[2]{0:T(128)} %iota_add_fusion.1.qb, s32[2]{0:T(128)} %get-tuple-element.79.qk, s32[2]{0:T(128)} %get-tuple-element.80.qp, bf16[2,144,512]{2,1,0:T(8,128)(2,1)} %pad_maximum_fusion.1.refs_0_.refs_2_, ...), custom_call_target="tpu_custom_call" | custom-call | flops 2147483648 | bytes 131072 | tf_op jit(solution)/shard_map/attend/pallas_call | solution.py:256
  175.3 8.1 %attend.15.mine = bf16[256,512]{1,0:T(8,128)(2,1)} custom-call(s32[8,16]{1,0:T(8,128)} %get-tuple-element.70.tab, s32[8]{0:T(128)} %get-tuple-element.74.cnt, s32[2]{0:T(128)} %iota_add_fusion.qb, s32[2]{0:T(128)} %get-tuple-element.77.qk, s32[2]{0:T(128)} %get-tuple-element.78.qp, bf16[2,144,512]{2,1,0:T(8,128)(2,1)} %pad_maximum_fusion.1.refs_0_.refs_2_, ...), custom_call_target="tpu_custom_call" | custom-call | flops 2147483648 | bytes 131072 | tf_op jit(solution)/shard_map/attend/pallas_call | solution.py:256
  183.5 2.1 collective-permute-start.26
  187.0 5.7 %collective-permute-done.26.near = bf16[256,512]{1,0:T(8,128)(2,1)S(1)} collective-permute-done((bf16[256,512]{1,0:T(8,128)(2,1)S(1)}, bf16[256,512]{1,0:T(8,128)(2,1)S(1)}, u32[]{:S(2)}, u32[]{:S(2)}) %collective-permute-start.26) | collective-permute-done | bytes 262176 | tf_op jit(solution)/shard_map/ppermute | solution.py:376
  194.0 4.3 %collective-permute-done.32.near = bf16[256,512]{1,0:T(8,128)(2,1)S(1)} collective-permute-done((bf16[256,512]{1,0:T(8,128)(2,1)}, bf16[256,512]{1,0:T(8,128)(2,1)S(1)}, u32[]{:S(2)}, u32[]{:S(2)}) %collective-permute-start.32) | collective-permute-done | bytes 262176 | tf_op jit(solution)/shard_map/ppermute | solution.py:376
  200.3 1.4 collective-permute-start.27
  203.8 1.4 collective-permute-start.28
  205.2 2.9 %collective-permute-done.23.out_b = bf16[256,512]{1,0:T(8,128)(2,1)} collective-permute-done((bf16[256,512]{1,0:T(8,128)(2,1)S(1)}, bf16[256,512]{1,0:T(8,128)(2,1)}, u32[]{:S(2)}, u32[]{:S(2)}) %collective-permute-start.23) | collective-permute-done | bytes 262176 | tf_op jit(solution)/shard_map/ppermute | solution.py:376
  210.7 8.4 %project.5 = (f32[256,1024]{1,0:T(8,128)}, bf16[256,1024]{1,0:T(8,128)(2,1)}) custom-call(s32[5]{0:T(128)} %concatenate.37.at, s32[1]{0:T(128)} %bitcast.5.middle, bf16[256,512]{1,0:T(8,128)(2,1)} %attend.13.mine, bf16[256,512]{1,0:T(8,128)(2,1)} %copy-done.16, bf16[256,512]{1,0:T(8,128)(2,1)} %copy-done.17, bf16[256,512]{1,0:T(8,128)(2,1)} %copy-done.21, ...), custom_call_target="tpu_custom_call" | custom-call | flops 2147483648 | bytes 11534336 | tf_op jit(solution)/shard_map/project/pallas_call | solution.py:321
  224.8 8.4 %project.7 = (f32[256,1024]{1,0:T(8,128)}, bf16[256,1024]{1,0:T(8,128)(2,1)}) custom-call(s32[5]{0:T(128)} %concatenate.37.at, s32[1]{0:T(128)} %bitcast.5.middle, bf16[256,512]{1,0:T(8,128)(2,1)} %attend.15.mine, bf16[256,512]{1,0:T(8,128)(2,1)} %copy-done.15, bf16[256,512]{1,0:T(8,128)(2,1)} %copy-done.18, bf16[256,512]{1,0:T(8,128)(2,1)} %copy-done.19, ...), custom_call_target="tpu_custom_call" | custom-call | flops 2147483648 | bytes 11534336 | tf_op jit(solution)/shard_map/project/pallas_call | solution.py:321
  233.7 4.6 %collective-permute-done.16.out_b = bf16[256,512]{1,0:T(8,128)(2,1)S(1)} collective-permute-done((bf16[256,512]{1,0:T(8,128)(2,1)S(1)}, bf16[256,512]{1,0:T(8,128)(2,1)S(1)}, u32[]{:S(2)}, u32[]{:S(2)}) %collective-permute-start.16) | collective-permute-done | bytes 262176 | tf_op jit(solution)/shard_map/ppermute | solution.py:376
  239.0 8.4 %project.4 = (f32[256,1024]{1,0:T(8,128)}, bf16[256,1024]{1,0:T(8,128)(2,1)}) custom-call(s32[5]{0:T(128)} %concatenate.37.at, s32[1]{0:T(128)} %bitcast.5.middle, bf16[256,512]{1,0:T(8,128)(2,1)} %attend.12.mine, bf16[256,512]{1,0:T(8,128)(2,1)} %copy-done.12, bf16[256,512]{1,0:T(8,128)(2,1)} %copy-done.13, bf16[256,512]{1,0:T(8,128)(2,1)} %copy-done.20, ...), custom_call_target="tpu_custom_call" | custom-call | flops 2147483648 | bytes 11534336 | tf_op jit(solution)/shard_map/project/pallas_call | solution.py:321
  250.6 8.4 %project.6 = (f32[256,1024]{1,0:T(8,128)}, bf16[256,1024]{1,0:T(8,128)(2,1)}) custom-call(s32[5]{0:T(128)} %concatenate.37.at, s32[1]{0:T(128)} %bitcast.5.middle, bf16[256,512]{1,0:T(8,128)(2,1)} %attend.14.mine, bf16[256,512]{1,0:T(8,128)(2,1)} %copy-done.14, bf16[256,512]{1,0:T(8,128)(2,1)} %collective-permute-done.27.in_a, ...), custom_call_target="tpu_custom_call" | custom-call | flops 2147483648 | bytes 11534336 | tf_op jit(solution)/shard_map/project/pallas_call | solution.py:321
  260.2 3.3 %collective-permute-done.25 = bf16[256,1024]{1,0:T(8,128)(2,1)S(1)} collective-permute-done((bf16[256,1024]{1,0:T(8,128)(2,1)}, bf16[256,1024]{1,0:T(8,128)(2,1)S(1)}, u32[]{:S(2)}, u32[]{:S(2)}) %collective-permute-start.25) | collective-permute-done | bytes 524320 | tf_op jit(solution)/shard_map/ppermute | solution.py:376
  263.8 10.5 %collective-permute-done.38 = bf16[256,1024]{1,0:T(8,128)(2,1)S(1)} collective-permute-done((bf16[256,1024]{1,0:T(8,128)(2,1)S(1)}, bf16[256,1024]{1,0:T(8,128)(2,1)S(1)}, u32[]{:S(2)}, u32[]{:S(2)}) %collective-permute-start.38) | collective-permute-done | bytes 524320 | tf_op jit(solution)/shard_map/ppermute | solution.py:376
  (186 shorter events, 47.8 us)
Async XLA Ops:
  4.0 30.5 %collective-permute-start.2 = (bf16[144,1024]{1,0:T(8,128)(2,1)}, bf16[144,1024]{1,0:T(8,128)(2,1)}, u32[]{:S(2)}, u32[]{:S(2)}) collective-permute-start(bf16[144,1024]{1,0:T(8,128)(2,1)} %get-tuple-element.65), channel_id=1, source_target_pairs={{0,8},{2,10},{4,12},{6,14},{8,0},{10,2},{12,4},{14,6},{1,9},{3,11}... | collective-permute-start | bytes 884744 | tf_op jit(solution)/shard_map/ppermute | solution.py:376
  8.1 29.4 %collective-permute-start.3 = (bf16[144,1024]{1,0:T(8,128)(2,1)}, bf16[144,1024]{1,0:T(8,128)(2,1)}, u32[]{:S(2)}, u32[]{:S(2)}) collective-permute-start(bf16[144,1024]{1,0:T(8,128)(2,1)} %get-tuple-element.67), channel_id=1, source_target_pairs={{0,12},{2,14},{4,8},{6,10},{8,4},{10,6},{12,0},{14,2},{1,13},{3,15... | collective-permute-start | bytes 884744 | tf_op jit(solution)/shard_map/ppermute | solution.py:376
  9.4 21.7 %collective-permute-start = (bf16[144,1024]{1,0:T(8,128)(2,1)}, bf16[144,1024]{1,0:T(8,128)(2,1)}, u32[]{:S(2)}, u32[]{:S(2)}) collective-permute-start(bf16[144,1024]{1,0:T(8,128)(2,1)} %get-tuple-element.66), channel_id=1, source_target_pairs={{0,4},{2,6},{4,0},{6,2},{8,12},{10,14},{12,8},{14,10},{1,5},{3,7},... | collective-permute-start | bytes 884744 | tf_op jit(solution)/shard_map/ppermute | solution.py:376
  10.9 61.0 %collective-permute-start.11 = (bf16[1024,256]{1,0:T(8,128)(2,1)S(1)}, bf16[1024,256]{1,0:T(8,128)(2,1)}, u32[]{:S(2)}, u32[]{:S(2)}) collective-permute-start(bf16[1024,256]{1,0:T(8,128)(2,1)S(1)} %get-tuple-element.49), channel_id=1, source_target_pairs={{0,2},{2,0},{4,6},{6,4},{8,10},{10,8},{12,14},{14,12},{1,3},{3,1},... | collective-permute-start | bytes 1572872 | tf_op jit(solution)/shard_map/ppermute | solution.py:376
  10.9 35.8 %collective-permute-start.9 = (bf16[1024,256]{1,0:T(8,128)(2,1)}, bf16[1024,256]{1,0:T(8,128)(2,1)}, u32[]{:S(2)}, u32[]{:S(2)}) collective-permute-start(bf16[1024,256]{1,0:T(8,128)(2,1)} %get-tuple-element.52), channel_id=1, source_target_pairs={{0,4},{2,6},{4,0},{6,2},{8,12},{10,14},{12,8},{14,10},{1,5},{3,7},... | collective-permute-start | bytes 1572872 | tf_op jit(solution)/shard_map/ppermute | solution.py:376
  31.1 38.5 %collective-permute-start.7 = (bf16[1024,256]{1,0:T(8,128)(2,1)}, bf16[1024,256]{1,0:T(8,128)(2,1)}, u32[]{:S(2)}, u32[]{:S(2)}) collective-permute-start(bf16[1024,256]{1,0:T(8,128)(2,1)} %get-tuple-element.50), channel_id=1, source_target_pairs={{0,8},{2,10},{4,12},{6,14},{8,0},{10,2},{12,4},{14,6},{1,9},{3,11}... | collective-permute-start | bytes 1572872 | tf_op jit(solution)/shard_map/ppermute | solution.py:376
  34.5 35.1 %collective-permute-start.5 = (bf16[1024,256]{1,0:T(8,128)(2,1)S(1)}, bf16[1024,256]{1,0:T(8,128)(2,1)S(1)}, u32[]{:S(2)}, u32[]{:S(2)}) collective-permute-start(bf16[1024,256]{1,0:T(8,128)(2,1)S(1)} %get-tuple-element.51), channel_id=1, source_target_pairs={{0,12},{2,14},{4,8},{6,10},{8,4},{10,6},{12,0},{14,2},{1,13},{3,15... | collective-permute-start | bytes 1572872 | tf_op jit(solution)/shard_map/ppermute | solution.py:376
  39.1 31.0 %collective-permute-start.4 = (bf16[2,144,512]{2,1,0:T(8,128)(2,1)S(1)}, bf16[2,144,512]{2,1,0:T(8,128)(2,1)S(1)}, u32[]{:S(2)}, u32[]{:S(2)}) collective-permute-start(bf16[2,144,512]{2,1,0:T(8,128)(2,1)S(1)} %pad_maximum_fusion.5), channel_id=1, source_target_pairs={{0,2},{2,0},{4,6},{6,4},{8,10},{10,8},{12,14},{14,12},{1,3},{3,1},... | collective-permute-start | bytes 884744 | tf_op jit(solution)/shard_map/ppermute | solution.py:376
  46.7 162.7 %collective-permute-start.17 = (bf16[4,512,1024]{2,1,0:T(8,128)(2,1)}, bf16[4,512,1024]{2,1,0:T(8,128)(2,1)}, u32[]{:S(2)}, u32[]{:S(2)}) collective-permute-start(bf16[4,512,1024]{2,1,0:T(8,128)(2,1)} %dynamic-slice_bitcast_fusion), channel_id=1, source_target_pairs={{0,2},{2,0},{4,6},{6,4},{8,10},{10,8},{12,14},{14,12},{1,3},{3,1},... | collective-permute-start | bytes 12582920 | tf_op jit(solution)/shard_map/ppermute | solution.py:376
  69.6 25.6 %collective-permute-start.10 = (bf16[1024,256]{1,0:T(8,128)(2,1)}, bf16[1024,256]{1,0:T(8,128)(2,1)}, u32[]{:S(2)}, u32[]{:S(2)}) collective-permute-start(bf16[1024,256]{1,0:T(8,128)(2,1)} %collective-permute-done.9), channel_id=1, source_target_pairs={{0,2},{2,0},{4,6},{6,4},{8,10},{10,8},{12,14},{14,12},{1,3},{3,1},... | collective-permute-start | bytes 1572872 | tf_op jit(solution)/shard_map/ppermute | solution.py:376
  69.6 45.4 %collective-permute-start.8 = (bf16[1024,256]{1,0:T(8,128)(2,1)}, bf16[1024,256]{1,0:T(8,128)(2,1)S(1)}, u32[]{:S(2)}, u32[]{:S(2)}) collective-permute-start(bf16[1024,256]{1,0:T(8,128)(2,1)} %collective-permute-done.7), channel_id=1, source_target_pairs={{0,2},{2,0},{4,6},{6,4},{8,10},{10,8},{12,14},{14,12},{1,3},{3,1},... | collective-permute-start | bytes 1572872 | tf_op jit(solution)/shard_map/ppermute | solution.py:376
  70.1 64.9 %collective-permute-start.6 = (bf16[1024,256]{1,0:T(8,128)(2,1)S(1)}, bf16[1024,256]{1,0:T(8,128)(2,1)S(1)}, u32[]{:S(2)}, u32[]{:S(2)}) collective-permute-start(bf16[1024,256]{1,0:T(8,128)(2,1)S(1)} %collective-permute-done.5), channel_id=1, source_target_pairs={{0,2},{2,0},{4,6},{6,4},{8,10},{10,8},{12,14},{14,12},{1,3},{3,1},... | collective-permute-start | bytes 1572872 | tf_op jit(solution)/shard_map/ppermute | solution.py:376
  142.5 40.9 %collective-permute-start.12 = (bf16[256,512]{1,0:T(8,128)(2,1)}, bf16[256,512]{1,0:T(8,128)(2,1)S(1)}, u32[]{:S(2)}, u32[]{:S(2)}) collective-permute-start(bf16[256,512]{1,0:T(8,128)(2,1)} %attend.12.mine), channel_id=1, source_target_pairs={{0,4},{2,6},{4,0},{6,2},{8,12},{10,14},{12,8},{14,10},{1,5},{3,7},... | collective-permute-start | bytes 786440 | tf_op jit(solution)/shard_map/ppermute | solution.py:376
  153.1 32.4 %collective-permute-start.13 = (bf16[256,512]{1,0:T(8,128)(2,1)}, bf16[256,512]{1,0:T(8,128)(2,1)S(1)}, u32[]{:S(2)}, u32[]{:S(2)}) collective-permute-start(bf16[256,512]{1,0:T(8,128)(2,1)} %attend.12.mine), channel_id=1, source_target_pairs={{4,8},{6,10},{8,4},{10,6},{5,9},{7,11},{9,5},{11,7},{20,24},{22,26... | collective-permute-start | bytes 786440 | tf_op jit(solution)/shard_map/ppermute | solution.py:376
  160.5 25.2 %collective-permute-start.19 = (bf16[256,512]{1,0:T(8,128)(2,1)}, bf16[256,512]{1,0:T(8,128)(2,1)S(1)}, u32[]{:S(2)}, u32[]{:S(2)}) collective-permute-start(bf16[256,512]{1,0:T(8,128)(2,1)} %attend.13.mine), channel_id=1, source_target_pairs={{0,4},{2,6},{4,0},{6,2},{8,12},{10,14},{12,8},{14,10},{1,5},{3,7},... | collective-permute-start | bytes 786440 | tf_op jit(solution)/shard_map/ppermute | solution.py:376
  165.1 21.2 %collective-permute-start.20 = (bf16[256,512]{1,0:T(8,128)(2,1)}, bf16[256,512]{1,0:T(8,128)(2,1)S(1)}, u32[]{:S(2)}, u32[]{:S(2)}) collective-permute-start(bf16[256,512]{1,0:T(8,128)(2,1)} %attend.13.mine), channel_id=1, source_target_pairs={{4,8},{6,10},{8,4},{10,6},{5,9},{7,11},{9,5},{11,7},{20,24},{22,26... | collective-permute-start | bytes 786440 | tf_op jit(solution)/shard_map/ppermute | solution.py:376
  185.6 13.4 %collective-permute-start.21 = (bf16[256,512]{1,0:T(8,128)(2,1)S(1)}, bf16[256,512]{1,0:T(8,128)(2,1)S(1)}, u32[]{:S(2)}, u32[]{:S(2)}) collective-permute-start(bf16[256,512]{1,0:T(8,128)(2,1)S(1)} %collective-permute-done.19.near), channel_id=1, source_target_pairs={{4,8},{6,10},{8,4},{10,6},{5,9},{7,11},{9,5},{11,7},{20,24},{22,26... | collective-permute-start | bytes 786440 | tf_op jit(solution)/shard_map/ppermute | solution.py:376
  186.3 14.0 %collective-permute-start.33 = (bf16[256,512]{1,0:T(8,128)(2,1)}, bf16[256,512]{1,0:T(8,128)(2,1)S(1)}, u32[]{:S(2)}, u32[]{:S(2)}) collective-permute-start(bf16[256,512]{1,0:T(8,128)(2,1)} %attend.15.mine), channel_id=1, source_target_pairs={{4,8},{6,10},{8,4},{10,6},{5,9},{7,11},{9,5},{11,7},{20,24},{22,26... | collective-permute-start | bytes 786440 | tf_op jit(solution)/shard_map/ppermute | solution.py:376
  200.3 18.9 %collective-permute-start.27 = (bf16[256,512]{1,0:T(8,128)(2,1)S(1)}, bf16[256,512]{1,0:T(8,128)(2,1)}, u32[]{:S(2)}, u32[]{:S(2)}) collective-permute-start(bf16[256,512]{1,0:T(8,128)(2,1)S(1)} %copy-done.6), channel_id=1, source_target_pairs={{4,8},{6,10},{8,4},{10,6},{5,9},{7,11},{9,5},{11,7},{20,24},{22,26... | collective-permute-start | bytes 786440 | tf_op jit(solution)/shard_map/ppermute | solution.py:376
  203.1 16.2 %collective-permute-start.14 = (bf16[256,512]{1,0:T(8,128)(2,1)S(1)}, bf16[256,512]{1,0:T(8,128)(2,1)S(1)}, u32[]{:S(2)}, u32[]{:S(2)}) collective-permute-start(bf16[256,512]{1,0:T(8,128)(2,1)S(1)} %collective-permute-done.12.near), channel_id=1, source_target_pairs={{4,8},{6,10},{8,4},{10,6},{5,9},{7,11},{9,5},{11,7},{20,24},{22,26... | collective-permute-start | bytes 786440 | tf_op jit(solution)/shard_map/ppermute | solution.py:376
  203.8 16.9 %collective-permute-start.28 = (bf16[256,512]{1,0:T(8,128)(2,1)S(1)}, bf16[256,512]{1,0:T(8,128)(2,1)}, u32[]{:S(2)}, u32[]{:S(2)}) collective-permute-start(bf16[256,512]{1,0:T(8,128)(2,1)S(1)} %collective-permute-done.26.near), channel_id=1, source_target_pairs={{4,8},{6,10},{8,4},{10,6},{5,9},{7,11},{9,5},{11,7},{20,24},{22,26... | collective-permute-start | bytes 786440 | tf_op jit(solution)/shard_map/ppermute | solution.py:376
  208.1 13.9 %collective-permute-start.35 = (bf16[256,512]{1,0:T(8,128)(2,1)S(1)}, bf16[256,512]{1,0:T(8,128)(2,1)S(1)}, u32[]{:S(2)}, u32[]{:S(2)}) collective-permute-start(bf16[256,512]{1,0:T(8,128)(2,1)S(1)} %collective-permute-done.33.in_a), channel_id=1, source_target_pairs={{4,0},{6,2},{8,12},{10,14},{5,1},{7,3},{9,13},{11,15},{20,16},{22,... | collective-permute-start | bytes 786440 | tf_op jit(solution)/shard_map/ppermute | solution.py:376
  209.4 14.0 %collective-permute-start.36 = (bf16[256,512]{1,0:T(8,128)(2,1)S(1)}, bf16[256,512]{1,0:T(8,128)(2,1)S(1)}, u32[]{:S(2)}, u32[]{:S(2)}) collective-permute-start(bf16[256,512]{1,0:T(8,128)(2,1)S(1)} %collective-permute-done.34.in_b), channel_id=1, source_target_pairs={{4,0},{6,2},{8,12},{10,14},{5,1},{7,3},{9,13},{11,15},{20,16},{22,... | collective-permute-start | bytes 786440 | tf_op jit(solution)/shard_map/ppermute | solution.py:376
  219.3 28.3 %collective-permute-start.24 = (bf16[256,1024]{1,0:T(8,128)(2,1)}, bf16[256,1024]{1,0:T(8,128)(2,1)S(1)}, u32[]{:S(2)}, u32[]{:S(2)}) collective-permute-start(bf16[256,1024]{1,0:T(8,128)(2,1)} %get-tuple-element.44), channel_id=1, source_target_pairs={{0,2},{2,0},{4,6},{6,4},{8,10},{10,8},{12,14},{14,12},{1,3},{3,1},... | collective-permute-start | bytes 1572872 | tf_op jit(solution)/shard_map/ppermute | solution.py:376
  219.4 13.8 %collective-permute-start.15 = (bf16[256,512]{1,0:T(8,128)(2,1)S(1)}, bf16[256,512]{1,0:T(8,128)(2,1)S(1)}, u32[]{:S(2)}, u32[]{:S(2)}) collective-permute-start(bf16[256,512]{1,0:T(8,128)(2,1)S(1)} %collective-permute-done.13.in_a), channel_id=1, source_target_pairs={{4,0},{6,2},{8,12},{10,14},{5,1},{7,3},{9,13},{11,15},{20,16},{22,... | collective-permute-start | bytes 786440 | tf_op jit(solution)/shard_map/ppermute | solution.py:376
  220.7 17.6 %collective-permute-start.16 = (bf16[256,512]{1,0:T(8,128)(2,1)S(1)}, bf16[256,512]{1,0:T(8,128)(2,1)S(1)}, u32[]{:S(2)}, u32[]{:S(2)}) collective-permute-start(bf16[256,512]{1,0:T(8,128)(2,1)S(1)} %collective-permute-done.14.in_b), channel_id=1, source_target_pairs={{4,0},{6,2},{8,12},{10,14},{5,1},{7,3},{9,13},{11,15},{20,16},{22,... | collective-permute-start | bytes 786440 | tf_op jit(solution)/shard_map/ppermute | solution.py:376
  222.0 27.8 %collective-permute-start.29 = (bf16[256,512]{1,0:T(8,128)(2,1)}, bf16[256,512]{1,0:T(8,128)(2,1)S(1)}, u32[]{:S(2)}, u32[]{:S(2)}) collective-permute-start(bf16[256,512]{1,0:T(8,128)(2,1)} %collective-permute-done.27.in_a), channel_id=1, source_target_pairs={{4,0},{6,2},{8,12},{10,14},{5,1},{7,3},{9,13},{11,15},{20,16},{22,... | collective-permute-start | bytes 786440 | tf_op jit(solution)/shard_map/ppermute | solution.py:376
  223.5 26.4 %collective-permute-start.30 = (bf16[256,512]{1,0:T(8,128)(2,1)}, bf16[256,512]{1,0:T(8,128)(2,1)}, u32[]{:S(2)}, u32[]{:S(2)}) collective-permute-start(bf16[256,512]{1,0:T(8,128)(2,1)} %collective-permute-done.28.in_b), channel_id=1, source_target_pairs={{4,0},{6,2},{8,12},{10,14},{5,1},{7,3},{9,13},{11,15},{20,16},{22,... | collective-permute-start | bytes 786440 | tf_op jit(solution)/shard_map/ppermute | solution.py:376
  233.2 26.0 %collective-permute-start.37 = (bf16[256,1024]{1,0:T(8,128)(2,1)}, bf16[256,1024]{1,0:T(8,128)(2,1)S(1)}, u32[]{:S(2)}, u32[]{:S(2)}) collective-permute-start(bf16[256,1024]{1,0:T(8,128)(2,1)} %get-tuple-element.48), channel_id=1, source_target_pairs={{0,2},{2,0},{4,6},{6,4},{8,10},{10,8},{12,14},{14,12},{1,3},{3,1},... | collective-permute-start | bytes 1572872 | tf_op jit(solution)/shard_map/ppermute | solution.py:376
  247.5 12.8 %collective-permute-start.18 = (bf16[256,1024]{1,0:T(8,128)(2,1)}, bf16[256,1024]{1,0:T(8,128)(2,1)S(1)}, u32[]{:S(2)}, u32[]{:S(2)}) collective-permute-start(bf16[256,1024]{1,0:T(8,128)(2,1)} %get-tuple-element.42), channel_id=1, source_target_pairs={{0,2},{2,0},{4,6},{6,4},{8,10},{10,8},{12,14},{14,12},{1,3},{3,1},... | collective-permute-start | bytes 1572872 | tf_op jit(solution)/shard_map/ppermute | solution.py:376
  248.5 15.0 %collective-permute-start.25 = (bf16[256,1024]{1,0:T(8,128)(2,1)}, bf16[256,1024]{1,0:T(8,128)(2,1)S(1)}, u32[]{:S(2)}, u32[]{:S(2)}) collective-permute-start(bf16[256,1024]{1,0:T(8,128)(2,1)} %add_convert_fusion.3), channel_id=1, source_target_pairs={{0,1},{1,0},{2,3},{3,2},{4,5},{5,4},{6,7},{7,6},{8,9},{9,8},{10,11... | collective-permute-start | bytes 1572872 | tf_op jit(solution)/shard_map/ppermute | solution.py:376
  259.4 14.9 %collective-permute-start.38 = (bf16[256,1024]{1,0:T(8,128)(2,1)S(1)}, bf16[256,1024]{1,0:T(8,128)(2,1)S(1)}, u32[]{:S(2)}, u32[]{:S(2)}) collective-permute-start(bf16[256,1024]{1,0:T(8,128)(2,1)S(1)} %add_convert_fusion.1), channel_id=1, source_target_pairs={{0,1},{1,0},{2,3},{3,2},{4,5},{5,4},{6,7},{7,6},{8,9},{9,8},{10,11... | collective-permute-start | bytes 1572872 | tf_op jit(solution)/shard_map/ppermute | solution.py:376
  (36 other events, 492.8 us)
where the time goes:
time: 277 us; the launch traced here: 276 us
  Pallas kernels  126 us (45%)
  waiting for transfers between devices  67.3 us (24%)
  starting transfers between devices  49.4 us (18%)
  local copies, waits for them, and re-layouts  17.7 us (6%)
  other arithmetic  14.8 us (5%)
    pallas_call x8, Pallas kernels, attend(): pl.pallas_call(functools.partial(attend_kernel, first, last, heads, bool(...  91.9 us
    ppermute x39, waiting for transfers between devices, permute(): return lax.ppermute(array, axis, perm)  67.3 us
    ppermute x39, starting transfers between devices, permute(): return lax.ppermute(array, axis, perm)  49.4 us
    pallas_call x4, Pallas kernels, project(): pl.pallas_call(project_kernel, out_shape=(jax.ShapeDtypeStruct((rows, col...  33.8 us
  transfers between devices with their start and end apart: 39, of which 12 were waited for; matrix products, arithmetic and copies ran while one was open for 9% of the time, Pallas kernels for 46%

commit v1 on v0

--- a/solution.py
+++ b/solution.py
@@ -16,6 +16,7 @@
 key_group = 4
 meta_rows = 16
 share = 16
+attend_vmem = 16 << 20
 
 
 slab_rows = 512
@@ -122,29 +123,53 @@
     return lax.psum_scatter(terms, "rows", scatter_dimension=0, tiled=True).astype(jnp.bfloat16)
 
 
-def attend_kernel(first, last, heads, held, tab, cnt, qb, qk, qp, *refs):
-    q_refs, (kv_a, kv_b, *refs) = refs[:4], refs[4:]
-    if held:
-        acc_in, top_in, *refs = refs
+def attend_kernel(chip, last, heads, tab, cnt, qb, qk, qp, *refs):
+    q_refs, refs = refs[:2], refs[2:]
+    chips = 4 if last else 1
+    kv_refs, refs = refs[: 2 * chips], refs[2 * chips :]
     if last:
-        o_ref, kv, s_all, tops, q_rows, sems, acc = refs
+        acc_in, high_in, refs = refs[:chip], refs[chip : 2 * chip], refs[2 * chip :]
+        o_ref, kv, q_rows, sems, acc, high, top = refs
     else:
-        acc_out, top_out, kv, s_all, tops, q_rows, sems = refs
-        acc = acc_out.at[0]
+        acc_out, high_out, kv, q_rows, sems = refs
+        acc, high = acc_out.at[0], high_out.at[0]
     step = pl.program_id(0)
     width = HEAD_WIDTH
-    half = kv_a.shape[0]
-
-    @pl.when(step == 0)
-    def _():
+    half = kv_refs[0].shape[0]
+    block = qb[step]
+    lane = lax.broadcasted_iota(jnp.int32, (1, BLOCK_TOKENS), 1)
+
+    def fetch(which):
         copies = [
-            pltpu.make_async_copy(source, kv.at[pl.ds(half * i, half)], sems.at[i])
-            for i, source in enumerate((kv_a, kv_b))
+            pltpu.make_async_copy(kv_refs[which * 2 + i], kv.at[pl.ds(half * i, half)], sems.at[i])
+            for i in range(2)
         ]
         for copy in copies:
             copy.start()
         for copy in copies:
             copy.wait()
+
+    def group_of(of, j):
+        entries = [tab[of, block, j * key_group + p] for p in range(key_group)]
+        hidden = [jnp.where(lane < e % 256, 0.0, masked_low) for e in entries]
+        values = jnp.concatenate([kv[e // 256, :, width:] for e in entries], axis=0)
+        values = jnp.concatenate([values, jnp.ones_like(values)], axis=1)
+        keys = [kv[e // 256, :, :width] for e in entries]
+        return keys, hidden, values
+
+    def groups_of(of):
+        return (cnt[of, block] + (key_group - 1)) // key_group
+
+    def exponents(keys, hidden, i):
+        pair = jnp.concatenate(keys[i : i + 2], axis=0)
+        scores = lax.dot_general(
+            q_rows[...], pair, (((1,), (1,)), ((), ())), preferred_element_type=jnp.float32
+        )
+        return scores * exp2_scale + jnp.concatenate(hidden[i : i + 2], axis=1)
+
+    @pl.when(step == 0)
+    def _():
+        fetch(chips - 1)
 
     for which, q_ref in enumerate(q_refs):
 
@@ -155,118 +180,113 @@
                     0, :, h * width : (h + 1) * width
                 ]
 
-    block = qb[step]
-    groups = (cnt[block] + (key_group - 1)) // key_group
-    tops[...] = jnp.full_like(tops, masked_low)
-    lane = lax.broadcasted_iota(jnp.int32, (1, BLOCK_TOKENS), 1)
-
-    def find(j, carry):
-        top = tops[...]
-        for p in range(0, key_group, 2):
-            entries = [tab[block, j * key_group + p + i] for i in range(2)]
-            keys = jnp.concatenate([kv[e // 256, :, :width] for e in entries], axis=0)
-            hidden = jnp.concatenate(
-                [jnp.where(lane < e % 256, 0.0, masked_low) for e in entries], axis=1
-            )
-            scores = lax.dot_general(
-                q_rows[...], keys, (((1,), (1,)), ((), ())), preferred_element_type=jnp.float32
-            )
-            scores = scores + hidden
-            s_all[j, :, p * BLOCK_TOKENS : (p + 2) * BLOCK_TOKENS] = scores
-            top = jnp.maximum(top, jnp.maximum(scores[:, :width], scores[:, width:]))
-        tops[...] = top
+    if last:
+        acc[...] = functools.reduce(jnp.add, [a[0] for a in acc_in])
+        high[...] = functools.reduce(jnp.maximum, [a[0] for a in high_in])
+    else:
+        acc[...] = jnp.zeros(acc.shape, jnp.float32)
+        high[...] = jnp.full(high.shape, masked_low, jnp.float32)
+
+    def fold(j, carry):
+        keys, hidden, values = group_of(chip, j)
+        probs = []
+        highest = high[...]
+        for i in range(0, key_group, 2):
+            x = exponents(keys, hidden, i)
+            for side in (x[:, :BLOCK_TOKENS], x[:, BLOCK_TOKENS:]):
+                highest = jnp.maximum(highest, jnp.max(side.reshape(-1, 8, BLOCK_TOKENS), axis=0))
+            probs.append(jnp.exp2(x).astype(jnp.bfloat16))
+        high[...] = highest
+        acc[...] += jnp.dot(
+            jnp.concatenate(probs, axis=1), values, preferred_element_type=jnp.float32
+        )
         return carry
 
-    lax.fori_loop(0, groups, find, 0)
-    top = jnp.max(tops[...], axis=1, keepdims=True) * exp2_scale
-    top = jnp.broadcast_to(top, tops.shape)
-    if first:
+    lax.fori_loop(0, groups_of(chip), fold, 0)
+    if not last:
+        return
+
+    unsafe = (jnp.max(high[...]) > 100.0) | (jnp.min(acc[:, width:]) < 2.0**-80)
+
+    @pl.when(unsafe)
+    def _():
         acc[...] = jnp.zeros(acc.shape, jnp.float32)
-    else:
-        before = top_in[0]
-        top = jnp.maximum(top, before)
-        fade = jnp.exp2(before - top)
-        acc[:, :width] = acc_in[0, :, :width] * fade
-        acc[:, width:] = acc_in[0, :, width:] * fade
-    tops[...] = top
-    if not last:
-        top_out[0] = top
-
-    def gather(j, carry):
-        entries = [tab[block, j * key_group + p] for p in range(key_group)]
-        values = jnp.concatenate([kv[e // 256, :, width:] for e in entries], axis=0)
-        values = jnp.concatenate([values, jnp.ones_like(values)], axis=1)
-        probs = jnp.concatenate(
-            [
-                jnp.exp2(
-                    s_all[j, :, p * BLOCK_TOKENS : (p + 1) * BLOCK_TOKENS] * exp2_scale - tops[...]
-                ).astype(jnp.bfloat16)
-                for p in range(key_group)
-            ],
-            axis=1,
-        )
-        acc[...] += jnp.dot(probs, values, preferred_element_type=jnp.float32)
-        return carry
-
-    lax.fori_loop(0, groups, gather, 0)
-    if last:
-        for h in range(heads):
-            rows = slice(h * BLOCK_TOKENS, (h + 1) * BLOCK_TOKENS)
-            o_ref[:, h * width : (h + 1) * width] = (acc[rows, :width] / acc[rows, width:]).astype(
-                o_ref.dtype
-            )
-
-
-def attend(lists, at, q_four, kv_own, kv_swap, state=(), first=False, last=False):
+        top[...] = jnp.full(top.shape, masked_low, jnp.float32)
+        for of in range(chips):
+            fetch(of)
+
+            def fold_top(j, carry):
+                keys, hidden, values = group_of(of, j)
+                for i in range(0, key_group, 2):
+                    x = exponents(keys, hidden, i)
+                    before = top[...]
+                    after = jnp.maximum(before, jnp.max(x, axis=1, keepdims=True))
+                    fade = jnp.exp2(before - after)
+                    top[...] = after
+                    probs = jnp.exp2(x - jnp.concatenate([after, after], axis=1))
+                    acc[...] = acc[...] * jnp.concatenate([fade, fade], axis=1) + jnp.dot(
+                        probs.astype(jnp.bfloat16),
+                        values[i * BLOCK_TOKENS : (i + 2) * BLOCK_TOKENS],
+                        preferred_element_type=jnp.float32,
+                    )
+                return carry
+
+            lax.fori_loop(0, groups_of(of), fold_top, 0)
+
+    for h in range(heads):
+        rows = slice(h * BLOCK_TOKENS, (h + 1) * BLOCK_TOKENS)
+        o_ref[:, h * width : (h + 1) * width] = (acc[rows, :width] / acc[rows, width:]).astype(
+            o_ref.dtype
+        )
+
+
+def attend(chip, lists, at, q_two, kv_refs, state=None):
+    last = state is not None
     tab, cnt = lists
     qb, qk, qp = at
     count = qb.shape[0]
-    width = q_four[0].shape[2]
+    width = q_two[0].shape[2]
     heads = width // HEAD_WIDTH
     rows = heads * BLOCK_TOKENS
-    blocks = tab.shape[1]
-    everyone = cnt.shape[0]
+    blocks = tab.shape[2]
+    everyone = cnt.shape[1]
     q_spec = pl.BlockSpec((1, BLOCK_TOKENS, width), lambda i, tab, cnt, qb, qk, qp: (qk[i], 0, 0))
     acc_spec = pl.BlockSpec((1, rows, 2 * HEAD_WIDTH), lambda i, tab, cnt, qb, qk, qp: (qb[i], 0, 0))
-    top_spec = pl.BlockSpec((1, rows, HEAD_WIDTH), lambda i, tab, cnt, qb, qk, qp: (qb[i], 0, 0))
+    high_spec = pl.BlockSpec((1, 8, BLOCK_TOKENS), lambda i, tab, cnt, qb, qk, qp: (qb[i], 0, 0))
     scratch = [
         pltpu.VMEM((blocks, BLOCK_TOKENS, 2 * HEAD_WIDTH), jnp.bfloat16),
-        pltpu.VMEM((blocks // key_group, rows, key_group * BLOCK_TOKENS), jnp.float32),
-        pltpu.VMEM((rows, HEAD_WIDTH), jnp.float32),
         pltpu.VMEM((rows, HEAD_WIDTH), jnp.bfloat16),
         pltpu.SemaphoreType.DMA((2,)),
     ]
-    state_specs = [acc_spec, top_spec]
-    if first:
-        state_specs = [pl.BlockSpec(memory_space=pl.ANY)] * 2
     if last:
         out_shape = jax.ShapeDtypeStruct((count * BLOCK_TOKENS, width), jnp.bfloat16)
         out_specs = pl.BlockSpec((BLOCK_TOKENS, width), lambda i, *_: (i, 0))
-        scratch.append(pltpu.VMEM((rows, 2 * HEAD_WIDTH), jnp.float32))
-        aliases = {}
+        scratch += [
+            pltpu.VMEM((rows, 2 * HEAD_WIDTH), jnp.float32),
+            pltpu.VMEM((8, BLOCK_TOKENS), jnp.float32),
+            pltpu.VMEM((rows, HEAD_WIDTH), jnp.float32),
+        ]
     else:
         out_shape = (
             jax.ShapeDtypeStruct((everyone, rows, 2 * HEAD_WIDTH), jnp.float32),
-            jax.ShapeDtypeStruct((everyone, rows, HEAD_WIDTH), jnp.float32),
-        )
-        out_specs = (acc_spec, top_spec)
-        aliases = {11 + i: i for i in range(len(state))}
-    shape = (kv_own.shape[0] // BLOCK_TOKENS, BLOCK_TOKENS, kv_own.shape[1])
+            jax.ShapeDtypeStruct((everyone, 8, BLOCK_TOKENS), jnp.float32),
+        )
+        out_specs = (acc_spec, high_spec)
+    shape = (kv_refs[0].shape[0] // BLOCK_TOKENS, BLOCK_TOKENS, kv_refs[0].shape[1])
     work = count * blocks // 2 * rows * BLOCK_TOKENS
     return pl.pallas_call(
-        functools.partial(attend_kernel, first, last, heads, bool(state)),
+        functools.partial(attend_kernel, chip, last, heads),
         out_shape=out_shape,
         grid_spec=pltpu.PrefetchScalarGridSpec(
             num_scalar_prefetch=5,
             grid=(count,),
-            in_specs=[q_spec] * 4
-            + [pl.BlockSpec(memory_space=pl.ANY)] * 2
-            + state_specs[: len(state)],
+            in_specs=[q_spec] * 2
+            + [pl.BlockSpec(memory_space=pl.ANY)] * len(kv_refs)
+            + ([acc_spec] * chip + [high_spec] * chip if last else []),
             out_specs=out_specs,
             scratch_shapes=scratch,
         ),
-        input_output_aliases=aliases,
-        compiler_params=pltpu.CompilerParams(vmem_limit_bytes=60 << 20),
+        compiler_params=pltpu.CompilerParams(vmem_limit_bytes=attend_vmem),
         cost_estimate=pl.CostEstimate(
             flops=work * 4 * HEAD_WIDTH * 4, bytes_accessed=work // 8, transcendentals=work
         ),
@@ -277,10 +297,9 @@
         qb,
         qk,
         qp,
-        *q_four,
-        kv_own.reshape(shape),
-        kv_swap.reshape(shape),
-        *state,
+        *q_two,
+        *[a.reshape(shape) for a in kv_refs],
+        *((*[a for a, _ in state], *[h for _, h in state]) if last else ()),
     )
 
 
@@ -407,41 +426,27 @@
     q_come = [q_for(z)]
     for k in range(1, chips):
         q_come.append(permute(q_for(z ^ k), apart(2 * k)))
-    kv_own = [kv_for(z)]
-    for k in range(1, chips):
-        kv_own.append(permute(kv_for(z ^ k), apart(2 * k)))
-    kv_swap = [swap(kv_own[k]) for k in range(chips)]
-
-    near_own = columns_of(q_come[:2], core)
-    near_swap = swap(columns_of(q_come[:2], 1 - core))
-    far_own = columns_of(q_come[2:], core)
-    far_swap = swap(columns_of(q_come[2:], 1 - core))
-    q_four = [near_own, near_swap, far_own, far_swap]
-
-    def lists_of(own, other):
-        notes = jnp.stack([own[:, q_len, :64], other[:, q_len, :64]], axis=1)
-        tab, cnt = key_lists(notes.astype(jnp.int32), 2 * chips)
-        return [(tab[i], cnt[i]) for i in range(2)]
-
-    lists = lists_of(near_own, near_swap)
-    lists, far_notes = lax.optimization_barrier((lists, (far_own, far_swap)))
-    lists = lists + lists_of(*far_notes)
+    kv = []
+    for k in range(chips):
+        own = kv_for(z ^ k)
+        if k:
+            own = permute(own, apart(2 * k))
+        kv.append((own, swap(own)))
+
+    q_own = columns_of(q_come, core)
+    q_swap = swap(columns_of(q_come, 1 - core))
+    q_two = (q_own, q_swap)
+    notes = jnp.stack([q_own[:, q_len, :64], q_swap[:, q_len, :64]], axis=1)
+    lists = key_lists(notes.astype(jnp.int32), 2 * chips)
 
     def places(blocks):
         blocks = blocks.astype(jnp.int32)
         k = (blocks // 2) ^ z
-        which = 2 * (k // 2) + ((blocks % 2) ^ core)
-        return blocks, (k % 2).astype(jnp.int32), which.astype(jnp.int32)
-
-    four = jnp.arange(4, dtype=jnp.int32)
-    near = places(4 * (z // 2) + four)
-    far = places(4 * (1 - z // 2) + four)
+        which = (blocks % 2) ^ core
+        return blocks, k.astype(jnp.int32), which.astype(jnp.int32)
+
     everything = places(jnp.arange(2 * chips, dtype=jnp.int32))
-    q_near = q_four[:2] * 2
-    state = attend(lists[0], near, q_near, kv_own[0], kv_swap[0], first=True)
-    state = attend(lists[0], far, q_four, kv_own[0], kv_swap[0], state, first=True)
-    state = attend(lists[1], everything, q_four, kv_own[1], kv_swap[1], state)
-    state = attend(lists[2], everything, q_four, kv_own[2], kv_swap[2], state)
+    state = [attend(k, lists, everything, q_two, kv[k]) for k in range(chips - 1)]
 
     w_split = out_weight.reshape(chips, 2, depth, out_weight.shape[1])
     w_swap = swap(lax.dynamic_index_in_dim(w_split, 1 - core, 1, keepdims=False))
@@ -456,7 +461,8 @@
 
     def chunk(chip):
         pieces = places(2 * chip + jnp.arange(2, dtype=jnp.int32))
-        mine = attend(lists[last], pieces, q_four, kv_own[last], kv_swap[last], state, last=True)
+        every_key = [a for of in kv for a in of]
+        mine = attend(last, lists, pieces, q_two, every_key, state)
         beside = permute(mine, apart(2))
         in_a = permute(mine, across)
         in_b = permute(beside, across)

time: 277 us -> 321 us (1.16)
  Pallas kernels: 126 us -> 173 us
  waiting for transfers between devices: 67.3 us -> 75.9 us
  other arithmetic: 14.8 us -> 9.54 us
  starting transfers between devices: 49.4 us -> 44.7 us
    pallas_call x8 -> x7, Pallas kernels: 91.9 us -> 139 us  [attend(): pl.pallas_call(functools.partial(attend_kernel, chip, last, heads), out_s...]
    ppermute x39 -> x38, waiting for transfers between devices: 67.3 us -> 75.9 us  [permute(): return lax.ppermute(array, axis, perm)]
    ppermute x39 -> x38, starting transfers between devices: 49.4 us -> 44.7 us  [permute(): return lax.ppermute(array, axis, perm)]
    select_n x7 -> x0, other arithmetic: 4.13 us -> none  [places(): return (blocks, (k % 2).astype(jnp.int32), which.astype(jnp.int32))]
  transfers between devices with their start and end apart: 39 -> 38, of which waited for: 12 -> 9; matrix products, arithmetic and copies ran while one was open for 9% -> 6% of each run, Pallas kernels for 46% -> 54%
where the time goes in v1:
time: 321 us; the launch traced here: 318 us
  Pallas kernels  173 us (54%)
  waiting for transfers between devices  75.9 us (24%)
  starting transfers between devices  44.7 us (14%)
  local copies, waits for them, and re-layouts  14.9 us (5%)
  other arithmetic  9.54 us (3%)
    pallas_call x7, Pallas kernels, attend(): pl.pallas_call(functools.partial(attend_kernel, chip, last, heads), out_s...  139 us
    ppermute x38, waiting for transfers between devices, permute(): return lax.ppermute(array, axis, perm)  75.9 us
    ppermute x38, starting transfers between devices, permute(): return lax.ppermute(array, axis, perm)  44.7 us
    pallas_call x4, Pallas kernels, project(): pl.pallas_call(project_kernel, out_shape=(jax.ShapeDtypeStruct((rows, col...  33.8 us
  transfers between devices with their start and end apart: 38, of which 9 were waited for; matrix products, arithmetic and copies ran while one was open for 6% of the time, Pallas kernels for 54%

profile of v1, /device:TPU:0, one launch (start us, length us, event | category | flops | bytes accessed | tf_op | source)
XLA Modules:
  0.0 318.5 jit_solution(14183863096322969713)
XLA Ops:
  4.0 3.1 collective-permute-start
  7.0 2.6 collective-permute-start.1
  10.9 3.8 %collective-permute-start.9 = (bf16[1024,256]{1,0:T(8,128)(2,1)}, bf16[1024,256]{1,0:T(8,128)(2,1)S(1)}, u32[]{:S(2)}, u32[]{:S(2)}) collective-permute-start(bf16[1024,256]{1,0:T(8,128)(2,1)} %get-tuple-element.33), channel_id=1, source_target_pairs={{0,12},{2,14},{4,8},{6,10},{8,4},{10,6},{12,0},{14,2},{1,13},{3,15... | collective-permute-start | bytes 1572872 | tf_op jit(solution)/shard_map/ppermute | solution.py:395
  16.5 4.3 %collective-permute-done = bf16[144,1024]{1,0:T(8,128)(2,1)} collective-permute-done((bf16[144,1024]{1,0:T(8,128)(2,1)}, bf16[144,1024]{1,0:T(8,128)(2,1)}, u32[]{:S(2)}, u32[]{:S(2)}) %collective-permute-start) | collective-permute-done | bytes 294944 | tf_op jit(solution)/shard_map/ppermute | solution.py:395
  20.8 2.1 collective-permute-start.7
  22.9 1.6 dynamic-slice_bitcast_fusion.7
  24.6 17.5 %collective-permute-done.1 = bf16[144,1024]{1,0:T(8,128)(2,1)} collective-permute-done((bf16[144,1024]{1,0:T(8,128)(2,1)}, bf16[144,1024]{1,0:T(8,128)(2,1)}, u32[]{:S(2)}, u32[]{:S(2)}) %collective-permute-start.1) | collective-permute-done | bytes 294944 | tf_op jit(solution)/shard_map/ppermute | solution.py:395
  42.0 1.7 dynamic-slice_bitcast_fusion.6
  43.7 1.6 dynamic-slice_bitcast_fusion.5
  47.4 4.7 %dynamic-slice_bitcast_fusion = bf16[4,512,1024]{2,1,0:T(8,128)(2,1)} fusion(bf16[4,2,512,1024]{3,2,1,0:T(8,128)(2,1)} %bitcast.58, s32[]{:T(128)S(6)} %select_n.125), kind=kLoop, calls=%fused_computation | loop fusion | bytes 8388612 | tf_op jit(solution)/shard_map/jit(dynamic_index_in_dim)/squeeze | solution.py:452
  52.8 27.8 %collective-permute-done.7 = bf16[1024,256]{1,0:T(8,128)(2,1)S(1)} collective-permute-done((bf16[1024,256]{1,0:T(8,128)(2,1)}, bf16[1024,256]{1,0:T(8,128)(2,1)S(1)}, u32[]{:S(2)}, u32[]{:S(2)}) %collective-permute-start.7) | collective-permute-done | bytes 524320 | tf_op jit(solution)/shard_map/ppermute | solution.py:395
  82.6 12.8 %attend.7 = (f32[8,512,256]{2,1,0:T(8,128)S(1)}, f32[8,8,128]{2,1,0:T(8,128)S(1)}) custom-call(s32[4,8,16]{2,1,0:T(8,128)S(1)} %select_reduce_fusion.tab, s32[4,8]{1,0:T(4,128)S(1)} %convert_reduce_fusion.cnt, s32[8]{0:T(128)S(1)} %iota.43.qb, s32[8]{0:T(128)S(1)} %get-tuple-element.54.qk, s32[8]{0:T(128)S(1)} %get-tuple-element.53.qp, ...), custom_call_target="tpu_custom_call" | custom-call | flops 8589934592 | bytes 524288 | tf_op jit(solution)/shard_map/attend/pallas_call | solution.py:277
  95.3 12.2 %attend.9 = (f32[8,512,256]{2,1,0:T(8,128)S(1)}, f32[8,8,128]{2,1,0:T(8,128)S(1)}) custom-call(s32[4,8,16]{2,1,0:T(8,128)S(1)} %select_reduce_fusion.tab, s32[4,8]{1,0:T(4,128)S(1)} %convert_reduce_fusion.cnt, s32[8]{0:T(128)S(1)} %iota.46.qb, s32[8]{0:T(128)S(1)} %get-tuple-element.54.qk, s32[8]{0:T(128)S(1)} %get-tuple-element.53.qp, ...), custom_call_target="tpu_custom_call" | custom-call | flops 8589934592 | bytes 524288 | tf_op jit(solution)/shard_map/attend/pallas_call | solution.py:277
  107.6 12.8 %attend.8 = (f32[8,512,256]{2,1,0:T(8,128)S(1)}, f32[8,8,128]{2,1,0:T(8,128)S(1)}) custom-call(s32[4,8,16]{2,1,0:T(8,128)S(1)} %select_reduce_fusion.tab, s32[4,8]{1,0:T(4,128)S(1)} %convert_reduce_fusion.cnt, s32[8]{0:T(128)S(1)} %iota.45.qb, s32[8]{0:T(128)S(1)} %get-tuple-element.54.qk, s32[8]{0:T(128)S(1)} %get-tuple-element.53.qp, ...), custom_call_target="tpu_custom_call" | custom-call | flops 8589934592 | bytes 524288 | tf_op jit(solution)/shard_map/attend/pallas_call | solution.py:277
  120.4 20.7 %attend.10.mine = bf16[256,512]{1,0:T(8,128)(2,1)S(1)} custom-call(s32[4,8,16]{2,1,0:T(8,128)S(1)} %select_reduce_fusion.tab, s32[4,8]{1,0:T(4,128)S(1)} %convert_reduce_fusion.cnt, s32[2]{0:T(128)S(1)} %copy-done.8, s32[2]{0:T(128)S(1)} %copy-done.7, s32[2]{0:T(128)S(1)} %copy-done.6, bf16[4,144,512]{2,1,0:T(8,128)(2,1)S(1)} %pad_maximum_fusion.1.refs_0_, ...), custom_call_target="tpu_custom_call" | custom-call | flops 2147483648 | bytes 131072 | tf_op jit(solution)/shard_map/attend/pallas_call | solution.py:277
  142.6 1.6 collective-permute-start.11
  144.1 25.7 %attend.13.mine = bf16[256,512]{1,0:T(8,128)(2,1)S(1)} custom-call(s32[4,8,16]{2,1,0:T(8,128)S(1)} %select_reduce_fusion.tab, s32[4,8]{1,0:T(4,128)S(1)} %convert_reduce_fusion.cnt, s32[2]{0:T(128)S(1)} %copy-done.9, s32[2]{0:T(128)S(1)} %get-tuple-element.62.qk, s32[2]{0:T(128)S(1)} %get-tuple-element.61.qp, ...), custom_call_target="tpu_custom_call" | custom-call | flops 2147483648 | bytes 131072 | tf_op jit(solution)/shard_map/attend/pallas_call | solution.py:277
  170.0 20.7 %attend.11.mine = bf16[256,512]{1,0:T(8,128)(2,1)S(1)} custom-call(s32[4,8,16]{2,1,0:T(8,128)S(1)} %select_reduce_fusion.tab, s32[4,8]{1,0:T(4,128)S(1)} %convert_reduce_fusion.cnt, s32[2]{0:T(128)S(1)} %iota_add_fusion.2.qb, s32[2]{0:T(128)S(1)} %copy-done.5, s32[2]{0:T(128)S(1)} %copy-done.4, bf16[4,144,512]{2,1,0:T(8,128)(2,1)S(1)} %pad_maximum_fusion.1.refs_0_, ...), custom_call_target="tpu_custom_call" | custom-call | flops 2147483648 | bytes 131072 | tf_op jit(solution)/shard_map/attend/pallas_call | solution.py:277
  191.4 4.3 %collective-permute-start.18 = (bf16[256,512]{1,0:T(8,128)(2,1)S(1)}, bf16[256,512]{1,0:T(8,128)(2,1)}, u32[]{:S(2)}, u32[]{:S(2)}) collective-permute-start(bf16[256,512]{1,0:T(8,128)(2,1)S(1)} %attend.11.mine), channel_id=1, source_target_pairs={{0,4},{2,6},{4,0},{6,2},{8,12},{10,14},{12,8},{14,10},{1,5},{3,7},... | collective-permute-start | bytes 786440 | tf_op jit(solution)/shard_map/ppermute | solution.py:395
  198.4 33.9 %attend.12.mine = bf16[256,512]{1,0:T(8,128)(2,1)S(1)} custom-call(s32[4,8,16]{2,1,0:T(8,128)S(1)} %select_reduce_fusion.tab, s32[4,8]{1,0:T(4,128)S(1)} %convert_reduce_fusion.cnt, s32[2]{0:T(128)S(1)} %iota_add_fusion.1.qb, s32[2]{0:T(128)S(1)} %get-tuple-element.60.qk, s32[2]{0:T(128)S(1)} %get-tuple-element.59.qp, ...), custom_call_target="tpu_custom_call" | custom-call | flops 2147483648 | bytes 131072 | tf_op jit(solution)/shard_map/attend/pallas_call | solution.py:277
  232.4 3.8 %collective-permute-start.25 = (bf16[256,512]{1,0:T(8,128)(2,1)S(1)}, bf16[256,512]{1,0:T(8,128)(2,1)S(1)}, u32[]{:S(2)}, u32[]{:S(2)}) collective-permute-start(bf16[256,512]{1,0:T(8,128)(2,1)S(1)} %attend.12.mine), channel_id=1, source_target_pairs={{0,4},{2,6},{4,0},{6,2},{8,12},{10,14},{12,8},{14,10},{1,5},{3,7},... | collective-permute-start | bytes 786440 | tf_op jit(solution)/shard_map/ppermute | solution.py:395
  239.6 2.8 collective-permute-done.25.near
  245.1 3.2 %collective-permute-done.34.out_a = bf16[256,512]{1,0:T(8,128)(2,1)S(1)} collective-permute-done((bf16[256,512]{1,0:T(8,128)(2,1)}, bf16[256,512]{1,0:T(8,128)(2,1)S(1)}, u32[]{:S(2)}, u32[]{:S(2)}) %collective-permute-start.34) | collective-permute-done | bytes 262176 | tf_op jit(solution)/shard_map/ppermute | solution.py:395
  249.5 4.3 %collective-permute-done.35.out_b = bf16[256,512]{1,0:T(8,128)(2,1)S(1)} collective-permute-done((bf16[256,512]{1,0:T(8,128)(2,1)}, bf16[256,512]{1,0:T(8,128)(2,1)S(1)}, u32[]{:S(2)}, u32[]{:S(2)}) %collective-permute-start.35) | collective-permute-done | bytes 262176 | tf_op jit(solution)/shard_map/ppermute | solution.py:395
  255.9 8.5 %project.7 = (f32[256,1024]{1,0:T(8,128)}, bf16[256,1024]{1,0:T(8,128)(2,1)}) custom-call(s32[5]{0:T(128)} %concatenate.37.at, s32[1]{0:T(128)} %bitcast.5.middle, bf16[256,512]{1,0:T(8,128)(2,1)} %copy-done.3, bf16[256,512]{1,0:T(8,128)(2,1)} %copy-done.20, bf16[256,512]{1,0:T(8,128)(2,1)} %collective-permute-done.32.in_a, ...), custom_call_target="tpu_custom_call" | custom-call | flops 2147483648 | bytes 11534336 | tf_op jit(solution)/shard_map/project/pallas_call | solution.py:340
  268.4 1.5 collective-permute-start.15
  270.0 8.5 %project.5 = (f32[256,1024]{1,0:T(8,128)}, bf16[256,1024]{1,0:T(8,128)(2,1)}) custom-call(s32[5]{0:T(128)} %concatenate.37.at, s32[1]{0:T(128)} %bitcast.5.middle, bf16[256,512]{1,0:T(8,128)(2,1)} %copy-done.1, bf16[256,512]{1,0:T(8,128)(2,1)} %collective-permute-done.18.near, bf16[256,512]{1,0:T(8,128)(2,1)} %copy-done.19, bf16[256,512]{1,0:T(8,128)(2,1)} %copy-done.22, ...), custom_call_target="tpu_custom_call" | custom-call | flops 2147483648 | bytes 11534336 | tf_op jit(solution)/shard_map/project/pallas_call | solution.py:340
  279.1 2.1 collective-permute-done.29.out_b
  281.9 8.4 %project.6 = (f32[256,1024]{1,0:T(8,128)}, bf16[256,1024]{1,0:T(8,128)(2,1)}) custom-call(s32[5]{0:T(128)} %concatenate.37.at, s32[1]{0:T(128)} %bitcast.5.middle, bf16[256,512]{1,0:T(8,128)(2,1)} %copy-done.2, bf16[256,512]{1,0:T(8,128)(2,1)} %copy-done.21, bf16[256,512]{1,0:T(8,128)(2,1)} %copy-done.23, bf16[256,512]{1,0:T(8,128)(2,1)} %copy-done.24, ...), custom_call_target="tpu_custom_call" | custom-call | flops 2147483648 | bytes 11534336 | tf_op jit(solution)/shard_map/project/pallas_call | solution.py:340
  293.6 8.4 %project.4 = (f32[256,1024]{1,0:T(8,128)}, bf16[256,1024]{1,0:T(8,128)(2,1)}) custom-call(s32[5]{0:T(128)} %concatenate.37.at, s32[1]{0:T(128)} %bitcast.5.middle, bf16[256,512]{1,0:T(8,128)(2,1)} %copy-done, bf16[256,512]{1,0:T(8,128)(2,1)} %copy-done.18, bf16[256,512]{1,0:T(8,128)(2,1)} %collective-permute-done.12.in_a, ...), custom_call_target="tpu_custom_call" | custom-call | flops 2147483648 | bytes 11534336 | tf_op jit(solution)/shard_map/project/pallas_call | solution.py:340
  303.1 3.4 %collective-permute-done.37 = bf16[256,1024]{1,0:T(8,128)(2,1)S(1)} collective-permute-done((bf16[256,1024]{1,0:T(8,128)(2,1)}, bf16[256,1024]{1,0:T(8,128)(2,1)S(1)}, u32[]{:S(2)}, u32[]{:S(2)}) %collective-permute-start.37) | collective-permute-done | bytes 524320 | tf_op jit(solution)/shard_map/ppermute | solution.py:395
  306.7 10.5 %collective-permute-done.24 = bf16[256,1024]{1,0:T(8,128)(2,1)S(1)} collective-permute-done((bf16[256,1024]{1,0:T(8,128)(2,1)S(1)}, bf16[256,1024]{1,0:T(8,128)(2,1)S(1)}, u32[]{:S(2)}, u32[]{:S(2)}) %collective-permute-start.24) | collective-permute-done | bytes 524320 | tf_op jit(solution)/shard_map/ppermute | solution.py:395
  (167 shorter events, 36.7 us)
Async XLA Ops:
  4.0 16.8 %collective-permute-start = (bf16[144,1024]{1,0:T(8,128)(2,1)}, bf16[144,1024]{1,0:T(8,128)(2,1)}, u32[]{:S(2)}, u32[]{:S(2)}) collective-permute-start(bf16[144,1024]{1,0:T(8,128)(2,1)} %get-tuple-element.50), channel_id=1, source_target_pairs={{0,4},{2,6},{4,0},{6,2},{8,12},{10,14},{12,8},{14,10},{1,5},{3,7},... | collective-permute-start | bytes 884744 | tf_op jit(solution)/shard_map/ppermute | solution.py:395
  7.0 35.0 %collective-permute-start.1 = (bf16[144,1024]{1,0:T(8,128)(2,1)}, bf16[144,1024]{1,0:T(8,128)(2,1)}, u32[]{:S(2)}, u32[]{:S(2)}) collective-permute-start(bf16[144,1024]{1,0:T(8,128)(2,1)} %get-tuple-element.51), channel_id=1, source_target_pairs={{0,8},{2,10},{4,12},{6,14},{8,0},{10,2},{12,4},{14,6},{1,9},{3,11}... | collective-permute-start | bytes 884744 | tf_op jit(solution)/shard_map/ppermute | solution.py:395
  9.6 34.1 %collective-permute-start.2 = (bf16[144,1024]{1,0:T(8,128)(2,1)}, bf16[144,1024]{1,0:T(8,128)(2,1)}, u32[]{:S(2)}, u32[]{:S(2)}) collective-permute-start(bf16[144,1024]{1,0:T(8,128)(2,1)} %get-tuple-element.52), channel_id=1, source_target_pairs={{0,12},{2,14},{4,8},{6,10},{8,4},{10,6},{12,0},{14,2},{1,13},{3,15... | collective-permute-start | bytes 884744 | tf_op jit(solution)/shard_map/ppermute | solution.py:395
  10.9 41.3 %collective-permute-start.9 = (bf16[1024,256]{1,0:T(8,128)(2,1)}, bf16[1024,256]{1,0:T(8,128)(2,1)S(1)}, u32[]{:S(2)}, u32[]{:S(2)}) collective-permute-start(bf16[1024,256]{1,0:T(8,128)(2,1)} %get-tuple-element.33), channel_id=1, source_target_pairs={{0,12},{2,14},{4,8},{6,10},{8,4},{10,6},{12,0},{14,2},{1,13},{3,15... | collective-permute-start | bytes 1572872 | tf_op jit(solution)/shard_map/ppermute | solution.py:395
  14.7 37.6 %collective-permute-start.5 = (bf16[1024,256]{1,0:T(8,128)(2,1)}, bf16[1024,256]{1,0:T(8,128)(2,1)S(1)}, u32[]{:S(2)}, u32[]{:S(2)}) collective-permute-start(bf16[1024,256]{1,0:T(8,128)(2,1)} %get-tuple-element.34), channel_id=1, source_target_pairs={{0,4},{2,6},{4,0},{6,2},{8,12},{10,14},{12,8},{14,10},{1,5},{3,7},... | collective-permute-start | bytes 1572872 | tf_op jit(solution)/shard_map/ppermute | solution.py:395
  20.8 59.8 %collective-permute-start.7 = (bf16[1024,256]{1,0:T(8,128)(2,1)}, bf16[1024,256]{1,0:T(8,128)(2,1)S(1)}, u32[]{:S(2)}, u32[]{:S(2)}) collective-permute-start(bf16[1024,256]{1,0:T(8,128)(2,1)} %get-tuple-element.36), channel_id=1, source_target_pairs={{0,8},{2,10},{4,12},{6,14},{8,0},{10,2},{12,4},{14,6},{1,9},{3,11}... | collective-permute-start | bytes 1572872 | tf_op jit(solution)/shard_map/ppermute | solution.py:395
  42.0 40.5 %collective-permute-start.4 = (bf16[1024,256]{1,0:T(8,128)(2,1)S(1)}, bf16[1024,256]{1,0:T(8,128)(2,1)}, u32[]{:S(2)}, u32[]{:S(2)}) collective-permute-start(bf16[1024,256]{1,0:T(8,128)(2,1)S(1)} %get-tuple-element.35), channel_id=1, source_target_pairs={{0,2},{2,0},{4,6},{6,4},{8,10},{10,8},{12,14},{14,12},{1,3},{3,1},... | collective-permute-start | bytes 1572872 | tf_op jit(solution)/shard_map/ppermute | solution.py:395
  46.2 34.4 %collective-permute-start.3 = (bf16[4,144,512]{2,1,0:T(8,128)(2,1)}, bf16[4,144,512]{2,1,0:T(8,128)(2,1)S(1)}, u32[]{:S(2)}, u32[]{:S(2)}) collective-permute-start(bf16[4,144,512]{2,1,0:T(8,128)(2,1)} %pad_maximum_fusion.2), channel_id=1, source_target_pairs={{0,2},{2,0},{4,6},{6,4},{8,10},{10,8},{12,14},{14,12},{1,3},{3,1},... | collective-permute-start | bytes 1769480 | tf_op jit(solution)/shard_map/ppermute | solution.py:395
  52.2 202.3 %collective-permute-start.16 = (bf16[4,512,1024]{2,1,0:T(8,128)(2,1)}, bf16[4,512,1024]{2,1,0:T(8,128)(2,1)}, u32[]{:S(2)}, u32[]{:S(2)}) collective-permute-start(bf16[4,512,1024]{2,1,0:T(8,128)(2,1)} %dynamic-slice_bitcast_fusion), channel_id=1, source_target_pairs={{0,2},{2,0},{4,6},{6,4},{8,10},{10,8},{12,14},{14,12},{1,3},{3,1},... | collective-permute-start | bytes 12582920 | tf_op jit(solution)/shard_map/ppermute | solution.py:395
  52.3 68.1 %collective-permute-start.10 = (bf16[1024,256]{1,0:T(8,128)(2,1)S(1)}, bf16[1024,256]{1,0:T(8,128)(2,1)}, u32[]{:S(2)}, u32[]{:S(2)}) collective-permute-start(bf16[1024,256]{1,0:T(8,128)(2,1)S(1)} %collective-permute-done.9), channel_id=1, source_target_pairs={{0,2},{2,0},{4,6},{6,4},{8,10},{10,8},{12,14},{14,12},{1,3},{3,1},... | collective-permute-start | bytes 1572872 | tf_op jit(solution)/shard_map/ppermute | solution.py:395
  80.6 26.9 %collective-permute-start.6 = (bf16[1024,256]{1,0:T(8,128)(2,1)S(1)}, bf16[1024,256]{1,0:T(8,128)(2,1)}, u32[]{:S(2)}, u32[]{:S(2)}) collective-permute-start(bf16[1024,256]{1,0:T(8,128)(2,1)S(1)} %collective-permute-done.5), channel_id=1, source_target_pairs={{0,2},{2,0},{4,6},{6,4},{8,10},{10,8},{12,14},{14,12},{1,3},{3,1},... | collective-permute-start | bytes 1572872 | tf_op jit(solution)/shard_map/ppermute | solution.py:395
  80.6 14.7 %collective-permute-start.8 = (bf16[1024,256]{1,0:T(8,128)(2,1)S(1)}, bf16[1024,256]{1,0:T(8,128)(2,1)}, u32[]{:S(2)}, u32[]{:S(2)}) collective-permute-start(bf16[1024,256]{1,0:T(8,128)(2,1)S(1)} %collective-permute-done.7), channel_id=1, source_target_pairs={{0,2},{2,0},{4,6},{6,4},{8,10},{10,8},{12,14},{14,12},{1,3},{3,1},... | collective-permute-start | bytes 1572872 | tf_op jit(solution)/shard_map/ppermute | solution.py:395
  141.2 50.2 %collective-permute-start.12 = (bf16[256,512]{1,0:T(8,128)(2,1)S(1)}, bf16[256,512]{1,0:T(8,128)(2,1)}, u32[]{:S(2)}, u32[]{:S(2)}) collective-permute-start(bf16[256,512]{1,0:T(8,128)(2,1)S(1)} %attend.10.mine), channel_id=1, source_target_pairs={{4,8},{6,10},{8,4},{10,6},{5,9},{7,11},{9,5},{11,7},{20,24},{22,26... | collective-permute-start | bytes 786440 | tf_op jit(solution)/shard_map/ppermute | solution.py:395
  142.6 53.2 %collective-permute-start.11 = (bf16[256,512]{1,0:T(8,128)(2,1)S(1)}, bf16[256,512]{1,0:T(8,128)(2,1)S(1)}, u32[]{:S(2)}, u32[]{:S(2)}) collective-permute-start(bf16[256,512]{1,0:T(8,128)(2,1)S(1)} %attend.10.mine), channel_id=1, source_target_pairs={{0,4},{2,6},{4,0},{6,2},{8,12},{10,14},{12,8},{14,10},{1,5},{3,7},... | collective-permute-start | bytes 786440 | tf_op jit(solution)/shard_map/ppermute | solution.py:395
  169.9 27.2 %collective-permute-start.31 = (bf16[256,512]{1,0:T(8,128)(2,1)S(1)}, bf16[256,512]{1,0:T(8,128)(2,1)S(1)}, u32[]{:S(2)}, u32[]{:S(2)}) collective-permute-start(bf16[256,512]{1,0:T(8,128)(2,1)S(1)} %attend.13.mine), channel_id=1, source_target_pairs={{0,4},{2,6},{4,0},{6,2},{8,12},{10,14},{12,8},{14,10},{1,5},{3,7},... | collective-permute-start | bytes 786440 | tf_op jit(solution)/shard_map/ppermute | solution.py:395
  190.7 41.7 %collective-permute-start.19 = (bf16[256,512]{1,0:T(8,128)(2,1)S(1)}, bf16[256,512]{1,0:T(8,128)(2,1)S(1)}, u32[]{:S(2)}, u32[]{:S(2)}) collective-permute-start(bf16[256,512]{1,0:T(8,128)(2,1)S(1)} %attend.11.mine), channel_id=1, source_target_pairs={{4,8},{6,10},{8,4},{10,6},{5,9},{7,11},{9,5},{11,7},{20,24},{22,26... | collective-permute-start | bytes 786440 | tf_op jit(solution)/shard_map/ppermute | solution.py:395
  191.4 44.9 %collective-permute-start.18 = (bf16[256,512]{1,0:T(8,128)(2,1)S(1)}, bf16[256,512]{1,0:T(8,128)(2,1)}, u32[]{:S(2)}, u32[]{:S(2)}) collective-permute-start(bf16[256,512]{1,0:T(8,128)(2,1)S(1)} %attend.11.mine), channel_id=1, source_target_pairs={{0,4},{2,6},{4,0},{6,2},{8,12},{10,14},{12,8},{14,10},{1,5},{3,7},... | collective-permute-start | bytes 786440 | tf_op jit(solution)/shard_map/ppermute | solution.py:395
  195.7 41.2 %collective-permute-start.32 = (bf16[256,512]{1,0:T(8,128)(2,1)S(1)}, bf16[256,512]{1,0:T(8,128)(2,1)}, u32[]{:S(2)}, u32[]{:S(2)}) collective-permute-start(bf16[256,512]{1,0:T(8,128)(2,1)S(1)} %attend.13.mine), channel_id=1, source_target_pairs={{4,8},{6,10},{8,4},{10,6},{5,9},{7,11},{9,5},{11,7},{20,24},{22,26... | collective-permute-start | bytes 786440 | tf_op jit(solution)/shard_map/ppermute | solution.py:395
  197.1 41.2 %collective-permute-start.33 = (bf16[256,512]{1,0:T(8,128)(2,1)S(1)}, bf16[256,512]{1,0:T(8,128)(2,1)}, u32[]{:S(2)}, u32[]{:S(2)}) collective-permute-start(bf16[256,512]{1,0:T(8,128)(2,1)S(1)} %collective-permute-done.31.near), channel_id=1, source_target_pairs={{4,8},{6,10},{8,4},{10,6},{5,9},{7,11},{9,5},{11,7},{20,24},{22,26... | collective-permute-start | bytes 786440 | tf_op jit(solution)/shard_map/ppermute | solution.py:395
  238.3 15.6 %collective-permute-start.35 = (bf16[256,512]{1,0:T(8,128)(2,1)}, bf16[256,512]{1,0:T(8,128)(2,1)S(1)}, u32[]{:S(2)}, u32[]{:S(2)}) collective-permute-start(bf16[256,512]{1,0:T(8,128)(2,1)} %collective-permute-done.33.in_b), channel_id=1, source_target_pairs={{4,0},{6,2},{8,12},{10,14},{5,1},{7,3},{9,13},{11,15},{20,16},{22,... | collective-permute-start | bytes 786440 | tf_op jit(solution)/shard_map/ppermute | solution.py:395
  242.4 22.0 %collective-permute-start.26 = (bf16[256,512]{1,0:T(8,128)(2,1)S(1)}, bf16[256,512]{1,0:T(8,128)(2,1)S(1)}, u32[]{:S(2)}, u32[]{:S(2)}) collective-permute-start(bf16[256,512]{1,0:T(8,128)(2,1)S(1)} %attend.12.mine), channel_id=1, source_target_pairs={{4,8},{6,10},{8,4},{10,6},{5,9},{7,11},{9,5},{11,7},{20,24},{22,26... | collective-permute-start | bytes 786440 | tf_op jit(solution)/shard_map/ppermute | solution.py:395
  243.7 20.8 %collective-permute-start.13 = (bf16[256,512]{1,0:T(8,128)(2,1)}, bf16[256,512]{1,0:T(8,128)(2,1)}, u32[]{:S(2)}, u32[]{:S(2)}) collective-permute-start(bf16[256,512]{1,0:T(8,128)(2,1)} %copy-done.18), channel_id=1, source_target_pairs={{4,8},{6,10},{8,4},{10,6},{5,9},{7,11},{9,5},{11,7},{20,24},{22,26... | collective-permute-start | bytes 786440 | tf_op jit(solution)/shard_map/ppermute | solution.py:395
  248.2 18.9 %collective-permute-start.21 = (bf16[256,512]{1,0:T(8,128)(2,1)}, bf16[256,512]{1,0:T(8,128)(2,1)S(1)}, u32[]{:S(2)}, u32[]{:S(2)}) collective-permute-start(bf16[256,512]{1,0:T(8,128)(2,1)} %copy-done.19), channel_id=1, source_target_pairs={{4,0},{6,2},{8,12},{10,14},{5,1},{7,3},{9,13},{11,15},{20,16},{22,... | collective-permute-start | bytes 786440 | tf_op jit(solution)/shard_map/ppermute | solution.py:395
  254.5 13.9 %collective-permute-start.22 = (bf16[256,512]{1,0:T(8,128)(2,1)S(1)}, bf16[256,512]{1,0:T(8,128)(2,1)S(1)}, u32[]{:S(2)}, u32[]{:S(2)}) collective-permute-start(bf16[256,512]{1,0:T(8,128)(2,1)S(1)} %collective-permute-done.20.in_b), channel_id=1, source_target_pairs={{4,0},{6,2},{8,12},{10,14},{5,1},{7,3},{9,13},{11,15},{20,16},{22,... | collective-permute-start | bytes 786440 | tf_op jit(solution)/shard_map/ppermute | solution.py:395
  264.4 26.0 %collective-permute-start.36 = (bf16[256,1024]{1,0:T(8,128)(2,1)}, bf16[256,1024]{1,0:T(8,128)(2,1)S(1)}, u32[]{:S(2)}, u32[]{:S(2)}) collective-permute-start(bf16[256,1024]{1,0:T(8,128)(2,1)} %get-tuple-element.32), channel_id=1, source_target_pairs={{0,2},{2,0},{4,6},{6,4},{8,10},{10,8},{12,14},{14,12},{1,3},{3,1},... | collective-permute-start | bytes 1572872 | tf_op jit(solution)/shard_map/ppermute | solution.py:395
  264.5 14.0 %collective-permute-start.28 = (bf16[256,512]{1,0:T(8,128)(2,1)S(1)}, bf16[256,512]{1,0:T(8,128)(2,1)S(1)}, u32[]{:S(2)}, u32[]{:S(2)}) collective-permute-start(bf16[256,512]{1,0:T(8,128)(2,1)S(1)} %collective-permute-done.26.in_a), channel_id=1, source_target_pairs={{4,0},{6,2},{8,12},{10,14},{5,1},{7,3},{9,13},{11,15},{20,16},{22,... | collective-permute-start | bytes 786440 | tf_op jit(solution)/shard_map/ppermute | solution.py:395
  265.8 15.4 %collective-permute-start.29 = (bf16[256,512]{1,0:T(8,128)(2,1)S(1)}, bf16[256,512]{1,0:T(8,128)(2,1)S(1)}, u32[]{:S(2)}, u32[]{:S(2)}) collective-permute-start(bf16[256,512]{1,0:T(8,128)(2,1)S(1)} %collective-permute-done.27.in_b), channel_id=1, source_target_pairs={{4,0},{6,2},{8,12},{10,14},{5,1},{7,3},{9,13},{11,15},{20,16},{22,... | collective-permute-start | bytes 786440 | tf_op jit(solution)/shard_map/ppermute | solution.py:395
  267.1 25.8 %collective-permute-start.14 = (bf16[256,512]{1,0:T(8,128)(2,1)}, bf16[256,512]{1,0:T(8,128)(2,1)S(1)}, u32[]{:S(2)}, u32[]{:S(2)}) collective-permute-start(bf16[256,512]{1,0:T(8,128)(2,1)} %collective-permute-done.12.in_a), channel_id=1, source_target_pairs={{4,0},{6,2},{8,12},{10,14},{5,1},{7,3},{9,13},{11,15},{20,16},{22,... | collective-permute-start | bytes 786440 | tf_op jit(solution)/shard_map/ppermute | solution.py:395
  268.4 24.5 %collective-permute-start.15 = (bf16[256,512]{1,0:T(8,128)(2,1)}, bf16[256,512]{1,0:T(8,128)(2,1)}, u32[]{:S(2)}, u32[]{:S(2)}) collective-permute-start(bf16[256,512]{1,0:T(8,128)(2,1)} %collective-permute-done.13.in_b), channel_id=1, source_target_pairs={{4,0},{6,2},{8,12},{10,14},{5,1},{7,3},{9,13},{11,15},{20,16},{22,... | collective-permute-start | bytes 786440 | tf_op jit(solution)/shard_map/ppermute | solution.py:395
  278.5 23.8 %collective-permute-start.23 = (bf16[256,1024]{1,0:T(8,128)(2,1)}, bf16[256,1024]{1,0:T(8,128)(2,1)S(1)}, u32[]{:S(2)}, u32[]{:S(2)}) collective-permute-start(bf16[256,1024]{1,0:T(8,128)(2,1)} %get-tuple-element.28), channel_id=1, source_target_pairs={{0,2},{2,0},{4,6},{6,4},{8,10},{10,8},{12,14},{14,12},{1,3},{3,1},... | collective-permute-start | bytes 1572872 | tf_op jit(solution)/shard_map/ppermute | solution.py:395
  291.4 15.0 %collective-permute-start.37 = (bf16[256,1024]{1,0:T(8,128)(2,1)}, bf16[256,1024]{1,0:T(8,128)(2,1)S(1)}, u32[]{:S(2)}, u32[]{:S(2)}) collective-permute-start(bf16[256,1024]{1,0:T(8,128)(2,1)} %add_convert_fusion.1), channel_id=1, source_target_pairs={{0,1},{1,0},{2,3},{3,2},{4,5},{5,4},{6,7},{7,6},{8,9},{9,8},{10,11... | collective-permute-start | bytes 1572872 | tf_op jit(solution)/shard_map/ppermute | solution.py:395
  302.5 14.7 %collective-permute-start.24 = (bf16[256,1024]{1,0:T(8,128)(2,1)S(1)}, bf16[256,1024]{1,0:T(8,128)(2,1)S(1)}, u32[]{:S(2)}, u32[]{:S(2)}) collective-permute-start(bf16[256,1024]{1,0:T(8,128)(2,1)S(1)} %add_convert_fusion.3), channel_id=1, source_target_pairs={{0,1},{1,0},{2,3},{3,2},{4,5},{5,4},{6,7},{7,6},{8,9},{9,8},{10,11... | collective-permute-start | bytes 1572872 | tf_op jit(solution)/shard_map/ppermute | solution.py:395
  (38 other events, 556.3 us)

commit v2 on v1

--- a/solution.py
+++ b/solution.py
@@ -17,6 +17,8 @@
 meta_rows = 16
 share = 16
 attend_vmem = 16 << 20
+project_vmem = 24 << 20
+chunks = ((False, 0, 2), (False, 2, 2), (True, 0, 2), (True, 2, 2))
 
 
 slab_rows = 512
@@ -123,25 +125,44 @@
     return lax.psum_scatter(terms, "rows", scatter_dimension=0, tiled=True).astype(jnp.bfloat16)
 
 
-def attend_kernel(chip, last, heads, tab, cnt, qb, qk, qp, *refs):
+def query_block(i, pos, part):
+    if part is None:
+        return i
+    mine, offset = part
+    return 4 * (pos[2] if mine else 1 - pos[2]) + offset + i
+
+
+def query_slot(i, pos, part):
+    block = query_block(i, pos, part)
+    return (block // 2) ^ pos[0], (block % 2) ^ pos[1]
+
+
+def attend_kernel(folded, part, last, heads, tab, pos, *refs):
     q_refs, refs = refs[:2], refs[2:]
     chips = 4 if last else 1
     kv_refs, refs = refs[: 2 * chips], refs[2 * chips :]
     if last:
-        acc_in, high_in, refs = refs[:chip], refs[chip : 2 * chip], refs[2 * chip :]
-        o_ref, kv, q_rows, sems, acc, high, top = refs
+        early = chips - len(folded)
+        acc_in, refs = refs[:early], refs[early:]
+        o_ref, kv, q_rows, sems, acc, top = refs
     else:
-        acc_out, high_out, kv, q_rows, sems = refs
-        acc, high = acc_out.at[0], high_out.at[0]
+        acc_out, kv, q_rows, sems = refs
+        acc = acc_out.at[0]
     step = pl.program_id(0)
     width = HEAD_WIDTH
     half = kv_refs[0].shape[0]
-    block = qb[step]
+    block = query_block(step, pos, part)
     lane = lax.broadcasted_iota(jnp.int32, (1, BLOCK_TOKENS), 1)
-
-    def fetch(which):
+    rows = heads * BLOCK_TOKENS
+    sums = acc.at[pl.ds(0, rows)]
+    high = acc.at[pl.ds(rows, 8), pl.ds(0, BLOCK_TOKENS)]
+
+    def fetch(which, place):
+        base = place * share
         copies = [
-            pltpu.make_async_copy(kv_refs[which * 2 + i], kv.at[pl.ds(half * i, half)], sems.at[i])
+            pltpu.make_async_copy(
+                kv_refs[which * 2 + i], kv.at[pl.ds(base + half * i, half)], sems.at[2 * place + i]
+            )
             for i in range(2)
         ]
         for copy in copies:
@@ -149,16 +170,17 @@
         for copy in copies:
             copy.wait()
 
-    def group_of(of, j):
+    def group_of(of, place, j):
+        base = place * share
         entries = [tab[of, block, j * key_group + p] for p in range(key_group)]
         hidden = [jnp.where(lane < e % 256, 0.0, masked_low) for e in entries]
-        values = jnp.concatenate([kv[e // 256, :, width:] for e in entries], axis=0)
+        values = jnp.concatenate([kv[base + e // 256, :, width:] for e in entries], axis=0)
         values = jnp.concatenate([values, jnp.ones_like(values)], axis=1)
-        keys = [kv[e // 256, :, :width] for e in entries]
+        keys = [kv[base + e // 256, :, :width] for e in entries]
         return keys, hidden, values
 
     def groups_of(of):
-        return (cnt[of, block] + (key_group - 1)) // key_group
+        return (tab[of, block, share] + (key_group - 1)) // key_group
 
     def exponents(keys, hidden, i):
         pair = jnp.concatenate(keys[i : i + 2], axis=0)
@@ -169,11 +191,13 @@
 
     @pl.when(step == 0)
     def _():
-        fetch(chips - 1)
-
+        for place, of in enumerate(folded):
+            fetch(of if last else 0, place)
+
+    other_core = query_slot(step, pos, part)[1]
     for which, q_ref in enumerate(q_refs):
 
-        @pl.when(qp[step] == which)
+        @pl.when(other_core == which)
         def _():
             for h in range(heads):
                 q_rows[h * BLOCK_TOKENS : (h + 1) * BLOCK_TOKENS] = q_ref[
@@ -181,14 +205,16 @@
                 ]
 
     if last:
-        acc[...] = functools.reduce(jnp.add, [a[0] for a in acc_in])
-        high[...] = functools.reduce(jnp.maximum, [a[0] for a in high_in])
+        sums[...] = functools.reduce(jnp.add, [a[0, :rows] for a in acc_in])
+        high[...] = functools.reduce(
+            jnp.maximum, [a[0, rows:, :BLOCK_TOKENS] for a in acc_in]
+        )
     else:
         acc[...] = jnp.zeros(acc.shape, jnp.float32)
         high[...] = jnp.full(high.shape, masked_low, jnp.float32)
 
-    def fold(j, carry):
-        keys, hidden, values = group_of(chip, j)
+    def fold(of, place, j, carry):
+        keys, hidden, values = group_of(of, place, j)
         probs = []
         highest = high[...]
         for i in range(0, key_group, 2):
@@ -197,26 +223,27 @@
                 highest = jnp.maximum(highest, jnp.max(side.reshape(-1, 8, BLOCK_TOKENS), axis=0))
             probs.append(jnp.exp2(x).astype(jnp.bfloat16))
         high[...] = highest
-        acc[...] += jnp.dot(
+        sums[...] += jnp.dot(
             jnp.concatenate(probs, axis=1), values, preferred_element_type=jnp.float32
         )
         return carry
 
-    lax.fori_loop(0, groups_of(chip), fold, 0)
+    for place, of in enumerate(folded):
+        lax.fori_loop(0, groups_of(of), functools.partial(fold, of, place), 0)
     if not last:
         return
 
-    unsafe = (jnp.max(high[...]) > 100.0) | (jnp.min(acc[:, width:]) < 2.0**-80)
+    unsafe = (jnp.max(high[...]) > 100.0) | (jnp.min(sums[:, width:]) < 2.0**-80)
 
     @pl.when(unsafe)
     def _():
-        acc[...] = jnp.zeros(acc.shape, jnp.float32)
+        sums[...] = jnp.zeros(sums.shape, jnp.float32)
         top[...] = jnp.full(top.shape, masked_low, jnp.float32)
         for of in range(chips):
-            fetch(of)
+            fetch(of, 0)
 
             def fold_top(j, carry):
-                keys, hidden, values = group_of(of, j)
+                keys, hidden, values = group_of(of, 0, j)
                 for i in range(0, key_group, 2):
                     x = exponents(keys, hidden, i)
                     before = top[...]
@@ -224,7 +251,7 @@
                     fade = jnp.exp2(before - after)
                     top[...] = after
                     probs = jnp.exp2(x - jnp.concatenate([after, after], axis=1))
-                    acc[...] = acc[...] * jnp.concatenate([fade, fade], axis=1) + jnp.dot(
+                    sums[...] = sums[...] * jnp.concatenate([fade, fade], axis=1) + jnp.dot(
                         probs.astype(jnp.bfloat16),
                         values[i * BLOCK_TOKENS : (i + 2) * BLOCK_TOKENS],
                         preferred_element_type=jnp.float32,
@@ -232,57 +259,57 @@
                 return carry
 
             lax.fori_loop(0, groups_of(of), fold_top, 0)
+        fetch(folded[0], 0)
 
     for h in range(heads):
-        rows = slice(h * BLOCK_TOKENS, (h + 1) * BLOCK_TOKENS)
-        o_ref[:, h * width : (h + 1) * width] = (acc[rows, :width] / acc[rows, width:]).astype(
+        at = slice(h * BLOCK_TOKENS, (h + 1) * BLOCK_TOKENS)
+        o_ref[:, h * width : (h + 1) * width] = (sums[at, :width] / sums[at, width:]).astype(
             o_ref.dtype
         )
 
 
-def attend(chip, lists, at, q_two, kv_refs, state=None):
+def attend(folded, tab, pos, q_two, kv_refs, count, part=None, state=None):
     last = state is not None
-    tab, cnt = lists
-    qb, qk, qp = at
-    count = qb.shape[0]
+    state = state or []
     width = q_two[0].shape[2]
     heads = width // HEAD_WIDTH
     rows = heads * BLOCK_TOKENS
-    blocks = tab.shape[2]
-    everyone = cnt.shape[1]
-    q_spec = pl.BlockSpec((1, BLOCK_TOKENS, width), lambda i, tab, cnt, qb, qk, qp: (qk[i], 0, 0))
-    acc_spec = pl.BlockSpec((1, rows, 2 * HEAD_WIDTH), lambda i, tab, cnt, qb, qk, qp: (qb[i], 0, 0))
-    high_spec = pl.BlockSpec((1, 8, BLOCK_TOKENS), lambda i, tab, cnt, qb, qk, qp: (qb[i], 0, 0))
+    q_spec = pl.BlockSpec(
+        (1, BLOCK_TOKENS, width), lambda i, tab, pos: (query_slot(i, pos, part)[0], 0, 0)
+    )
+    acc_block = (1, rows + 8, 2 * HEAD_WIDTH)
+
+    def acc_spec(whole):
+        if whole:
+            return pl.BlockSpec(acc_block, lambda i, tab, pos: (query_block(i, pos, part), 0, 0))
+        return pl.BlockSpec(acc_block, lambda i, tab, pos: (i + (part[1] if last else 0), 0, 0))
+
     scratch = [
-        pltpu.VMEM((blocks, BLOCK_TOKENS, 2 * HEAD_WIDTH), jnp.bfloat16),
+        pltpu.VMEM((len(folded) * share, BLOCK_TOKENS, 2 * HEAD_WIDTH), jnp.bfloat16),
         pltpu.VMEM((rows, HEAD_WIDTH), jnp.bfloat16),
-        pltpu.SemaphoreType.DMA((2,)),
+        pltpu.SemaphoreType.DMA((2 * len(folded),)),
     ]
     if last:
         out_shape = jax.ShapeDtypeStruct((count * BLOCK_TOKENS, width), jnp.bfloat16)
         out_specs = pl.BlockSpec((BLOCK_TOKENS, width), lambda i, *_: (i, 0))
         scratch += [
-            pltpu.VMEM((rows, 2 * HEAD_WIDTH), jnp.float32),
-            pltpu.VMEM((8, BLOCK_TOKENS), jnp.float32),
+            pltpu.VMEM((rows + 8, 2 * HEAD_WIDTH), jnp.float32),
             pltpu.VMEM((rows, HEAD_WIDTH), jnp.float32),
         ]
     else:
-        out_shape = (
-            jax.ShapeDtypeStruct((everyone, rows, 2 * HEAD_WIDTH), jnp.float32),
-            jax.ShapeDtypeStruct((everyone, 8, BLOCK_TOKENS), jnp.float32),
-        )
-        out_specs = (acc_spec, high_spec)
+        out_shape = jax.ShapeDtypeStruct((count, rows + 8, 2 * HEAD_WIDTH), jnp.float32)
+        out_specs = acc_spec(part is None)
     shape = (kv_refs[0].shape[0] // BLOCK_TOKENS, BLOCK_TOKENS, kv_refs[0].shape[1])
-    work = count * blocks // 2 * rows * BLOCK_TOKENS
+    work = count * len(folded) * share // 2 * rows * BLOCK_TOKENS
     return pl.pallas_call(
-        functools.partial(attend_kernel, chip, last, heads),
+        functools.partial(attend_kernel, folded, part, last, heads),
         out_shape=out_shape,
         grid_spec=pltpu.PrefetchScalarGridSpec(
-            num_scalar_prefetch=5,
+            num_scalar_prefetch=2,
             grid=(count,),
             in_specs=[q_spec] * 2
             + [pl.BlockSpec(memory_space=pl.ANY)] * len(kv_refs)
-            + ([acc_spec] * chip + [high_spec] * chip if last else []),
+            + [acc_spec(whole) for whole, _ in state],
             out_specs=out_specs,
             scratch_shapes=scratch,
         ),
@@ -291,79 +318,81 @@
             flops=work * 4 * HEAD_WIDTH * 4, bytes_accessed=work // 8, transcendentals=work
         ),
         name="attend",
-    )(
-        tab,
-        cnt,
-        qb,
-        qk,
-        qp,
-        *q_two,
-        *[a.reshape(shape) for a in kv_refs],
-        *((*[a for a, _ in state], *[h for _, h in state]) if last else ()),
-    )
-
-
-def project_kernel(at, middle, mine, near, in_a, in_b, out_a, out_b, w_own, w_swap, *refs):
-    own_ref, other_ref, one, two, sems = refs
-    column = pl.program_id(0)
-
-    @pl.when(column == 0)
+    )(tab, pos, *q_two, *[a.reshape(shape) for a in kv_refs], *[a for _, a in state])
+
+
+def piece_chip(i, z):
+    far = jnp.where(z < 2, 2, 1)
+    return z ^ i if i < 2 else far ^ (i % 2)
+
+
+def project_kernel(pos, near, come, out, w_own, w_swap, *refs):
+    own_ref, other_ref, parts, sems = refs
+    ends = (pos[0] == 0) | (pos[0] == 3)
+
+    def bring(i, source):
+        return pltpu.make_async_copy(source, parts.at[pl.ds(2 * i, 2)], sems.at[i])
+
+    bring(0, near).start()
+
+    @pl.when(ends)
     def _():
-        for flag, pair in ((1, (in_a, in_b)), (0, (out_a, out_b))):
-
-            @pl.when(middle[0] == flag)
-            def _():
-                copies = [
-                    pltpu.make_async_copy(pair[0], one, sems.at[0]),
-                    pltpu.make_async_copy(pair[1], two, sems.at[1]),
-                ]
-                for copy in copies:
-                    copy.start()
-                for copy in copies:
-                    copy.wait()
-
-    for w_ref, o_ref in ((w_swap, other_ref), (w_own, own_ref)):
-        total = None
-        for i, part in enumerate((mine, near, one, two)):
-            term = jnp.dot(part[...], w_ref[at[i]], preferred_element_type=jnp.float32)
-            total = term if total is None else total + term
-        o_ref[...] = total.astype(o_ref.dtype)
-
-
-def project(at, middle, parts, w_own, w_swap):
-    rows, depth = parts[0].shape
+        bring(1, out).start()
+
+    @pl.when(jnp.logical_not(ends))
+    def _():
+        bring(1, come).start()
+
+    for i in range(2):
+        bring(i, near).wait()
+    depth = near.shape[2]
+    tile = 256
+    own_rows = pl.ds(pl.multiple_of(pos[1] * depth, depth), depth)
+    places = [piece_chip(i, pos[0]) for i in range(4)]
+
+    for at in range(0, own_ref.shape[1], tile):
+        columns = slice(at, at + tile)
+        for w_ref, w_rows, o_ref in (
+            (w_swap, slice(0, depth), other_ref),
+            (w_own, own_rows, own_ref),
+        ):
+            terms = [
+                jnp.dot(
+                    parts[i],
+                    w_ref[places[i], w_rows, columns],
+                    preferred_element_type=jnp.float32,
+                )
+                for i in range(4)
+            ]
+            o_ref[:, columns] = functools.reduce(jnp.add, terms).astype(o_ref.dtype)
+
+
+def project(pos, near, come, out, w_own, w_swap):
+    rows, depth = near.shape[1:]
     chips, _, columns = w_own.shape
-    tile = 256
-    whole = pl.BlockSpec((rows, depth), lambda j, *_: (0, 0))
-    strip = pl.BlockSpec((rows, tile), lambda j, *_: (0, j))
-    result = jax.ShapeDtypeStruct((rows, columns), jnp.bfloat16)
+    vmem = pl.BlockSpec(memory_space=pltpu.VMEM)
     return pl.pallas_call(
         project_kernel,
-        out_shape=(jax.ShapeDtypeStruct((rows, columns), jnp.float32), result),
-        grid_spec=pltpu.PrefetchScalarGridSpec(
-            num_scalar_prefetch=2,
-            grid=(columns // tile,),
-            in_specs=[whole, whole]
-            + [pl.BlockSpec(memory_space=pl.ANY)] * 4
-            + [
-                pl.BlockSpec((chips, depth, tile), lambda j, at, middle: (0, at[chips], j)),
-                pl.BlockSpec((chips, depth, tile), lambda j, *_: (0, 0, j)),
-            ],
-            out_specs=(strip, strip),
-            scratch_shapes=[
-                pltpu.VMEM((rows, depth), jnp.bfloat16),
-                pltpu.VMEM((rows, depth), jnp.bfloat16),
-                pltpu.SemaphoreType.DMA((2,)),
-            ],
+        out_shape=(
+            jax.ShapeDtypeStruct((rows, columns), jnp.float32),
+            jax.ShapeDtypeStruct((rows, columns), jnp.bfloat16),
         ),
-        compiler_params=pltpu.CompilerParams(vmem_limit_bytes=60 << 20),
+        in_specs=[pl.BlockSpec(memory_space=pltpu.SMEM)]
+        + [pl.BlockSpec(memory_space=pl.ANY)] * 3
+        + [vmem] * 2,
+        out_specs=(vmem, vmem),
+        scratch_shapes=[
+            pltpu.VMEM((chips, rows, depth), jnp.bfloat16),
+            pltpu.SemaphoreType.DMA((2,)),
+        ],
+        compiler_params=pltpu.CompilerParams(vmem_limit_bytes=project_vmem),
         cost_estimate=pl.CostEstimate(
-            flops=2 * rows * 4 * depth * 2 * columns,
+            flops=2 * rows * chips * depth * 2 * columns,
             bytes_accessed=2 * (8 * depth * columns + 6 * rows * depth + 3 * rows * columns),
             transcendentals=0,
         ),
         name="project",
-    )(at, middle, *parts, w_own, w_swap)
+    )(pos, near, come, out, w_own, w_swap)
 
 
 def apart(k):
@@ -388,7 +417,7 @@
         ),
         axis=2,
     )
-    return tab, jnp.sum(ones, axis=2)
+    return jnp.concatenate([tab, jnp.sum(ones, axis=2, keepdims=True)], axis=2)
 
 
 def permute(array, perm, axis="tensor"):
@@ -437,50 +466,43 @@
     q_swap = swap(columns_of(q_come, 1 - core))
     q_two = (q_own, q_swap)
     notes = jnp.stack([q_own[:, q_len, :64], q_swap[:, q_len, :64]], axis=1)
-    lists = key_lists(notes.astype(jnp.int32), 2 * chips)
-
-    def places(blocks):
-        blocks = blocks.astype(jnp.int32)
-        k = (blocks // 2) ^ z
-        which = (blocks % 2) ^ core
-        return blocks, k.astype(jnp.int32), which.astype(jnp.int32)
-
-    everything = places(jnp.arange(2 * chips, dtype=jnp.int32))
-    state = [attend(k, lists, everything, q_two, kv[k]) for k in range(chips - 1)]
-
-    w_split = out_weight.reshape(chips, 2, depth, out_weight.shape[1])
-    w_swap = swap(lax.dynamic_index_in_dim(w_split, 1 - core, 1, keepdims=False))
+    tab = key_lists(notes.astype(jnp.int32), 2 * chips)
+    pos = jnp.stack([z, core, row]).astype(jnp.int32)
+    q_two = (q_own, q_swap)
+    whole = [attend((k,), tab, pos, q_two, kv[k], 2 * chips) for k in range(2)]
+    halves = [attend((2,), tab, pos, q_two, kv[2], chips, (mine, 0)) for mine in (False, True)]
+
     w_own = out_weight.reshape(chips, wide, out_weight.shape[1])
-    far_chip = jnp.where(z < 2, 2, 1)
-    chip_of = jnp.stack([z, z ^ 1, far_chip, far_chip ^ 1])
-    at = jnp.concatenate([chip_of, core[None]]).astype(jnp.int32)
-    middle = ((z == 1) | (z == 2)).astype(jnp.int32).reshape(1)
+    w_swap = lax.dynamic_slice(
+        w_own, (0, (1 - core) * depth, 0), (chips, depth, out_weight.shape[1])
+    )
+    w_swap = swap(w_swap)
     across = [(2, 4), (3, 5), (4, 2), (5, 3)]
     outward = [(2, 0), (3, 1), (4, 6), (5, 7)]
-    last = chips - 1
-
-    def chunk(chip):
-        pieces = places(2 * chip + jnp.arange(2, dtype=jnp.int32))
-        every_key = [a for of in kv for a in of]
-        mine = attend(last, lists, pieces, q_two, every_key, state)
-        beside = permute(mine, apart(2))
-        in_a = permute(mine, across)
-        in_b = permute(beside, across)
-        out_a = permute(in_a, outward)
-        out_b = permute(in_b, outward)
-        own, other = project(at, middle, (mine, beside, in_a, in_b, out_a, out_b), w_own, w_swap)
+    every_key = [a for of in kv for a in of]
+
+    def chunk(part, count):
+        state = [(True, a) for a in whole] + [(False, halves[part[0]])]
+        mine = attend((3,), tab, pos, q_two, every_key, count, part, state)
+        near = jnp.stack([mine, permute(mine, apart(2))])
+        come = permute(near, across)
+        out = permute(come, outward)
+        own, other = project(pos, near, come, out, w_own, w_swap)
         return own, swap(other)
 
     theirs = []
-    for i in range(2):
-        own, come = chunk(2 * (1 - row) + i)
-        term = (own + come.astype(jnp.float32)).astype(jnp.bfloat16)
-        theirs.append(permute(term, [(0, 1), (1, 0)], "rows"))
     ours = []
-    for i in range(2):
-        own, come = chunk(2 * row + i)
-        ours.append(own + come.astype(jnp.float32) + theirs[i].astype(jnp.float32))
-    return jnp.concatenate(ours, axis=0).astype(jnp.bfloat16)
+    for mine, offset, count in chunks:
+        own, come = chunk((mine, offset), count)
+        total = own + come.astype(jnp.float32)
+        if mine:
+            come = jnp.concatenate(theirs, axis=0) if len(theirs) > 1 else theirs[0]
+            come = come[offset * BLOCK_TOKENS : (offset + count) * BLOCK_TOKENS]
+            ours.append((total + come.astype(jnp.float32)).astype(jnp.bfloat16))
+        else:
+            sent = total.astype(jnp.bfloat16)
+            theirs.append(permute(sent, [(0, 1), (1, 0)], "rows"))
+    return jnp.concatenate(ours, axis=0)
 
 
 def solution(mesh):

time: 321 us -> 317 us (0.988)
  waiting for transfers between devices: 75.9 us -> 93.4 us
  starting transfers between devices: 44.7 us -> 31.9 us
  Pallas kernels: 173 us -> 169 us
    ppermute x38 -> x30, waiting for transfers between devices: 75.9 us -> 93.4 us  [permute(): return lax.ppermute(array, axis, perm)]
    pallas_call x4, Pallas kernels: 33.8 us -> 18.9 us  [project(): pl.pallas_call(project_kernel, out_shape=(jax.ShapeDtypeStruct((rows, col...]
    ppermute x38 -> x30, starting transfers between devices: 44.7 us -> 31.9 us  [permute(): return lax.ppermute(array, axis, perm)]
    pallas_call x7 -> x8, Pallas kernels: 139 us -> 150 us  [attend(): pl.pallas_call(functools.partial(attend_kernel, folded, part, last, heads...]
    squeeze x1 -> x0, local copies, waits for them, and re-layouts: 4.73 us -> none  [exchanged_shards(): lax.dynamic_index_in_dim(w_split, 1 - core, 1, keepdims=False)]
    dynamic_slice x0 -> x1, local copies, waits for them, and re-layouts: none -> 4.66 us  [exchanged_shards(): lax.dynamic_slice(w_own, (0, (1 - core) * depth, 0), (chips, depth, out_w...]
  transfers between devices with their start and end apart: 38 -> 30, of which waited for: 9 -> 10; matrix products, arithmetic and copies ran while one was open for 6% -> 5% of each run, Pallas kernels for 54% -> 54%
where the time goes in v2:
time: 317 us; the launch traced here: 314 us
  Pallas kernels  169 us (53%)
  waiting for transfers between devices  93.4 us (29%)
  starting transfers between devices  31.9 us (10%)
  local copies, waits for them, and re-layouts  12.9 us (4%)
  other arithmetic  6.68 us (2%)
    pallas_call x8, Pallas kernels, attend(): pl.pallas_call(functools.partial(attend_kernel, folded, part, last, heads...  150 us
    ppermute x30, waiting for transfers between devices, permute(): return lax.ppermute(array, axis, perm)  93.4 us
    ppermute x30, starting transfers between devices, permute(): return lax.ppermute(array, axis, perm)  31.9 us
    pallas_call x4, Pallas kernels, project(): pl.pallas_call(project_kernel, out_shape=(jax.ShapeDtypeStruct((rows, col...  18.9 us
  transfers between devices with their start and end apart: 30, of which 10 were waited for; matrix products, arithmetic and copies ran while one was open for 5% of the time, Pallas kernels for 54%

profile of v2, /device:TPU:0, one launch (start us, length us, event | category | flops | bytes accessed | tf_op | source)
XLA Modules:
  0.0 314.1 jit_solution(18245158551803550158)
XLA Ops:
  4.0 3.1 collective-permute-start
  7.0 2.6 collective-permute-start.1
  10.9 3.8 %collective-permute-start.9 = (bf16[1024,256]{1,0:T(8,128)(2,1)}, bf16[1024,256]{1,0:T(8,128)(2,1)S(1)}, u32[]{:S(2)}, u32[]{:S(2)}) collective-permute-start(bf16[1024,256]{1,0:T(8,128)(2,1)} %get-tuple-element.21), channel_id=1, source_target_pairs={{0,12},{2,14},{4,8},{6,10},{8,4},{10,6},{12,0},{14,2},{1,13},{3,15... | collective-permute-start | bytes 1572872 | tf_op jit(solution)/shard_map/ppermute | solution.py:424
  14.8 6.0 %collective-permute-done = bf16[144,1024]{1,0:T(8,128)(2,1)} collective-permute-done((bf16[144,1024]{1,0:T(8,128)(2,1)}, bf16[144,1024]{1,0:T(8,128)(2,1)}, u32[]{:S(2)}, u32[]{:S(2)}) %collective-permute-start) | collective-permute-done | bytes 294944 | tf_op jit(solution)/shard_map/ppermute | solution.py:424
  20.8 2.1 collective-permute-start.7
  22.9 1.7 dynamic-slice_bitcast_fusion.6
  24.6 17.5 %collective-permute-done.1 = bf16[144,1024]{1,0:T(8,128)(2,1)} collective-permute-done((bf16[144,1024]{1,0:T(8,128)(2,1)}, bf16[144,1024]{1,0:T(8,128)(2,1)}, u32[]{:S(2)}, u32[]{:S(2)}) %collective-permute-start.1) | collective-permute-done | bytes 294944 | tf_op jit(solution)/shard_map/ppermute | solution.py:424
  42.0 1.7 dynamic-slice_bitcast_fusion.5
  46.9 4.7 %constant_dynamic-slice_fusion = bf16[4,512,1024]{2,1,0:T(8,128)(2,1)} fusion(bf16[4,1024,1024]{2,1,0:T(8,128)(2,1)} %bitcast.40, s32[]{:T(128)S(6)} %select_n.63), kind=kLoop, calls=%fused_computation.41 | loop fusion | bytes 8388612 | tf_op jit(solution)/shard_map/dynamic_slice | solution.py:476
  52.2 28.3 %collective-permute-done.7 = bf16[1024,256]{1,0:T(8,128)(2,1)S(1)} collective-permute-done((bf16[1024,256]{1,0:T(8,128)(2,1)}, bf16[1024,256]{1,0:T(8,128)(2,1)S(1)}, u32[]{:S(2)}, u32[]{:S(2)}) %collective-permute-start.7) | collective-permute-done | bytes 524320 | tf_op jit(solution)/shard_map/ppermute | solution.py:424
  82.7 12.9 %attend.8.refs_10_ = f32[8,520,256]{2,1,0:T(8,128)S(1)} custom-call(s32[4,8,17]{2,1,0:T(8,128)S(1)} %pad_add_fusion.tab, s32[3]{0:T(128)S(1)} %pad_add_fusion.1.pos, bf16[4,144,512]{2,1,0:T(8,128)(2,1)S(1)} %pad_maximum_fusion.1.refs_0_, bf16[4,144,512]{2,1,0:T(8,128)(2,1)S(1)} %collective-permute-done.3.refs_1_, bf16[8,128,256]{2,1,0:T(8,128)(2,1)S(1)} %bitcast.47, ...), custom_call_target="tpu_custom_call" | custom-call | flops 8589934592 | bytes 524288 | tf_op jit(solution)/shard_map/attend/pallas_call | solution.py:304
  95.6 12.7 %attend.9.refs_11_ = f32[8,520,256]{2,1,0:T(8,128)S(1)} custom-call(s32[4,8,17]{2,1,0:T(8,128)S(1)} %pad_add_fusion.tab, s32[3]{0:T(128)S(1)} %pad_add_fusion.1.pos, bf16[4,144,512]{2,1,0:T(8,128)(2,1)S(1)} %pad_maximum_fusion.1.refs_0_, bf16[4,144,512]{2,1,0:T(8,128)(2,1)S(1)} %collective-permute-done.3.refs_1_, bf16[8,128,256]{2,1,0:T(8,128)(2,1)S(1)} %bitcast.56, ...), custom_call_target="tpu_custom_call" | custom-call | flops 8589934592 | bytes 524288 | tf_op jit(solution)/shard_map/attend/pallas_call | solution.py:304
  108.3 6.2 %attend.12.refs_12_ = f32[4,520,256]{2,1,0:T(8,128)S(1)} custom-call(s32[4,8,17]{2,1,0:T(8,128)S(1)} %pad_add_fusion.tab, s32[3]{0:T(128)S(1)} %pad_add_fusion.1.pos, bf16[4,144,512]{2,1,0:T(8,128)(2,1)S(1)} %pad_maximum_fusion.1.refs_0_, bf16[4,144,512]{2,1,0:T(8,128)(2,1)S(1)} %collective-permute-done.3.refs_1_, bf16[8,128,256]{2,1,0:T(8,128)(2,1)S(1)} %bitcast.61, ...), custom_call_target="tpu_custom_call" | custom-call | flops 4294967296 | bytes 262144 | tf_op jit(solution)/shard_map/attend/pallas_call | solution.py:304
  114.5 22.8 %attend.13 = bf16[256,512]{1,0:T(8,128)(2,1)S(1)} custom-call(s32[4,8,17]{2,1,0:T(8,128)S(1)} %pad_add_fusion.tab, s32[3]{0:T(128)S(1)} %pad_add_fusion.1.pos, bf16[4,144,512]{2,1,0:T(8,128)(2,1)S(1)} %pad_maximum_fusion.1.refs_0_, bf16[4,144,512]{2,1,0:T(8,128)(2,1)S(1)} %collective-permute-done.3.refs_1_, bf16[8,128,256]{2,1,0:T(8,128)(2,1)S(1)} %bitcast.48, ...), custom_call_target="tpu_custom_call" | custom-call | flops 2147483648 | bytes 131072 | tf_op jit(solution)/shard_map/attend/pallas_call | solution.py:304
  137.7 27.8 %attend.15 = bf16[256,512]{1,0:T(8,128)(2,1)S(1)} custom-call(s32[4,8,17]{2,1,0:T(8,128)S(1)} %pad_add_fusion.tab, s32[3]{0:T(128)S(1)} %pad_add_fusion.1.pos, bf16[4,144,512]{2,1,0:T(8,128)(2,1)S(1)} %pad_maximum_fusion.1.refs_0_, bf16[4,144,512]{2,1,0:T(8,128)(2,1)S(1)} %collective-permute-done.3.refs_1_, bf16[8,128,256]{2,1,0:T(8,128)(2,1)S(1)} %bitcast.49, ...), custom_call_target="tpu_custom_call" | custom-call | flops 2147483648 | bytes 131072 | tf_op jit(solution)/shard_map/attend/pallas_call | solution.py:304
  166.7 7.9 %attend.10.refs_12_ = f32[4,520,256]{2,1,0:T(8,128)S(1)} custom-call(s32[4,8,17]{2,1,0:T(8,128)S(1)} %pad_add_fusion.tab, s32[3]{0:T(128)S(1)} %pad_add_fusion.1.pos, bf16[4,144,512]{2,1,0:T(8,128)(2,1)S(1)} %pad_maximum_fusion.1.refs_0_, bf16[4,144,512]{2,1,0:T(8,128)(2,1)S(1)} %collective-permute-done.3.refs_1_, bf16[8,128,256]{2,1,0:T(8,128)(2,1)S(1)} %bitcast.64, ...), custom_call_target="tpu_custom_call" | custom-call | flops 4294967296 | bytes 262144 | tf_op jit(solution)/shard_map/attend/pallas_call | solution.py:304
  175.4 36.2 %attend.14 = bf16[256,512]{1,0:T(8,128)(2,1)S(1)} custom-call(s32[4,8,17]{2,1,0:T(8,128)S(1)} %pad_add_fusion.tab, s32[3]{0:T(128)S(1)} %pad_add_fusion.1.pos, bf16[4,144,512]{2,1,0:T(8,128)(2,1)S(1)} %pad_maximum_fusion.1.refs_0_, bf16[4,144,512]{2,1,0:T(8,128)(2,1)S(1)} %collective-permute-done.3.refs_1_, bf16[8,128,256]{2,1,0:T(8,128)(2,1)S(1)} %bitcast.50, ...), custom_call_target="tpu_custom_call" | custom-call | flops 2147483648 | bytes 131072 | tf_op jit(solution)/shard_map/attend/pallas_call | solution.py:304
  211.6 3.5 %collective-permute-start.21 = (bf16[256,512]{1,0:T(8,128)(2,1)S(1)}, bf16[256,512]{1,0:T(8,128)(2,1)S(1)}, u32[]{:S(2)}, u32[]{:S(2)}) collective-permute-start(bf16[256,512]{1,0:T(8,128)(2,1)S(1)} %attend.14), channel_id=1, source_target_pairs={{0,4},{2,6},{4,0},{6,2},{8,12},{10,14},{12,8},{14,10},{1,5},{3,7},... | collective-permute-start | bytes 786440 | tf_op jit(solution)/shard_map/ppermute | solution.py:424
  215.9 23.5 %attend.11 = bf16[256,512]{1,0:T(8,128)(2,1)S(1)} custom-call(s32[4,8,17]{2,1,0:T(8,128)S(1)} %pad_add_fusion.tab, s32[3]{0:T(128)S(1)} %pad_add_fusion.1.pos, bf16[4,144,512]{2,1,0:T(8,128)(2,1)S(1)} %pad_maximum_fusion.1.refs_0_, bf16[4,144,512]{2,1,0:T(8,128)(2,1)S(1)} %collective-permute-done.3.refs_1_, bf16[8,128,256]{2,1,0:T(8,128)(2,1)S(1)} %bitcast.51, ...), custom_call_target="tpu_custom_call" | custom-call | flops 2147483648 | bytes 131072 | tf_op jit(solution)/shard_map/attend/pallas_call | solution.py:304
  242.6 5.3 %collective-permute-done.11 = bf16[256,512]{1,0:T(8,128)(2,1)S(1)} collective-permute-done((bf16[256,512]{1,0:T(8,128)(2,1)S(1)}, bf16[256,512]{1,0:T(8,128)(2,1)S(1)}, u32[]{:S(2)}, u32[]{:S(2)}) %collective-permute-start.11) | collective-permute-done | bytes 262176 | tf_op jit(solution)/shard_map/ppermute | solution.py:424
  251.2 7.9 %collective-permute-done.27.out = bf16[2,256,512]{2,1,0:T(8,128)(2,1)S(1)} collective-permute-done((bf16[2,256,512]{2,1,0:T(8,128)(2,1)S(1)}, bf16[2,256,512]{2,1,0:T(8,128)(2,1)S(1)}, u32[]{:S(2)}, u32[]{:S(2)}) %collective-permute-start.27) | collective-permute-done | bytes 524320 | tf_op jit(solution)/shard_map/ppermute | solution.py:424
  259.1 4.7 %project.7 = (f32[256,1024]{1,0:T(8,128)S(1)}, bf16[256,1024]{1,0:T(8,128)(2,1)S(1)}) custom-call(s32[3]{0:T(128)S(1)} %pad_add_fusion.1.pos, bf16[2,256,512]{2,1,0:T(8,128)(2,1)S(1)} %pad_maximum_fusion.6.near, bf16[2,256,512]{2,1,0:T(8,128)(2,1)S(1)} %collective-permute-done.26.come, bf16[2,256,512]{2,1,0:T(8,128)(2,1)S(1)} %collective-permute-done.27.out, ...), custom_call_target="tpu_custom_call" | custom-call | flops 2147483648 | bytes 11534336 | tf_op jit(solution)/shard_map/project/pallas_call | solution.py:374
  265.2 5.2 %collective-permute-done.18.out = bf16[2,256,512]{2,1,0:T(8,128)(2,1)S(1)} collective-permute-done((bf16[2,256,512]{2,1,0:T(8,128)(2,1)S(1)}, bf16[2,256,512]{2,1,0:T(8,128)(2,1)S(1)}, u32[]{:S(2)}, u32[]{:S(2)}) %collective-permute-start.18) | collective-permute-done | bytes 524320 | tf_op jit(solution)/shard_map/ppermute | solution.py:424
  270.3 4.7 %project.5 = (f32[256,1024]{1,0:T(8,128)S(1)}, bf16[256,1024]{1,0:T(8,128)(2,1)S(1)}) custom-call(s32[3]{0:T(128)S(1)} %pad_add_fusion.1.pos, bf16[2,256,512]{2,1,0:T(8,128)(2,1)S(1)} %pad_maximum_fusion.4.near, bf16[2,256,512]{2,1,0:T(8,128)(2,1)S(1)} %collective-permute-done.17.come, bf16[2,256,512]{2,1,0:T(8,128)(2,1)S(1)} %collective-permute-done.18.out, ...), custom_call_target="tpu_custom_call" | custom-call | flops 2147483648 | bytes 11534336 | tf_op jit(solution)/shard_map/project/pallas_call | solution.py:374
  275.1 6.5 %collective-permute-done.23.out = bf16[2,256,512]{2,1,0:T(8,128)(2,1)S(1)} collective-permute-done((bf16[2,256,512]{2,1,0:T(8,128)(2,1)S(1)}, bf16[2,256,512]{2,1,0:T(8,128)(2,1)S(1)}, u32[]{:S(2)}, u32[]{:S(2)}) %collective-permute-start.23) | collective-permute-done | bytes 524320 | tf_op jit(solution)/shard_map/ppermute | solution.py:424
  281.6 4.9 %project.6 = (f32[256,1024]{1,0:T(8,128)S(1)}, bf16[256,1024]{1,0:T(8,128)(2,1)S(1)}) custom-call(s32[3]{0:T(128)S(1)} %pad_add_fusion.1.pos, bf16[2,256,512]{2,1,0:T(8,128)(2,1)S(1)} %pad_maximum_fusion.5.near, bf16[2,256,512]{2,1,0:T(8,128)(2,1)S(1)} %collective-permute-done.22.come, bf16[2,256,512]{2,1,0:T(8,128)(2,1)S(1)} %collective-permute-done.23.out, ...), custom_call_target="tpu_custom_call" | custom-call | flops 2147483648 | bytes 11534336 | tf_op jit(solution)/shard_map/project/pallas_call | solution.py:374
  286.7 2.3 collective-permute-start.29
  289.0 2.7 collective-permute-done.13.out
  291.7 4.7 %project.4 = (f32[256,1024]{1,0:T(8,128)S(1)}, bf16[256,1024]{1,0:T(8,128)(2,1)S(1)}) custom-call(s32[3]{0:T(128)S(1)} %pad_add_fusion.1.pos, bf16[2,256,512]{2,1,0:T(8,128)(2,1)S(1)} %pad_maximum_fusion.3.near, bf16[2,256,512]{2,1,0:T(8,128)(2,1)S(1)} %collective-permute-done.12.come, bf16[2,256,512]{2,1,0:T(8,128)(2,1)S(1)} %collective-permute-done.13.out, ...), custom_call_target="tpu_custom_call" | custom-call | flops 2147483648 | bytes 11534336 | tf_op jit(solution)/shard_map/project/pallas_call | solution.py:374
  296.6 1.9 collective-permute-start.20
  298.5 3.3 %collective-permute-done.29 = bf16[256,1024]{1,0:T(8,128)(2,1)S(1)} collective-permute-done((bf16[256,1024]{1,0:T(8,128)(2,1)S(1)}, bf16[256,1024]{1,0:T(8,128)(2,1)S(1)}, u32[]{:S(2)}, u32[]{:S(2)}) %collective-permute-start.29) | collective-permute-done | bytes 524320 | tf_op jit(solution)/shard_map/ppermute | solution.py:424
  302.1 10.8 %collective-permute-done.20 = bf16[256,1024]{1,0:T(8,128)(2,1)S(1)} collective-permute-done((bf16[256,1024]{1,0:T(8,128)(2,1)S(1)}, bf16[256,1024]{1,0:T(8,128)(2,1)S(1)}, u32[]{:S(2)}, u32[]{:S(2)}) %collective-permute-start.20) | collective-permute-done | bytes 524320 | tf_op jit(solution)/shard_map/ppermute | solution.py:424
  (95 shorter events, 24.3 us)
Async XLA Ops:
  4.0 16.8 %collective-permute-start = (bf16[144,1024]{1,0:T(8,128)(2,1)}, bf16[144,1024]{1,0:T(8,128)(2,1)}, u32[]{:S(2)}, u32[]{:S(2)}) collective-permute-start(bf16[144,1024]{1,0:T(8,128)(2,1)} %get-tuple-element.38), channel_id=1, source_target_pairs={{0,4},{2,6},{4,0},{6,2},{8,12},{10,14},{12,8},{14,10},{1,5},{3,7},... | collective-permute-start | bytes 884744 | tf_op jit(solution)/shard_map/ppermute | solution.py:424
  7.0 35.0 %collective-permute-start.1 = (bf16[144,1024]{1,0:T(8,128)(2,1)}, bf16[144,1024]{1,0:T(8,128)(2,1)}, u32[]{:S(2)}, u32[]{:S(2)}) collective-permute-start(bf16[144,1024]{1,0:T(8,128)(2,1)} %get-tuple-element.39), channel_id=1, source_target_pairs={{0,8},{2,10},{4,12},{6,14},{8,0},{10,2},{12,4},{14,6},{1,9},{3,11}... | collective-permute-start | bytes 884744 | tf_op jit(solution)/shard_map/ppermute | solution.py:424
  9.6 34.1 %collective-permute-start.2 = (bf16[144,1024]{1,0:T(8,128)(2,1)}, bf16[144,1024]{1,0:T(8,128)(2,1)}, u32[]{:S(2)}, u32[]{:S(2)}) collective-permute-start(bf16[144,1024]{1,0:T(8,128)(2,1)} %get-tuple-element.40), channel_id=1, source_target_pairs={{0,12},{2,14},{4,8},{6,10},{8,4},{10,6},{12,0},{14,2},{1,13},{3,15... | collective-permute-start | bytes 884744 | tf_op jit(solution)/shard_map/ppermute | solution.py:424
  10.9 40.7 %collective-permute-start.9 = (bf16[1024,256]{1,0:T(8,128)(2,1)}, bf16[1024,256]{1,0:T(8,128)(2,1)S(1)}, u32[]{:S(2)}, u32[]{:S(2)}) collective-permute-start(bf16[1024,256]{1,0:T(8,128)(2,1)} %get-tuple-element.21), channel_id=1, source_target_pairs={{0,12},{2,14},{4,8},{6,10},{8,4},{10,6},{12,0},{14,2},{1,13},{3,15... | collective-permute-start | bytes 1572872 | tf_op jit(solution)/shard_map/ppermute | solution.py:424
  14.7 37.0 %collective-permute-start.5 = (bf16[1024,256]{1,0:T(8,128)(2,1)}, bf16[1024,256]{1,0:T(8,128)(2,1)S(1)}, u32[]{:S(2)}, u32[]{:S(2)}) collective-permute-start(bf16[1024,256]{1,0:T(8,128)(2,1)} %get-tuple-element.22), channel_id=1, source_target_pairs={{0,4},{2,6},{4,0},{6,2},{8,12},{10,14},{12,8},{14,10},{1,5},{3,7},... | collective-permute-start | bytes 1572872 | tf_op jit(solution)/shard_map/ppermute | solution.py:424
  20.8 59.8 %collective-permute-start.7 = (bf16[1024,256]{1,0:T(8,128)(2,1)}, bf16[1024,256]{1,0:T(8,128)(2,1)S(1)}, u32[]{:S(2)}, u32[]{:S(2)}) collective-permute-start(bf16[1024,256]{1,0:T(8,128)(2,1)} %get-tuple-element.24), channel_id=1, source_target_pairs={{0,8},{2,10},{4,12},{6,14},{8,0},{10,2},{12,4},{14,6},{1,9},{3,11}... | collective-permute-start | bytes 1572872 | tf_op jit(solution)/shard_map/ppermute | solution.py:424
  42.0 40.7 %collective-permute-start.4 = (bf16[1024,256]{1,0:T(8,128)(2,1)S(1)}, bf16[1024,256]{1,0:T(8,128)(2,1)}, u32[]{:S(2)}, u32[]{:S(2)}) collective-permute-start(bf16[1024,256]{1,0:T(8,128)(2,1)S(1)} %get-tuple-element.23), channel_id=1, source_target_pairs={{0,2},{2,0},{4,6},{6,4},{8,10},{10,8},{12,14},{14,12},{1,3},{3,1},... | collective-permute-start | bytes 1572872 | tf_op jit(solution)/shard_map/ppermute | solution.py:424
  46.3 34.3 %collective-permute-start.3 = (bf16[4,144,512]{2,1,0:T(8,128)(2,1)}, bf16[4,144,512]{2,1,0:T(8,128)(2,1)S(1)}, u32[]{:S(2)}, u32[]{:S(2)}) collective-permute-start(bf16[4,144,512]{2,1,0:T(8,128)(2,1)} %pad_maximum_fusion.2), channel_id=1, source_target_pairs={{0,2},{2,0},{4,6},{6,4},{8,10},{10,8},{12,14},{14,12},{1,3},{3,1},... | collective-permute-start | bytes 1769480 | tf_op jit(solution)/shard_map/ppermute | solution.py:424
  51.7 207.4 %collective-permute-start.14 = (bf16[4,512,1024]{2,1,0:T(8,128)(2,1)}, bf16[4,512,1024]{2,1,0:T(8,128)(2,1)}, u32[]{:S(2)}, u32[]{:S(2)}) collective-permute-start(bf16[4,512,1024]{2,1,0:T(8,128)(2,1)} %constant_dynamic-slice_fusion), channel_id=1, source_target_pairs={{0,2},{2,0},{4,6},{6,4},{8,10},{10,8},{12,14},{14,12},{1,3},{3,1},... | collective-permute-start | bytes 12582920 | tf_op jit(solution)/shard_map/ppermute | solution.py:424
  51.8 62.8 %collective-permute-start.10 = (bf16[1024,256]{1,0:T(8,128)(2,1)S(1)}, bf16[1024,256]{1,0:T(8,128)(2,1)}, u32[]{:S(2)}, u32[]{:S(2)}) collective-permute-start(bf16[1024,256]{1,0:T(8,128)(2,1)S(1)} %collective-permute-done.9), channel_id=1, source_target_pairs={{0,2},{2,0},{4,6},{6,4},{8,10},{10,8},{12,14},{14,12},{1,3},{3,1},... | collective-permute-start | bytes 1572872 | tf_op jit(solution)/shard_map/ppermute | solution.py:424
  80.6 15.0 %collective-permute-start.6 = (bf16[1024,256]{1,0:T(8,128)(2,1)S(1)}, bf16[1024,256]{1,0:T(8,128)(2,1)}, u32[]{:S(2)}, u32[]{:S(2)}) collective-permute-start(bf16[1024,256]{1,0:T(8,128)(2,1)S(1)} %collective-permute-done.5), channel_id=1, source_target_pairs={{0,2},{2,0},{4,6},{6,4},{8,10},{10,8},{12,14},{14,12},{1,3},{3,1},... | collective-permute-start | bytes 1572872 | tf_op jit(solution)/shard_map/ppermute | solution.py:424
  80.6 27.7 %collective-permute-start.8 = (bf16[1024,256]{1,0:T(8,128)(2,1)S(1)}, bf16[1024,256]{1,0:T(8,128)(2,1)}, u32[]{:S(2)}, u32[]{:S(2)}) collective-permute-start(bf16[1024,256]{1,0:T(8,128)(2,1)S(1)} %collective-permute-done.7), channel_id=1, source_target_pairs={{0,2},{2,0},{4,6},{6,4},{8,10},{10,8},{12,14},{14,12},{1,3},{3,1},... | collective-permute-start | bytes 1572872 | tf_op jit(solution)/shard_map/ppermute | solution.py:424
  137.3 77.7 %collective-permute-start.16 = (bf16[256,512]{1,0:T(8,128)(2,1)S(1)}, bf16[256,512]{1,0:T(8,128)(2,1)S(1)}, u32[]{:S(2)}, u32[]{:S(2)}) collective-permute-start(bf16[256,512]{1,0:T(8,128)(2,1)S(1)} %attend.13), channel_id=1, source_target_pairs={{0,4},{2,6},{4,0},{6,2},{8,12},{10,14},{12,8},{14,10},{1,5},{3,7},... | collective-permute-start | bytes 786440 | tf_op jit(solution)/shard_map/ppermute | solution.py:424
  165.5 9.1 %collective-permute-start.25 = (bf16[256,512]{1,0:T(8,128)(2,1)S(1)}, bf16[256,512]{1,0:T(8,128)(2,1)S(1)}, u32[]{:S(2)}, u32[]{:S(2)}) collective-permute-start(bf16[256,512]{1,0:T(8,128)(2,1)S(1)} %attend.15), channel_id=1, source_target_pairs={{0,4},{2,6},{4,0},{6,2},{8,12},{10,14},{12,8},{14,10},{1,5},{3,7},... | collective-permute-start | bytes 786440 | tf_op jit(solution)/shard_map/ppermute | solution.py:424
  174.7 66.6 %collective-permute-start.26 = (bf16[2,256,512]{2,1,0:T(8,128)(2,1)S(1)}, bf16[2,256,512]{2,1,0:T(8,128)(2,1)S(1)}, u32[]{:S(2)}, u32[]{:S(2)}) collective-permute-start(bf16[2,256,512]{2,1,0:T(8,128)(2,1)S(1)} %pad_maximum_fusion.6.near), channel_id=1, source_target_pairs={{4,8},{6,10},{8,4},{10,6},{5,9},{7,11},{9,5},{11,7},{20,24},{22,26... | collective-permute-start | bytes 1572872 | tf_op jit(solution)/shard_map/ppermute | solution.py:424
  211.6 28.9 %collective-permute-start.21 = (bf16[256,512]{1,0:T(8,128)(2,1)S(1)}, bf16[256,512]{1,0:T(8,128)(2,1)S(1)}, u32[]{:S(2)}, u32[]{:S(2)}) collective-permute-start(bf16[256,512]{1,0:T(8,128)(2,1)S(1)} %attend.14), channel_id=1, source_target_pairs={{0,4},{2,6},{4,0},{6,2},{8,12},{10,14},{12,8},{14,10},{1,5},{3,7},... | collective-permute-start | bytes 786440 | tf_op jit(solution)/shard_map/ppermute | solution.py:424
  215.0 44.1 %slice-start = ((s8[8388608]{0:T(1024)(128)(4,1)}), s8[4194304]{0:T(1024)(128)(4,1)S(1)}, s32[]{:S(2)}) async-start(s8[8388608]{0:T(1024)(128)(4,1)} %bitcast.41), calls=%async_computation | async-start | bytes 8388608
  215.1 44.0 %slice-start.1 = ((s8[8388608]{0:T(1024)(128)(4,1)}), s8[4194304]{0:T(1024)(128)(4,1)S(1)}, s32[]{:S(2)}) async-start(s8[8388608]{0:T(1024)(128)(4,1)} %bitcast.41), calls=%async_computation.1 | async-start | bytes 8388608
  215.1 33.5 %collective-permute-start.17 = (bf16[2,256,512]{2,1,0:T(8,128)(2,1)S(1)}, bf16[2,256,512]{2,1,0:T(8,128)(2,1)S(1)}, u32[]{:S(2)}, u32[]{:S(2)}) collective-permute-start(bf16[2,256,512]{2,1,0:T(8,128)(2,1)S(1)} %pad_maximum_fusion.4.near), channel_id=1, source_target_pairs={{4,8},{6,10},{8,4},{10,6},{5,9},{7,11},{9,5},{11,7},{20,24},{22,26... | collective-permute-start | bytes 1572872 | tf_op jit(solution)/shard_map/ppermute | solution.py:424
  239.4 8.5 %collective-permute-start.11 = (bf16[256,512]{1,0:T(8,128)(2,1)S(1)}, bf16[256,512]{1,0:T(8,128)(2,1)S(1)}, u32[]{:S(2)}, u32[]{:S(2)}) collective-permute-start(bf16[256,512]{1,0:T(8,128)(2,1)S(1)} %attend.11), channel_id=1, source_target_pairs={{0,4},{2,6},{4,0},{6,2},{8,12},{10,14},{12,8},{14,10},{1,5},{3,7},... | collective-permute-start | bytes 786440 | tf_op jit(solution)/shard_map/ppermute | solution.py:424
  240.5 9.4 %collective-permute-start.22 = (bf16[2,256,512]{2,1,0:T(8,128)(2,1)S(1)}, bf16[2,256,512]{2,1,0:T(8,128)(2,1)S(1)}, u32[]{:S(2)}, u32[]{:S(2)}) collective-permute-start(bf16[2,256,512]{2,1,0:T(8,128)(2,1)S(1)} %pad_maximum_fusion.5.near), channel_id=1, source_target_pairs={{4,8},{6,10},{8,4},{10,6},{5,9},{7,11},{9,5},{11,7},{20,24},{22,26... | collective-permute-start | bytes 1572872 | tf_op jit(solution)/shard_map/ppermute | solution.py:424
  241.3 17.8 %collective-permute-start.27 = (bf16[2,256,512]{2,1,0:T(8,128)(2,1)S(1)}, bf16[2,256,512]{2,1,0:T(8,128)(2,1)S(1)}, u32[]{:S(2)}, u32[]{:S(2)}) collective-permute-start(bf16[2,256,512]{2,1,0:T(8,128)(2,1)S(1)} %collective-permute-done.26.come), channel_id=1, source_target_pairs={{4,0},{6,2},{8,12},{10,14},{5,1},{7,3},{9,13},{11,15},{20,16},{22,... | collective-permute-start | bytes 1572872 | tf_op jit(solution)/shard_map/ppermute | solution.py:424
  247.9 16.0 %collective-permute-start.12 = (bf16[2,256,512]{2,1,0:T(8,128)(2,1)S(1)}, bf16[2,256,512]{2,1,0:T(8,128)(2,1)S(1)}, u32[]{:S(2)}, u32[]{:S(2)}) collective-permute-start(bf16[2,256,512]{2,1,0:T(8,128)(2,1)S(1)} %pad_maximum_fusion.3.near), channel_id=1, source_target_pairs={{4,8},{6,10},{8,4},{10,6},{5,9},{7,11},{9,5},{11,7},{20,24},{22,26... | collective-permute-start | bytes 1572872 | tf_op jit(solution)/shard_map/ppermute | solution.py:424
  248.6 21.7 %collective-permute-start.18 = (bf16[2,256,512]{2,1,0:T(8,128)(2,1)S(1)}, bf16[2,256,512]{2,1,0:T(8,128)(2,1)S(1)}, u32[]{:S(2)}, u32[]{:S(2)}) collective-permute-start(bf16[2,256,512]{2,1,0:T(8,128)(2,1)S(1)} %collective-permute-done.17.come), channel_id=1, source_target_pairs={{4,0},{6,2},{8,12},{10,14},{5,1},{7,3},{9,13},{11,15},{20,16},{22,... | collective-permute-start | bytes 1572872 | tf_op jit(solution)/shard_map/ppermute | solution.py:424
  249.9 31.6 %collective-permute-start.23 = (bf16[2,256,512]{2,1,0:T(8,128)(2,1)S(1)}, bf16[2,256,512]{2,1,0:T(8,128)(2,1)S(1)}, u32[]{:S(2)}, u32[]{:S(2)}) collective-permute-start(bf16[2,256,512]{2,1,0:T(8,128)(2,1)S(1)} %collective-permute-done.22.come), channel_id=1, source_target_pairs={{4,0},{6,2},{8,12},{10,14},{5,1},{7,3},{9,13},{11,15},{20,16},{22,... | collective-permute-start | bytes 1572872 | tf_op jit(solution)/shard_map/ppermute | solution.py:424
  263.8 22.8 %collective-permute-start.28 = (bf16[256,1024]{1,0:T(8,128)(2,1)S(1)}, bf16[256,1024]{1,0:T(8,128)(2,1)S(1)}, u32[]{:S(2)}, u32[]{:S(2)}) collective-permute-start(bf16[256,1024]{1,0:T(8,128)(2,1)S(1)} %get-tuple-element.20), channel_id=1, source_target_pairs={{0,2},{2,0},{4,6},{6,4},{8,10},{10,8},{12,14},{14,12},{1,3},{3,1},... | collective-permute-start | bytes 1572872 | tf_op jit(solution)/shard_map/ppermute | solution.py:424
  263.9 27.9 %collective-permute-start.13 = (bf16[2,256,512]{2,1,0:T(8,128)(2,1)S(1)}, bf16[2,256,512]{2,1,0:T(8,128)(2,1)S(1)}, u32[]{:S(2)}, u32[]{:S(2)}) collective-permute-start(bf16[2,256,512]{2,1,0:T(8,128)(2,1)S(1)} %collective-permute-done.12.come), channel_id=1, source_target_pairs={{4,0},{6,2},{8,12},{10,14},{5,1},{7,3},{9,13},{11,15},{20,16},{22,... | collective-permute-start | bytes 1572872 | tf_op jit(solution)/shard_map/ppermute | solution.py:424
  275.0 21.5 %collective-permute-start.19 = (bf16[256,1024]{1,0:T(8,128)(2,1)S(1)}, bf16[256,1024]{1,0:T(8,128)(2,1)S(1)}, u32[]{:S(2)}, u32[]{:S(2)}) collective-permute-start(bf16[256,1024]{1,0:T(8,128)(2,1)S(1)} %get-tuple-element.16), channel_id=1, source_target_pairs={{0,2},{2,0},{4,6},{6,4},{8,10},{10,8},{12,14},{14,12},{1,3},{3,1},... | collective-permute-start | bytes 1572872 | tf_op jit(solution)/shard_map/ppermute | solution.py:424
  286.5 12.1 %collective-permute-start.24 = (bf16[256,1024]{1,0:T(8,128)(2,1)S(1)}, bf16[256,1024]{1,0:T(8,128)(2,1)S(1)}, u32[]{:S(2)}, u32[]{:S(2)}) collective-permute-start(bf16[256,1024]{1,0:T(8,128)(2,1)S(1)} %get-tuple-element.18), channel_id=1, source_target_pairs={{0,2},{2,0},{4,6},{6,4},{8,10},{10,8},{12,14},{14,12},{1,3},{3,1},... | collective-permute-start | bytes 1572872 | tf_op jit(solution)/shard_map/ppermute | solution.py:424
  286.7 15.1 %collective-permute-start.29 = (bf16[256,1024]{1,0:T(8,128)(2,1)S(1)}, bf16[256,1024]{1,0:T(8,128)(2,1)S(1)}, u32[]{:S(2)}, u32[]{:S(2)}) collective-permute-start(bf16[256,1024]{1,0:T(8,128)(2,1)S(1)} %add_convert_fusion.1), channel_id=1, source_target_pairs={{0,1},{1,0},{2,3},{3,2},{4,5},{5,4},{6,7},{7,6},{8,9},{9,8},{10,11... | collective-permute-start | bytes 1572872 | tf_op jit(solution)/shard_map/ppermute | solution.py:424
  296.4 5.7 %collective-permute-start.15 = (bf16[256,1024]{1,0:T(8,128)(2,1)S(1)}, bf16[256,1024]{1,0:T(8,128)(2,1)S(1)}, u32[]{:S(2)}, u32[]{:S(2)}) collective-permute-start(bf16[256,1024]{1,0:T(8,128)(2,1)S(1)} %get-tuple-element.14), channel_id=1, source_target_pairs={{0,2},{2,0},{4,6},{6,4},{8,10},{10,8},{12,14},{14,12},{1,3},{3,1},... | collective-permute-start | bytes 1572872 | tf_op jit(solution)/shard_map/ppermute | solution.py:424
  296.6 16.2 %collective-permute-start.20 = (bf16[256,1024]{1,0:T(8,128)(2,1)S(1)}, bf16[256,1024]{1,0:T(8,128)(2,1)S(1)}, u32[]{:S(2)}, u32[]{:S(2)}) collective-permute-start(bf16[256,1024]{1,0:T(8,128)(2,1)S(1)} %add_convert_fusion.3), channel_id=1, source_target_pairs={{0,1},{1,0},{2,3},{3,2},{4,5},{5,4},{6,7},{7,6},{8,9},{9,8},{10,11... | collective-permute-start | bytes 1572872 | tf_op jit(solution)/shard_map/ppermute | solution.py:424
  (4 other events, 23.7 us)

commit v3 on v2

--- a/solution.py
+++ b/solution.py
@@ -182,10 +182,10 @@
     def groups_of(of):
         return (tab[of, block, share] + (key_group - 1)) // key_group
 
-    def exponents(keys, hidden, i):
+    def exponents(keys, hidden, i, some=slice(None)):
         pair = jnp.concatenate(keys[i : i + 2], axis=0)
         scores = lax.dot_general(
-            q_rows[...], pair, (((1,), (1,)), ((), ())), preferred_element_type=jnp.float32
+            q_rows[some], pair, (((1,), (1,)), ((), ())), preferred_element_type=jnp.float32
         )
         return scores * exp2_scale + jnp.concatenate(hidden[i : i + 2], axis=1)
 
@@ -215,17 +215,19 @@
 
     def fold(of, place, j, carry):
         keys, hidden, values = group_of(of, place, j)
-        probs = []
         highest = high[...]
-        for i in range(0, key_group, 2):
-            x = exponents(keys, hidden, i)
-            for side in (x[:, :BLOCK_TOKENS], x[:, BLOCK_TOKENS:]):
-                highest = jnp.maximum(highest, jnp.max(side.reshape(-1, 8, BLOCK_TOKENS), axis=0))
-            probs.append(jnp.exp2(x).astype(jnp.bfloat16))
+        for at in range(0, rows, rows // 2):
+            some = slice(at, at + rows // 2)
+            probs = []
+            for i in range(0, key_group, 2):
+                x = exponents(keys, hidden, i, some)
+                for side in (x[:, :BLOCK_TOKENS], x[:, BLOCK_TOKENS:]):
+                    side = jnp.max(side.reshape(-1, 8, BLOCK_TOKENS), axis=0)
+                    highest = jnp.maximum(highest, side)
+                probs.append(jnp.exp2(x).astype(jnp.bfloat16))
+            probs = jnp.concatenate(probs, axis=1)
+            sums[some] += jnp.dot(probs, values, preferred_element_type=jnp.float32)
         high[...] = highest
-        sums[...] += jnp.dot(
-            jnp.concatenate(probs, axis=1), values, preferred_element_type=jnp.float32
-        )
         return carry
 
     for place, of in enumerate(folded):
@@ -326,73 +328,99 @@
     return z ^ i if i < 2 else far ^ (i % 2)
 
 
-def project_kernel(pos, near, come, out, w_own, w_swap, *refs):
-    own_ref, other_ref, parts, sems = refs
+def project_kernel(sides, held, far, pos, near, *refs):
+    come, out = refs[:2] if far else (near, near)
+    refs = refs[2 * far :]
+    w_refs, refs = refs[:sides], refs[sides:]
+    bases, refs = refs[: sides * held], refs[sides * held :]
+    o_refs, (parts, sems) = refs[:sides], refs[sides:]
     ends = (pos[0] == 0) | (pos[0] == 3)
 
     def bring(i, source):
         return pltpu.make_async_copy(source, parts.at[pl.ds(2 * i, 2)], sems.at[i])
 
-    bring(0, near).start()
-
-    @pl.when(ends)
-    def _():
-        bring(1, out).start()
-
-    @pl.when(jnp.logical_not(ends))
-    def _():
-        bring(1, come).start()
-
-    for i in range(2):
+    if not held:
+        bring(0, near).start()
+    if far:
+
+        @pl.when(ends)
+        def _():
+            bring(1, out).start()
+
+        @pl.when(jnp.logical_not(ends))
+        def _():
+            bring(1, come).start()
+
+    used = range(2 * held, 4 if far else 2)
+    for i in range(used.start // 2, used.stop // 2):
         bring(i, near).wait()
     depth = near.shape[2]
     tile = 256
     own_rows = pl.ds(pl.multiple_of(pos[1] * depth, depth), depth)
     places = [piece_chip(i, pos[0]) for i in range(4)]
 
-    for at in range(0, own_ref.shape[1], tile):
+    for at in range(0, o_refs[0].shape[1], tile):
         columns = slice(at, at + tile)
-        for w_ref, w_rows, o_ref in (
-            (w_swap, slice(0, depth), other_ref),
-            (w_own, own_rows, own_ref),
-        ):
+        for side, (w_ref, o_ref) in enumerate(zip(w_refs, o_refs)):
+            w_rows = own_rows if w_ref.shape[1] > depth else slice(0, depth)
             terms = [
                 jnp.dot(
                     parts[i],
                     w_ref[places[i], w_rows, columns],
                     preferred_element_type=jnp.float32,
                 )
-                for i in range(4)
+                for i in used
             ]
+            if held:
+                terms.append(bases[side][:, columns])
             o_ref[:, columns] = functools.reduce(jnp.add, terms).astype(o_ref.dtype)
 
 
-def project(pos, near, come, out, w_own, w_swap):
+def project(pos, near, far, weights, types, bases=()):
     rows, depth = near.shape[1:]
-    chips, _, columns = w_own.shape
+    chips, _, columns = weights[0].shape
+    sides = len(weights)
     vmem = pl.BlockSpec(memory_space=pltpu.VMEM)
     return pl.pallas_call(
-        project_kernel,
-        out_shape=(
-            jax.ShapeDtypeStruct((rows, columns), jnp.float32),
-            jax.ShapeDtypeStruct((rows, columns), jnp.bfloat16),
-        ),
+        functools.partial(project_kernel, sides, bool(bases), bool(far)),
+        out_shape=tuple(jax.ShapeDtypeStruct((rows, columns), kind) for kind in types),
         in_specs=[pl.BlockSpec(memory_space=pltpu.SMEM)]
-        + [pl.BlockSpec(memory_space=pl.ANY)] * 3
-        + [vmem] * 2,
-        out_specs=(vmem, vmem),
+        + [pl.BlockSpec(memory_space=pl.ANY)] * (1 + len(far))
+        + [vmem] * (sides + len(bases)),
+        out_specs=(vmem,) * sides,
         scratch_shapes=[
             pltpu.VMEM((chips, rows, depth), jnp.bfloat16),
             pltpu.SemaphoreType.DMA((2,)),
         ],
         compiler_params=pltpu.CompilerParams(vmem_limit_bytes=project_vmem),
         cost_estimate=pl.CostEstimate(
-            flops=2 * rows * chips * depth * 2 * columns,
-            bytes_accessed=2 * (8 * depth * columns + 6 * rows * depth + 3 * rows * columns),
+            flops=2 * rows * chips * depth * sides * columns,
+            bytes_accessed=2 * sides * (chips * depth + 3 * rows) * columns,
             transcendentals=0,
         ),
         name="project",
-    )(pos, near, come, out, w_own, w_swap)
+    )(pos, near, *far, *weights, *bases)
+
+
+def finish_kernel(own, come, theirs, *refs):
+    total = own[...] + come[...].astype(jnp.float32) + theirs[...].astype(jnp.float32)
+    refs[-1][...] = total.astype(jnp.bfloat16)
+
+
+def finish(at, size, own, come, theirs, result=None):
+    rows, columns = own.shape
+    block = pl.BlockSpec((rows, columns), lambda i: (0, 0))
+    held = () if result is None else (result,)
+    return pl.pallas_call(
+        finish_kernel,
+        out_shape=jax.ShapeDtypeStruct((size, columns), jnp.bfloat16),
+        grid=(1,),
+        in_specs=[block] * 3 + [pl.BlockSpec(memory_space=pl.ANY)] * len(held),
+        out_specs=pl.BlockSpec((rows, columns), lambda i: (at, 0)),
+        input_output_aliases={3: 0} if held else {},
+        compiler_params=pltpu.CompilerParams(vmem_limit_bytes=attend_vmem),
+        name="finish",
+    )(own, come, theirs, *held)
 
 
 def apart(k):
@@ -437,24 +465,22 @@
     def swap(array):
         return permute(array, apart(1))
 
-    meta = jnp.concatenate([attending.reshape(-1), block_fill]).astype(jnp.bfloat16)
-    meta = jnp.pad(meta[None, :], ((0, meta_rows - 1), (0, depth - meta.shape[0])))
-    meta = jnp.concatenate([meta, meta], axis=1)
-
     def q_for(chip):
-        own = lax.dynamic_slice(queries, (0, chip * wide), (q_len, wide))
-        return jnp.concatenate([own, meta], axis=0)
+        return lax.dynamic_slice(queries, (0, chip * wide), (q_len, wide))
 
     def kv_for(chip):
         return lax.dynamic_slice(keyvals, (0, chip * pair), (keyvals.shape[0], pair))
 
     def columns_of(arrays, which):
-        size = (q_len + meta_rows, depth)
+        size = (q_len, depth)
         return jnp.stack([lax.dynamic_slice(a, (0, which * depth), size) for a in arrays])
 
     q_come = [q_for(z)]
     for k in range(1, chips):
         q_come.append(permute(q_for(z ^ k), apart(2 * k)))
+    note = jnp.concatenate([attending.reshape(-1), block_fill]).astype(jnp.bfloat16)
+    note = jnp.pad(note[None, :], ((0, meta_rows - 1), (0, HEAD_WIDTH - note.shape[0])))
+    notes = [note] + [permute(note, apart(2 * k)) for k in range(1, chips)]
     kv = []
     for k in range(chips):
         own = kv_for(z ^ k)
@@ -465,7 +491,8 @@
     q_own = columns_of(q_come, core)
     q_swap = swap(columns_of(q_come, 1 - core))
     q_two = (q_own, q_swap)
-    notes = jnp.stack([q_own[:, q_len, :64], q_swap[:, q_len, :64]], axis=1)
+    notes = jnp.stack(notes)
+    notes = jnp.stack([notes[:, 0, :64], swap(notes)[:, 0, :64]], axis=1)
     tab = key_lists(notes.astype(jnp.int32), 2 * chips)
     pos = jnp.stack([z, core, row]).astype(jnp.int32)
     q_two = (q_own, q_swap)
@@ -481,28 +508,34 @@
     outward = [(2, 0), (3, 1), (4, 6), (5, 7)]
     every_key = [a for of in kv for a in of]
 
-    def chunk(part, count):
+    def chunk(i, part, count):
         state = [(True, a) for a in whole] + [(False, halves[part[0]])]
         mine = attend((3,), tab, pos, q_two, every_key, count, part, state)
         near = jnp.stack([mine, permute(mine, apart(2))])
         come = permute(near, across)
         out = permute(come, outward)
-        own, other = project(pos, near, come, out, w_own, w_swap)
+        far = (come, out)
+        if i + 1 < len(chunks):
+            both = (w_swap, w_own), (jnp.bfloat16, jnp.float32)
+            other, own = project(pos, near, far, *both)
+        else:
+            both = (w_swap, w_own), (jnp.float32, jnp.float32)
+            bases = project(pos, near, (), *both)
+            (other,) = project(pos, near, far, (w_swap,), (jnp.bfloat16,), bases[:1])
+            (own,) = project(pos, near, far, (w_own,), (jnp.float32,), bases[1:])
         return own, swap(other)
 
     theirs = []
-    ours = []
-    for mine, offset, count in chunks:
-        own, come = chunk((mine, offset), count)
-        total = own + come.astype(jnp.float32)
+    result = None
+    for i, (mine, offset, count) in enumerate(chunks):
+        own, come = chunk(i, (mine, offset), count)
         if mine:
-            come = jnp.concatenate(theirs, axis=0) if len(theirs) > 1 else theirs[0]
-            come = come[offset * BLOCK_TOKENS : (offset + count) * BLOCK_TOKENS]
-            ours.append((total + come.astype(jnp.float32)).astype(jnp.bfloat16))
+            other = theirs[offset // count]
+            result = finish(offset // count, q_len * 4, own, come, other, result)
         else:
-            sent = total.astype(jnp.bfloat16)
+            sent = (own + come.astype(jnp.float32)).astype(jnp.bfloat16)
             theirs.append(permute(sent, [(0, 1), (1, 0)], "rows"))
-    return jnp.concatenate(ours, axis=0)
+    return result
 
 
 def solution(mesh):

time: 317 us -> 275 us (0.87)
  Pallas kernels: 169 us -> 118 us
  waiting for transfers between devices: 93.4 us -> 99.8 us
    pallas_call x8, Pallas kernels: 150 us -> 102 us  [attend(): pl.pallas_call(functools.partial(attend_kernel, folded, part, last, heads...]
    ppermute x30 -> x34, waiting for transfers between devices: 93.4 us -> 99.8 us  [permute(): return lax.ppermute(array, axis, perm)]
    pallas_call x4 -> x8, Pallas kernels: 18.9 us -> 15.7 us  [the longest x6 13.8 us: project(): pl.pallas_call(functools.partial(project_kernel, sides, bool(bases), bool...]
    ppermute x30 -> x34, starting transfers between devices: 31.9 us -> 34 us  [permute(): return lax.ppermute(array, axis, perm)]
  transfers between devices with their start and end apart: 30 -> 34, of which waited for: 10 -> 11; matrix products, arithmetic and copies ran while one was open for 5% -> 7% of each run, Pallas kernels for 54% -> 43%
where the time goes in v3:
time: 275 us; the launch traced here: 274 us
  Pallas kernels  118 us (43%)
  waiting for transfers between devices  99.8 us (36%)
  starting transfers between devices  34 us (12%)
  local copies, waits for them, and re-layouts  13.9 us (5%)
  other arithmetic  8.29 us (3%)
    pallas_call x8, Pallas kernels, attend(): pl.pallas_call(functools.partial(attend_kernel, folded, part, last, heads...  102 us
    ppermute x34, waiting for transfers between devices, permute(): return lax.ppermute(array, axis, perm)  99.8 us
    ppermute x34, starting transfers between devices, permute(): return lax.ppermute(array, axis, perm)  34 us
    pallas_call x6, Pallas kernels, project(): pl.pallas_call(functools.partial(project_kernel, sides, bool(bases), bool...  13.8 us
  transfers between devices with their start and end apart: 34, of which 11 were waited for; matrix products, arithmetic and copies ran while one was open for 7% of the time, Pallas kernels for 43%

profile of v3, /device:TPU:0, one launch (start us, length us, event | category | flops | bytes accessed | tf_op | source)
XLA Modules:
  0.0 274.0 jit_solution(8725638026397028101)
XLA Ops:
  1.6 3.1 %collective-permute-start = (bf16[16,128]{1,0:T(8,128)(2,1)S(1)}, bf16[16,128]{1,0:T(8,128)(2,1)S(1)}, u32[]{:S(2)}, u32[]{:S(2)}) collective-permute-start(bf16[16,128]{1,0:T(8,128)(2,1)S(1)} %fusion.7), channel_id=1, source_target_pairs={{0,4},{2,6},{4,0},{6,2},{8,12},{10,14},{12,8},{14,10},{1,5},{3,7},... | collective-permute-start | bytes 12296 | tf_op jit(solution)/shard_map/ppermute | solution.py:452
  4.7 2.6 collective-permute-start.1
  7.3 1.9 constant_dynamic-slice_fusion.7
  10.0 3.5 %collective-permute-start.5 = (bf16[128,1024]{1,0:T(8,128)(2,1)S(1)}, bf16[128,1024]{1,0:T(8,128)(2,1)}, u32[]{:S(2)}, u32[]{:S(2)}) collective-permute-start(bf16[128,1024]{1,0:T(8,128)(2,1)S(1)} %get-tuple-element.28), channel_id=1, source_target_pairs={{0,8},{2,10},{4,12},{6,14},{8,0},{10,2},{12,4},{14,6},{1,9},{3,11}... | collective-permute-start | bytes 786440 | tf_op jit(solution)/shard_map/ppermute | solution.py:452
  13.6 4.8 %constant_dynamic-slice_fusion = bf16[4,512,1024]{2,1,0:T(8,128)(2,1)} fusion(bf16[4,1024,1024]{2,1,0:T(8,128)(2,1)} %bitcast.45, s32[]{:T(128)S(6)} %select_n.73), kind=kLoop, calls=%fused_computation.34 | loop fusion | bytes 8388612 | tf_op jit(solution)/shard_map/dynamic_slice | solution.py:503
  20.8 3.8 %collective-permute-start.13 = (bf16[1024,256]{1,0:T(8,128)(2,1)}, bf16[1024,256]{1,0:T(8,128)(2,1)S(1)}, u32[]{:S(2)}, u32[]{:S(2)}) collective-permute-start(bf16[1024,256]{1,0:T(8,128)(2,1)} %get-tuple-element.21), channel_id=1, source_target_pairs={{0,12},{2,14},{4,8},{6,10},{8,4},{10,6},{12,0},{14,2},{1,13},{3,15... | collective-permute-start | bytes 1572872 | tf_op jit(solution)/shard_map/ppermute | solution.py:452
  28.5 11.1 %collective-permute-done.5 = bf16[128,1024]{1,0:T(8,128)(2,1)} collective-permute-done((bf16[128,1024]{1,0:T(8,128)(2,1)S(1)}, bf16[128,1024]{1,0:T(8,128)(2,1)}, u32[]{:S(2)}, u32[]{:S(2)}) %collective-permute-start.5) | collective-permute-done | bytes 262176 | tf_op jit(solution)/shard_map/ppermute | solution.py:452
  40.7 1.6 dynamic-slice_bitcast_fusion
  45.1 1.3 select_reduce_fusion.1
  49.2 3.2 %collective-permute-done.9 = bf16[1024,256]{1,0:T(8,128)(2,1)S(1)} collective-permute-done((bf16[1024,256]{1,0:T(8,128)(2,1)}, bf16[1024,256]{1,0:T(8,128)(2,1)S(1)}, u32[]{:S(2)}, u32[]{:S(2)}) %collective-permute-start.9) | collective-permute-done | bytes 524320 | tf_op jit(solution)/shard_map/ppermute | solution.py:452
  52.4 28.1 %collective-permute-done.11 = bf16[1024,256]{1,0:T(8,128)(2,1)S(1)} collective-permute-done((bf16[1024,256]{1,0:T(8,128)(2,1)}, bf16[1024,256]{1,0:T(8,128)(2,1)S(1)}, u32[]{:S(2)}, u32[]{:S(2)}) %collective-permute-start.11) | collective-permute-done | bytes 524320 | tf_op jit(solution)/shard_map/ppermute | solution.py:452
  81.1 11.9 %attend.8.refs_10_ = f32[8,520,256]{2,1,0:T(8,128)S(1)} custom-call(s32[4,8,17]{2,1,0:T(8,128)S(1)} %pad_add_fusion.tab, s32[3]{0:T(128)S(1)} %pad_add_fusion.1.pos, bf16[4,128,512]{2,1,0:T(8,128)(2,1)S(1)} %pad_maximum_fusion.refs_0_, bf16[4,128,512]{2,1,0:T(8,128)(2,1)S(1)} %collective-permute-done.7.refs_1_, bf16[8,128,256]{2,1,0:T(8,128)(2,1)S(1)} %bitcast.53, ...), custom_call_target="tpu_custom_call" | custom-call | flops 8589934592 | bytes 524288 | tf_op jit(solution)/shard_map/attend/pallas_call | solution.py:306
  93.0 11.7 %attend.9.refs_11_ = f32[8,520,256]{2,1,0:T(8,128)S(1)} custom-call(s32[4,8,17]{2,1,0:T(8,128)S(1)} %pad_add_fusion.tab, s32[3]{0:T(128)S(1)} %pad_add_fusion.1.pos, bf16[4,128,512]{2,1,0:T(8,128)(2,1)S(1)} %pad_maximum_fusion.refs_0_, bf16[4,128,512]{2,1,0:T(8,128)(2,1)S(1)} %collective-permute-done.7.refs_1_, bf16[8,128,256]{2,1,0:T(8,128)(2,1)S(1)} %bitcast.62, ...), custom_call_target="tpu_custom_call" | custom-call | flops 8589934592 | bytes 524288 | tf_op jit(solution)/shard_map/attend/pallas_call | solution.py:306
  104.7 5.2 %attend.12.refs_12_ = f32[4,520,256]{2,1,0:T(8,128)S(1)} custom-call(s32[4,8,17]{2,1,0:T(8,128)S(1)} %pad_add_fusion.tab, s32[3]{0:T(128)S(1)} %pad_add_fusion.1.pos, bf16[4,128,512]{2,1,0:T(8,128)(2,1)S(1)} %pad_maximum_fusion.refs_0_, bf16[4,128,512]{2,1,0:T(8,128)(2,1)S(1)} %collective-permute-done.7.refs_1_, bf16[8,128,256]{2,1,0:T(8,128)(2,1)S(1)} %bitcast.67, ...), custom_call_target="tpu_custom_call" | custom-call | flops 4294967296 | bytes 262144 | tf_op jit(solution)/shard_map/attend/pallas_call | solution.py:306
  109.9 11.9 %attend.15 = bf16[256,512]{1,0:T(8,128)(2,1)S(1)} custom-call(s32[4,8,17]{2,1,0:T(8,128)S(1)} %pad_add_fusion.tab, s32[3]{0:T(128)S(1)} %pad_add_fusion.1.pos, bf16[4,128,512]{2,1,0:T(8,128)(2,1)S(1)} %pad_maximum_fusion.refs_0_, bf16[4,128,512]{2,1,0:T(8,128)(2,1)S(1)} %collective-permute-done.7.refs_1_, bf16[8,128,256]{2,1,0:T(8,128)(2,1)S(1)} %bitcast.54, ...), custom_call_target="tpu_custom_call" | custom-call | flops 2147483648 | bytes 131072 | tf_op jit(solution)/shard_map/attend/pallas_call | solution.py:306
  122.2 6.9 %attend.10.refs_12_ = f32[4,520,256]{2,1,0:T(8,128)S(1)} custom-call(s32[4,8,17]{2,1,0:T(8,128)S(1)} %pad_add_fusion.tab, s32[3]{0:T(128)S(1)} %pad_add_fusion.1.pos, bf16[4,128,512]{2,1,0:T(8,128)(2,1)S(1)} %pad_maximum_fusion.refs_0_, bf16[4,128,512]{2,1,0:T(8,128)(2,1)S(1)} %collective-permute-done.7.refs_1_, bf16[8,128,256]{2,1,0:T(8,128)(2,1)S(1)} %bitcast.69, ...), custom_call_target="tpu_custom_call" | custom-call | flops 4294967296 | bytes 262144 | tf_op jit(solution)/shard_map/attend/pallas_call | solution.py:306
  129.1 11.9 %attend.14 = bf16[256,512]{1,0:T(8,128)(2,1)S(1)} custom-call(s32[4,8,17]{2,1,0:T(8,128)S(1)} %pad_add_fusion.tab, s32[3]{0:T(128)S(1)} %pad_add_fusion.1.pos, bf16[4,128,512]{2,1,0:T(8,128)(2,1)S(1)} %pad_maximum_fusion.refs_0_, bf16[4,128,512]{2,1,0:T(8,128)(2,1)S(1)} %collective-permute-done.7.refs_1_, bf16[8,128,256]{2,1,0:T(8,128)(2,1)S(1)} %bitcast.55, ...), custom_call_target="tpu_custom_call" | custom-call | flops 2147483648 | bytes 131072 | tf_op jit(solution)/shard_map/attend/pallas_call | solution.py:306
  142.3 17.1 %attend.13 = bf16[256,512]{1,0:T(8,128)(2,1)S(1)} custom-call(s32[4,8,17]{2,1,0:T(8,128)S(1)} %pad_add_fusion.tab, s32[3]{0:T(128)S(1)} %pad_add_fusion.1.pos, bf16[4,128,512]{2,1,0:T(8,128)(2,1)S(1)} %pad_maximum_fusion.refs_0_, bf16[4,128,512]{2,1,0:T(8,128)(2,1)S(1)} %collective-permute-done.7.refs_1_, bf16[8,128,256]{2,1,0:T(8,128)(2,1)S(1)} %bitcast.56, ...), custom_call_target="tpu_custom_call" | custom-call | flops 2147483648 | bytes 131072 | tf_op jit(solution)/shard_map/attend/pallas_call | solution.py:306
  160.7 25.1 %attend.11 = bf16[256,512]{1,0:T(8,128)(2,1)S(1)} custom-call(s32[4,8,17]{2,1,0:T(8,128)S(1)} %pad_add_fusion.tab, s32[3]{0:T(128)S(1)} %pad_add_fusion.1.pos, bf16[4,128,512]{2,1,0:T(8,128)(2,1)S(1)} %pad_maximum_fusion.refs_0_, bf16[4,128,512]{2,1,0:T(8,128)(2,1)S(1)} %collective-permute-done.7.refs_1_, bf16[8,128,256]{2,1,0:T(8,128)(2,1)S(1)} %bitcast.57, ...), custom_call_target="tpu_custom_call" | custom-call | flops 2147483648 | bytes 131072 | tf_op jit(solution)/shard_map/attend/pallas_call | solution.py:306
  185.8 5.8 %collective-permute-start.15 = (bf16[256,512]{1,0:T(8,128)(2,1)S(1)}, bf16[256,512]{1,0:T(8,128)(2,1)S(1)}, u32[]{:S(2)}, u32[]{:S(2)}) collective-permute-start(bf16[256,512]{1,0:T(8,128)(2,1)S(1)} %attend.11), channel_id=1, source_target_pairs={{0,4},{2,6},{4,0},{6,2},{8,12},{10,14},{12,8},{14,10},{1,5},{3,7},... | collective-permute-start | bytes 786440 | tf_op jit(solution)/shard_map/ppermute | solution.py:452
  193.2 3.8 %collective-permute-done.15 = bf16[256,512]{1,0:T(8,128)(2,1)S(1)} collective-permute-done((bf16[256,512]{1,0:T(8,128)(2,1)S(1)}, bf16[256,512]{1,0:T(8,128)(2,1)S(1)}, u32[]{:S(2)}, u32[]{:S(2)}) %collective-permute-start.15) | collective-permute-done | bytes 262176 | tf_op jit(solution)/shard_map/ppermute | solution.py:452
  203.0 11.8 %collective-permute-done.31.refs_1_ = bf16[2,256,512]{2,1,0:T(8,128)(2,1)S(1)} collective-permute-done((bf16[2,256,512]{2,1,0:T(8,128)(2,1)S(1)}, bf16[2,256,512]{2,1,0:T(8,128)(2,1)S(1)}, u32[]{:S(2)}, u32[]{:S(2)}) %collective-permute-start.31) | collective-permute-done | bytes 524320 | tf_op jit(solution)/shard_map/ppermute | solution.py:452
  214.8 3.0 %project.11 = (bf16[256,1024]{1,0:T(8,128)(2,1)S(1)}, f32[256,1024]{1,0:T(8,128)S(1)}) custom-call(s32[3]{0:T(128)S(1)} %pad_add_fusion.1.pos, bf16[2,256,512]{2,1,0:T(8,128)(2,1)S(1)} %pad_maximum_fusion.5.near, bf16[2,256,512]{2,1,0:T(8,128)(2,1)S(1)} %collective-permute-done.30.refs_0_, bf16[2,256,512]{2,1,0:T(8,128)(2,1)S(1)} %collective-permute-done.31.refs_1_, ...), custom_call_target="tpu_custom_call" | custom-call | flops 2147483648 | bytes 11534336 | tf_op jit(solution)/shard_map/project/pallas_call | solution.py:384
  217.9 8.1 %collective-permute-done.22.refs_1_ = bf16[2,256,512]{2,1,0:T(8,128)(2,1)S(1)} collective-permute-done((bf16[2,256,512]{2,1,0:T(8,128)(2,1)S(1)}, bf16[2,256,512]{2,1,0:T(8,128)(2,1)S(1)}, u32[]{:S(2)}, u32[]{:S(2)}) %collective-permute-start.22) | collective-permute-done | bytes 524320 | tf_op jit(solution)/shard_map/ppermute | solution.py:452
  226.0 3.3 %project.9 = (bf16[256,1024]{1,0:T(8,128)(2,1)S(1)}, f32[256,1024]{1,0:T(8,128)S(1)}) custom-call(s32[3]{0:T(128)S(1)} %pad_add_fusion.1.pos, bf16[2,256,512]{2,1,0:T(8,128)(2,1)S(1)} %pad_maximum_fusion.3.near, bf16[2,256,512]{2,1,0:T(8,128)(2,1)S(1)} %collective-permute-done.21.refs_0_, bf16[2,256,512]{2,1,0:T(8,128)(2,1)S(1)} %collective-permute-done.22.refs_1_, ...), custom_call_target="tpu_custom_call" | custom-call | flops 2147483648 | bytes 11534336 | tf_op jit(solution)/shard_map/project/pallas_call | solution.py:384
  229.4 7.9 %collective-permute-done.27.refs_1_ = bf16[2,256,512]{2,1,0:T(8,128)(2,1)S(1)} collective-permute-done((bf16[2,256,512]{2,1,0:T(8,128)(2,1)S(1)}, bf16[2,256,512]{2,1,0:T(8,128)(2,1)S(1)}, u32[]{:S(2)}, u32[]{:S(2)}) %collective-permute-start.27) | collective-permute-done | bytes 524320 | tf_op jit(solution)/shard_map/ppermute | solution.py:452
  237.3 3.0 %project.10 = (bf16[256,1024]{1,0:T(8,128)(2,1)S(1)}, f32[256,1024]{1,0:T(8,128)S(1)}) custom-call(s32[3]{0:T(128)S(1)} %pad_add_fusion.1.pos, bf16[2,256,512]{2,1,0:T(8,128)(2,1)S(1)} %pad_maximum_fusion.4.near, bf16[2,256,512]{2,1,0:T(8,128)(2,1)S(1)} %collective-permute-done.26.refs_0_, bf16[2,256,512]{2,1,0:T(8,128)(2,1)S(1)} %collective-permute-done.27.refs_1_, ...), custom_call_target="tpu_custom_call" | custom-call | flops 2147483648 | bytes 11534336 | tf_op jit(solution)/shard_map/project/pallas_call | solution.py:384
  240.4 1.9 project.6
  242.2 3.6 %collective-permute-done.17.refs_1_ = bf16[2,256,512]{2,1,0:T(8,128)(2,1)S(1)} collective-permute-done((bf16[2,256,512]{2,1,0:T(8,128)(2,1)S(1)}, bf16[2,256,512]{2,1,0:T(8,128)(2,1)S(1)}, u32[]{:S(2)}, u32[]{:S(2)}) %collective-permute-start.17) | collective-permute-done | bytes 524320 | tf_op jit(solution)/shard_map/ppermute | solution.py:452
  247.4 1.3 collective-permute-start.33
  251.1 11.2 %collective-permute-done.33.theirs = bf16[256,1024]{1,0:T(8,128)(2,1)S(1)} collective-permute-done((bf16[256,1024]{1,0:T(8,128)(2,1)S(1)}, bf16[256,1024]{1,0:T(8,128)(2,1)S(1)}, u32[]{:S(2)}, u32[]{:S(2)}) %collective-permute-start.33) | collective-permute-done | bytes 524320 | tf_op jit(solution)/shard_map/ppermute | solution.py:452
  263.2 9.8 %collective-permute-done.24.theirs = bf16[256,1024]{1,0:T(8,128)(2,1)S(1)} collective-permute-done((bf16[256,1024]{1,0:T(8,128)(2,1)S(1)}, bf16[256,1024]{1,0:T(8,128)(2,1)S(1)}, u32[]{:S(2)}, u32[]{:S(2)}) %collective-permute-start.24) | collective-permute-done | bytes 524320 | tf_op jit(solution)/shard_map/ppermute | solution.py:452
  (99 shorter events, 32.1 us)
Async XLA Ops:
  1.6 19.1 %collective-permute-start = (bf16[16,128]{1,0:T(8,128)(2,1)S(1)}, bf16[16,128]{1,0:T(8,128)(2,1)S(1)}, u32[]{:S(2)}, u32[]{:S(2)}) collective-permute-start(bf16[16,128]{1,0:T(8,128)(2,1)S(1)} %fusion.7), channel_id=1, source_target_pairs={{0,4},{2,6},{4,0},{6,2},{8,12},{10,14},{12,8},{14,10},{1,5},{3,7},... | collective-permute-start | bytes 12296 | tf_op jit(solution)/shard_map/ppermute | solution.py:452
  4.7 16.1 %collective-permute-start.1 = (bf16[16,128]{1,0:T(8,128)(2,1)S(1)}, bf16[16,128]{1,0:T(8,128)(2,1)S(1)}, u32[]{:S(2)}, u32[]{:S(2)}) collective-permute-start(bf16[16,128]{1,0:T(8,128)(2,1)S(1)} %fusion.7), channel_id=1, source_target_pairs={{0,8},{2,10},{4,12},{6,14},{8,0},{10,2},{12,4},{14,6},{1,9},{3,11}... | collective-permute-start | bytes 12296 | tf_op jit(solution)/shard_map/ppermute | solution.py:452
  7.3 17.3 %collective-permute-start.2 = (bf16[16,128]{1,0:T(8,128)(2,1)S(1)}, bf16[16,128]{1,0:T(8,128)(2,1)S(1)}, u32[]{:S(2)}, u32[]{:S(2)}) collective-permute-start(bf16[16,128]{1,0:T(8,128)(2,1)S(1)} %fusion.7), channel_id=1, source_target_pairs={{0,12},{2,14},{4,8},{6,10},{8,4},{10,6},{12,0},{14,2},{1,13},{3,15... | collective-permute-start | bytes 12296 | tf_op jit(solution)/shard_map/ppermute | solution.py:452
  9.1 17.7 %collective-permute-start.4 = (bf16[128,1024]{1,0:T(8,128)(2,1)S(1)}, bf16[128,1024]{1,0:T(8,128)(2,1)}, u32[]{:S(2)}, u32[]{:S(2)}) collective-permute-start(bf16[128,1024]{1,0:T(8,128)(2,1)S(1)} %get-tuple-element.27), channel_id=1, source_target_pairs={{0,4},{2,6},{4,0},{6,2},{8,12},{10,14},{12,8},{14,10},{1,5},{3,7},... | collective-permute-start | bytes 786440 | tf_op jit(solution)/shard_map/ppermute | solution.py:452
  10.0 29.6 %collective-permute-start.5 = (bf16[128,1024]{1,0:T(8,128)(2,1)S(1)}, bf16[128,1024]{1,0:T(8,128)(2,1)}, u32[]{:S(2)}, u32[]{:S(2)}) collective-permute-start(bf16[128,1024]{1,0:T(8,128)(2,1)S(1)} %get-tuple-element.28), channel_id=1, source_target_pairs={{0,8},{2,10},{4,12},{6,14},{8,0},{10,2},{12,4},{14,6},{1,9},{3,11}... | collective-permute-start | bytes 786440 | tf_op jit(solution)/shard_map/ppermute | solution.py:452
  20.8 19.9 %collective-permute-start.6 = (bf16[128,1024]{1,0:T(8,128)(2,1)}, bf16[128,1024]{1,0:T(8,128)(2,1)}, u32[]{:S(2)}, u32[]{:S(2)}) collective-permute-start(bf16[128,1024]{1,0:T(8,128)(2,1)} %get-tuple-element.29), channel_id=1, source_target_pairs={{0,12},{2,14},{4,8},{6,10},{8,4},{10,6},{12,0},{14,2},{1,13},{3,15... | collective-permute-start | bytes 786440 | tf_op jit(solution)/shard_map/ppermute | solution.py:452
  20.8 28.3 %collective-permute-start.13 = (bf16[1024,256]{1,0:T(8,128)(2,1)}, bf16[1024,256]{1,0:T(8,128)(2,1)S(1)}, u32[]{:S(2)}, u32[]{:S(2)}) collective-permute-start(bf16[1024,256]{1,0:T(8,128)(2,1)} %get-tuple-element.21), channel_id=1, source_target_pairs={{0,12},{2,14},{4,8},{6,10},{8,4},{10,6},{12,0},{14,2},{1,13},{3,15... | collective-permute-start | bytes 1572872 | tf_op jit(solution)/shard_map/ppermute | solution.py:452
  25.8 26.6 %collective-permute-start.9 = (bf16[1024,256]{1,0:T(8,128)(2,1)}, bf16[1024,256]{1,0:T(8,128)(2,1)S(1)}, u32[]{:S(2)}, u32[]{:S(2)}) collective-permute-start(bf16[1024,256]{1,0:T(8,128)(2,1)} %get-tuple-element.22), channel_id=1, source_target_pairs={{0,4},{2,6},{4,0},{6,2},{8,12},{10,14},{12,8},{14,10},{1,5},{3,7},... | collective-permute-start | bytes 1572872 | tf_op jit(solution)/shard_map/ppermute | solution.py:452
  26.8 53.7 %collective-permute-start.11 = (bf16[1024,256]{1,0:T(8,128)(2,1)}, bf16[1024,256]{1,0:T(8,128)(2,1)S(1)}, u32[]{:S(2)}, u32[]{:S(2)}) collective-permute-start(bf16[1024,256]{1,0:T(8,128)(2,1)} %get-tuple-element.24), channel_id=1, source_target_pairs={{0,8},{2,10},{4,12},{6,14},{8,0},{10,2},{12,4},{14,6},{1,9},{3,11}... | collective-permute-start | bytes 1572872 | tf_op jit(solution)/shard_map/ppermute | solution.py:452
  39.7 40.9 %collective-permute-start.8 = (bf16[1024,256]{1,0:T(8,128)(2,1)S(1)}, bf16[1024,256]{1,0:T(8,128)(2,1)S(1)}, u32[]{:S(2)}, u32[]{:S(2)}) collective-permute-start(bf16[1024,256]{1,0:T(8,128)(2,1)S(1)} %get-tuple-element.23), channel_id=1, source_target_pairs={{0,2},{2,0},{4,6},{6,4},{8,10},{10,8},{12,14},{14,12},{1,3},{3,1},... | collective-permute-start | bytes 1572872 | tf_op jit(solution)/shard_map/ppermute | solution.py:452
  43.2 37.9 %collective-permute-start.7 = (bf16[4,128,512]{2,1,0:T(8,128)(2,1)}, bf16[4,128,512]{2,1,0:T(8,128)(2,1)S(1)}, u32[]{:S(2)}, u32[]{:S(2)}) collective-permute-start(bf16[4,128,512]{2,1,0:T(8,128)(2,1)} %pad_maximum_fusion.1), channel_id=1, source_target_pairs={{0,2},{2,0},{4,6},{6,4},{8,10},{10,8},{12,14},{14,12},{1,3},{3,1},... | collective-permute-start | bytes 1572872 | tf_op jit(solution)/shard_map/ppermute | solution.py:452
  49.1 165.7 %collective-permute-start.18 = (bf16[4,512,1024]{2,1,0:T(8,128)(2,1)}, bf16[4,512,1024]{2,1,0:T(8,128)(2,1)S(1)}, u32[]{:S(2)}, u32[]{:S(2)}) collective-permute-start(bf16[4,512,1024]{2,1,0:T(8,128)(2,1)} %constant_dynamic-slice_fusion), channel_id=1, source_target_pairs={{0,2},{2,0},{4,6},{6,4},{8,10},{10,8},{12,14},{14,12},{1,3},{3,1},... | collective-permute-start | bytes 12582920 | tf_op jit(solution)/shard_map/ppermute | solution.py:452
  52.4 57.5 %collective-permute-start.14 = (bf16[1024,256]{1,0:T(8,128)(2,1)S(1)}, bf16[1024,256]{1,0:T(8,128)(2,1)S(1)}, u32[]{:S(2)}, u32[]{:S(2)}) collective-permute-start(bf16[1024,256]{1,0:T(8,128)(2,1)S(1)} %collective-permute-done.13), channel_id=1, source_target_pairs={{0,2},{2,0},{4,6},{6,4},{8,10},{10,8},{12,14},{14,12},{1,3},{3,1},... | collective-permute-start | bytes 1572872 | tf_op jit(solution)/shard_map/ppermute | solution.py:452
  80.5 12.4 %collective-permute-start.10 = (bf16[1024,256]{1,0:T(8,128)(2,1)S(1)}, bf16[1024,256]{1,0:T(8,128)(2,1)S(1)}, u32[]{:S(2)}, u32[]{:S(2)}) collective-permute-start(bf16[1024,256]{1,0:T(8,128)(2,1)S(1)} %collective-permute-done.9), channel_id=1, source_target_pairs={{0,2},{2,0},{4,6},{6,4},{8,10},{10,8},{12,14},{14,12},{1,3},{3,1},... | collective-permute-start | bytes 1572872 | tf_op jit(solution)/shard_map/ppermute | solution.py:452
  80.5 24.1 %collective-permute-start.12 = (bf16[1024,256]{1,0:T(8,128)(2,1)S(1)}, bf16[1024,256]{1,0:T(8,128)(2,1)S(1)}, u32[]{:S(2)}, u32[]{:S(2)}) collective-permute-start(bf16[1024,256]{1,0:T(8,128)(2,1)S(1)} %collective-permute-done.11), channel_id=1, source_target_pairs={{0,2},{2,0},{4,6},{6,4},{8,10},{10,8},{12,14},{14,12},{1,3},{3,1},... | collective-permute-start | bytes 1572872 | tf_op jit(solution)/shard_map/ppermute | solution.py:452
  121.9 37.9 %collective-permute-start.29 = (bf16[256,512]{1,0:T(8,128)(2,1)S(1)}, bf16[256,512]{1,0:T(8,128)(2,1)S(1)}, u32[]{:S(2)}, u32[]{:S(2)}) collective-permute-start(bf16[256,512]{1,0:T(8,128)(2,1)S(1)} %attend.15), channel_id=1, source_target_pairs={{0,4},{2,6},{4,0},{6,2},{8,12},{10,14},{12,8},{14,10},{1,5},{3,7},... | collective-permute-start | bytes 786440 | tf_op jit(solution)/shard_map/ppermute | solution.py:452
  141.1 51.4 %collective-permute-start.25 = (bf16[256,512]{1,0:T(8,128)(2,1)S(1)}, bf16[256,512]{1,0:T(8,128)(2,1)S(1)}, u32[]{:S(2)}, u32[]{:S(2)}) collective-permute-start(bf16[256,512]{1,0:T(8,128)(2,1)S(1)} %attend.14), channel_id=1, source_target_pairs={{0,4},{2,6},{4,0},{6,2},{8,12},{10,14},{12,8},{14,10},{1,5},{3,7},... | collective-permute-start | bytes 786440 | tf_op jit(solution)/shard_map/ppermute | solution.py:452
  159.5 32.2 %collective-permute-start.20 = (bf16[256,512]{1,0:T(8,128)(2,1)S(1)}, bf16[256,512]{1,0:T(8,128)(2,1)S(1)}, u32[]{:S(2)}, u32[]{:S(2)}) collective-permute-start(bf16[256,512]{1,0:T(8,128)(2,1)S(1)} %attend.13), channel_id=1, source_target_pairs={{0,4},{2,6},{4,0},{6,2},{8,12},{10,14},{12,8},{14,10},{1,5},{3,7},... | collective-permute-start | bytes 786440 | tf_op jit(solution)/shard_map/ppermute | solution.py:452
  159.9 37.9 %collective-permute-start.30 = (bf16[2,256,512]{2,1,0:T(8,128)(2,1)S(1)}, bf16[2,256,512]{2,1,0:T(8,128)(2,1)S(1)}, u32[]{:S(2)}, u32[]{:S(2)}) collective-permute-start(bf16[2,256,512]{2,1,0:T(8,128)(2,1)S(1)} %pad_maximum_fusion.5.near), channel_id=1, source_target_pairs={{4,8},{6,10},{8,4},{10,6},{5,9},{7,11},{9,5},{11,7},{20,24},{22,26... | collective-permute-start | bytes 1572872 | tf_op jit(solution)/shard_map/ppermute | solution.py:452
  185.8 11.2 %collective-permute-start.15 = (bf16[256,512]{1,0:T(8,128)(2,1)S(1)}, bf16[256,512]{1,0:T(8,128)(2,1)S(1)}, u32[]{:S(2)}, u32[]{:S(2)}) collective-permute-start(bf16[256,512]{1,0:T(8,128)(2,1)S(1)} %attend.11), channel_id=1, source_target_pairs={{0,4},{2,6},{4,0},{6,2},{8,12},{10,14},{12,8},{14,10},{1,5},{3,7},... | collective-permute-start | bytes 786440 | tf_op jit(solution)/shard_map/ppermute | solution.py:452
  191.7 7.4 %collective-permute-start.21 = (bf16[2,256,512]{2,1,0:T(8,128)(2,1)S(1)}, bf16[2,256,512]{2,1,0:T(8,128)(2,1)S(1)}, u32[]{:S(2)}, u32[]{:S(2)}) collective-permute-start(bf16[2,256,512]{2,1,0:T(8,128)(2,1)S(1)} %pad_maximum_fusion.3.near), channel_id=1, source_target_pairs={{4,8},{6,10},{8,4},{10,6},{5,9},{7,11},{9,5},{11,7},{20,24},{22,26... | collective-permute-start | bytes 1572872 | tf_op jit(solution)/shard_map/ppermute | solution.py:452
  192.5 7.9 %collective-permute-start.26 = (bf16[2,256,512]{2,1,0:T(8,128)(2,1)S(1)}, bf16[2,256,512]{2,1,0:T(8,128)(2,1)S(1)}, u32[]{:S(2)}, u32[]{:S(2)}) collective-permute-start(bf16[2,256,512]{2,1,0:T(8,128)(2,1)S(1)} %pad_maximum_fusion.4.near), channel_id=1, source_target_pairs={{4,8},{6,10},{8,4},{10,6},{5,9},{7,11},{9,5},{11,7},{20,24},{22,26... | collective-permute-start | bytes 1572872 | tf_op jit(solution)/shard_map/ppermute | solution.py:452
  197.8 17.0 %collective-permute-start.31 = (bf16[2,256,512]{2,1,0:T(8,128)(2,1)S(1)}, bf16[2,256,512]{2,1,0:T(8,128)(2,1)S(1)}, u32[]{:S(2)}, u32[]{:S(2)}) collective-permute-start(bf16[2,256,512]{2,1,0:T(8,128)(2,1)S(1)} %collective-permute-done.30.refs_0_), channel_id=1, source_target_pairs={{4,0},{6,2},{8,12},{10,14},{5,1},{7,3},{9,13},{11,15},{20,16},{22,... | collective-permute-start | bytes 1572872 | tf_op jit(solution)/shard_map/ppermute | solution.py:452
  199.1 26.9 %collective-permute-start.22 = (bf16[2,256,512]{2,1,0:T(8,128)(2,1)S(1)}, bf16[2,256,512]{2,1,0:T(8,128)(2,1)S(1)}, u32[]{:S(2)}, u32[]{:S(2)}) collective-permute-start(bf16[2,256,512]{2,1,0:T(8,128)(2,1)S(1)} %collective-permute-done.21.refs_0_), channel_id=1, source_target_pairs={{4,0},{6,2},{8,12},{10,14},{5,1},{7,3},{9,13},{11,15},{20,16},{22,... | collective-permute-start | bytes 1572872 | tf_op jit(solution)/shard_map/ppermute | solution.py:452
  200.4 36.9 %collective-permute-start.27 = (bf16[2,256,512]{2,1,0:T(8,128)(2,1)S(1)}, bf16[2,256,512]{2,1,0:T(8,128)(2,1)S(1)}, u32[]{:S(2)}, u32[]{:S(2)}) collective-permute-start(bf16[2,256,512]{2,1,0:T(8,128)(2,1)S(1)} %collective-permute-done.26.refs_0_), channel_id=1, source_target_pairs={{4,0},{6,2},{8,12},{10,14},{5,1},{7,3},{9,13},{11,15},{20,16},{22,... | collective-permute-start | bytes 1572872 | tf_op jit(solution)/shard_map/ppermute | solution.py:452
  201.7 44.1 %collective-permute-start.17 = (bf16[2,256,512]{2,1,0:T(8,128)(2,1)S(1)}, bf16[2,256,512]{2,1,0:T(8,128)(2,1)S(1)}, u32[]{:S(2)}, u32[]{:S(2)}) collective-permute-start(bf16[2,256,512]{2,1,0:T(8,128)(2,1)S(1)} %collective-permute-done.16.refs_0_), channel_id=1, source_target_pairs={{4,0},{6,2},{8,12},{10,14},{5,1},{7,3},{9,13},{11,15},{20,16},{22,... | collective-permute-start | bytes 1572872 | tf_op jit(solution)/shard_map/ppermute | solution.py:452
  217.8 29.4 %collective-permute-start.32 = (bf16[256,1024]{1,0:T(8,128)(2,1)S(1)}, bf16[256,1024]{1,0:T(8,128)(2,1)S(1)}, u32[]{:S(2)}, u32[]{:S(2)}) collective-permute-start(bf16[256,1024]{1,0:T(8,128)(2,1)S(1)} %get-tuple-element.20), channel_id=1, source_target_pairs={{0,2},{2,0},{4,6},{6,4},{8,10},{10,8},{12,14},{14,12},{1,3},{3,1},... | collective-permute-start | bytes 1572872 | tf_op jit(solution)/shard_map/ppermute | solution.py:452
  229.3 19.5 %collective-permute-start.23 = (bf16[256,1024]{1,0:T(8,128)(2,1)S(1)}, bf16[256,1024]{1,0:T(8,128)(2,1)S(1)}, u32[]{:S(2)}, u32[]{:S(2)}) collective-permute-start(bf16[256,1024]{1,0:T(8,128)(2,1)S(1)} %get-tuple-element.16), channel_id=1, source_target_pairs={{0,2},{2,0},{4,6},{6,4},{8,10},{10,8},{12,14},{14,12},{1,3},{3,1},... | collective-permute-start | bytes 1572872 | tf_op jit(solution)/shard_map/ppermute | solution.py:452
  240.3 10.8 %collective-permute-start.28 = (bf16[256,1024]{1,0:T(8,128)(2,1)S(1)}, bf16[256,1024]{1,0:T(8,128)(2,1)S(1)}, u32[]{:S(2)}, u32[]{:S(2)}) collective-permute-start(bf16[256,1024]{1,0:T(8,128)(2,1)S(1)} %get-tuple-element.18), channel_id=1, source_target_pairs={{0,2},{2,0},{4,6},{6,4},{8,10},{10,8},{12,14},{14,12},{1,3},{3,1},... | collective-permute-start | bytes 1572872 | tf_op jit(solution)/shard_map/ppermute | solution.py:452
  247.2 16.1 %collective-permute-start.19 = (bf16[256,1024]{1,0:T(8,128)(2,1)S(1)}, bf16[256,1024]{1,0:T(8,128)(2,1)S(1)}, u32[]{:S(2)}, u32[]{:S(2)}) collective-permute-start(bf16[256,1024]{1,0:T(8,128)(2,1)S(1)} %project.8), channel_id=1, source_target_pairs={{0,2},{2,0},{4,6},{6,4},{8,10},{10,8},{12,14},{14,12},{1,3},{3,1},... | collective-permute-start | bytes 1572872 | tf_op jit(solution)/shard_map/ppermute | solution.py:452
  247.4 14.9 %collective-permute-start.33 = (bf16[256,1024]{1,0:T(8,128)(2,1)S(1)}, bf16[256,1024]{1,0:T(8,128)(2,1)S(1)}, u32[]{:S(2)}, u32[]{:S(2)}) collective-permute-start(bf16[256,1024]{1,0:T(8,128)(2,1)S(1)} %add_convert_fusion), channel_id=1, source_target_pairs={{0,1},{1,0},{2,3},{3,2},{4,5},{5,4},{6,7},{7,6},{8,9},{9,8},{10,11... | collective-permute-start | bytes 1572872 | tf_op jit(solution)/shard_map/ppermute | solution.py:452
  248.9 24.1 %collective-permute-start.24 = (bf16[256,1024]{1,0:T(8,128)(2,1)S(1)}, bf16[256,1024]{1,0:T(8,128)(2,1)S(1)}, u32[]{:S(2)}, u32[]{:S(2)}) collective-permute-start(bf16[256,1024]{1,0:T(8,128)(2,1)S(1)} %add_convert_fusion.1), channel_id=1, source_target_pairs={{0,1},{1,0},{2,3},{3,2},{4,5},{5,4},{6,7},{7,6},{8,9},{9,8},{10,11... | collective-permute-start | bytes 1572872 | tf_op jit(solution)/shard_map/ppermute | solution.py:452
  (5 other events, 121.7 us)

commit v4 on v3

--- a/solution.py
+++ b/solution.py
@@ -328,12 +328,13 @@
     return z ^ i if i < 2 else far ^ (i % 2)
 
 
-def project_kernel(sides, held, far, pos, near, *refs):
+def project_kernel(kinds, held, far, pos, near, *refs):
+    sides = len(kinds)
     come, out = refs[:2] if far else (near, near)
     refs = refs[2 * far :]
     w_refs, refs = refs[:sides], refs[sides:]
     bases, refs = refs[: sides * held], refs[sides * held :]
-    o_refs, (parts, sems) = refs[:sides], refs[sides:]
+    o_refs, (parts, w_swap, sems, w_sems) = refs[:sides], refs[sides:]
     ends = (pos[0] == 0) | (pos[0] == 3)
 
     def bring(i, source):
@@ -352,45 +353,58 @@
             bring(1, come).start()
 
     used = range(2 * held, 4 if far else 2)
+    places = [piece_chip(i, pos[0]) for i in range(4)]
+    copies = {}
+    if "swap" in kinds:
+        source = w_refs[kinds.index("swap")]
+        for i in used:
+            copies[i] = pltpu.make_async_copy(source.at[places[i]], w_swap.at[i], w_sems.at[i])
+            copies[i].start()
     for i in range(used.start // 2, used.stop // 2):
         bring(i, near).wait()
     depth = near.shape[2]
     tile = 256
     own_rows = pl.ds(pl.multiple_of(pos[1] * depth, depth), depth)
-    places = [piece_chip(i, pos[0]) for i in range(4)]
-
-    for at in range(0, o_refs[0].shape[1], tile):
-        columns = slice(at, at + tile)
-        for side, (w_ref, o_ref) in enumerate(zip(w_refs, o_refs)):
-            w_rows = own_rows if w_ref.shape[1] > depth else slice(0, depth)
-            terms = [
-                jnp.dot(
-                    parts[i],
-                    w_ref[places[i], w_rows, columns],
-                    preferred_element_type=jnp.float32,
-                )
-                for i in used
-            ]
+
+    for side in sorted(range(sides), key=lambda i: kinds[i] == "swap"):
+        if kinds[side] == "swap":
+            for i in used:
+                copies[i].wait()
+        for at in range(0, o_refs[side].shape[1], tile):
+            columns = slice(at, at + tile)
+            terms = []
+            for i in used:
+                if kinds[side] == "swap":
+                    weight = w_swap[i, :, columns]
+                else:
+                    weight = w_refs[side][places[i], own_rows, columns]
+                terms.append(jnp.dot(parts[i], weight, preferred_element_type=jnp.float32))
             if held:
                 terms.append(bases[side][:, columns])
+            o_ref = o_refs[side]
             o_ref[:, columns] = functools.reduce(jnp.add, terms).astype(o_ref.dtype)
 
 
 def project(pos, near, far, weights, types, bases=()):
+    vmem = pl.BlockSpec(memory_space=pltpu.VMEM)
     rows, depth = near.shape[1:]
     chips, _, columns = weights[0].shape
     sides = len(weights)
-    vmem = pl.BlockSpec(memory_space=pltpu.VMEM)
+    kinds = tuple("swap" if w.shape[1] == depth else "own" for w in weights)
+    places = [pl.BlockSpec(memory_space=pl.ANY) if kind == "swap" else vmem for kind in kinds]
     return pl.pallas_call(
-        functools.partial(project_kernel, sides, bool(bases), bool(far)),
+        functools.partial(project_kernel, kinds, bool(bases), bool(far)),
         out_shape=tuple(jax.ShapeDtypeStruct((rows, columns), kind) for kind in types),
         in_specs=[pl.BlockSpec(memory_space=pltpu.SMEM)]
         + [pl.BlockSpec(memory_space=pl.ANY)] * (1 + len(far))
-        + [vmem] * (sides + len(bases)),
+        + places
+        + [vmem] * len(bases),
         out_specs=(vmem,) * sides,
         scratch_shapes=[
             pltpu.VMEM((chips, rows, depth), jnp.bfloat16),
+            pltpu.VMEM((chips, depth, columns), jnp.bfloat16),
             pltpu.SemaphoreType.DMA((2,)),
+            pltpu.SemaphoreType.DMA((chips,)),
         ],
         compiler_params=pltpu.CompilerParams(vmem_limit_bytes=project_vmem),
         cost_estimate=pl.CostEstimate(
@@ -497,7 +511,7 @@
     pos = jnp.stack([z, core, row]).astype(jnp.int32)
     q_two = (q_own, q_swap)
     whole = [attend((k,), tab, pos, q_two, kv[k], 2 * chips) for k in range(2)]
-    halves = [attend((2,), tab, pos, q_two, kv[2], chips, (mine, 0)) for mine in (False, True)]
+    half = attend((2,), tab, pos, q_two, kv[2], chips, (False, 0))
 
     w_own = out_weight.reshape(chips, wide, out_weight.shape[1])
     w_swap = lax.dynamic_slice(
@@ -509,8 +523,9 @@
     every_key = [a for of in kv for a in of]
 
     def chunk(i, part, count):
-        state = [(True, a) for a in whole] + [(False, halves[part[0]])]
-        mine = attend((3,), tab, pos, q_two, every_key, count, part, state)
+        state = [(True, a) for a in whole] + [(False, half)] * (not part[0])
+        late = (2, 3) if part[0] else (3,)
+        mine = attend(late, tab, pos, q_two, every_key, count, part, state)
         near = jnp.stack([mine, permute(mine, apart(2))])
         come = permute(near, across)
         out = permute(come, outward)

time: 275 us -> 274 us (level)
    pallas_call x8 -> x7, Pallas kernels: 102 us -> 101 us  [attend(): pl.pallas_call(functools.partial(attend_kernel, folded, part, last, heads...]
  transfers between devices with their start and end apart: 34 -> 34, of which waited for: 11 -> 11; matrix products, arithmetic and copies ran while one was open for 7% -> 8% of each run, Pallas kernels for 43% -> 43%
where the time goes in v4:
time: 274 us; the launch traced here: 273 us
  Pallas kernels  118 us (43%)
  waiting for transfers between devices  98 us (36%)
  starting transfers between devices  34 us (12%)
  local copies, waits for them, and re-layouts  13.9 us (5%)
  other arithmetic  8.29 us (3%)
    pallas_call x7, Pallas kernels, attend(): pl.pallas_call(functools.partial(attend_kernel, folded, part, last, heads...  101 us
    ppermute x34, waiting for transfers between devices, permute(): return lax.ppermute(array, axis, perm)  98 us
    ppermute x34, starting transfers between devices, permute(): return lax.ppermute(array, axis, perm)  34 us
    pallas_call x6, Pallas kernels, project(): pl.pallas_call(functools.partial(project_kernel, kinds, bool(bases), bool...  15.7 us
  transfers between devices with their start and end apart: 34, of which 11 were waited for; matrix products, arithmetic and copies ran while one was open for 8% of the time, Pallas kernels for 43%

profile of v4, /device:TPU:0, one launch (start us, length us, event | category | flops | bytes accessed | tf_op | source)
XLA Modules:
  0.0 273.0 jit_solution(7629119416161852769)
XLA Ops:
  1.6 3.1 %collective-permute-start = (bf16[16,128]{1,0:T(8,128)(2,1)S(1)}, bf16[16,128]{1,0:T(8,128)(2,1)S(1)}, u32[]{:S(2)}, u32[]{:S(2)}) collective-permute-start(bf16[16,128]{1,0:T(8,128)(2,1)S(1)} %fusion.7), channel_id=1, source_target_pairs={{0,4},{2,6},{4,0},{6,2},{8,12},{10,14},{12,8},{14,10},{1,5},{3,7},... | collective-permute-start | bytes 12296 | tf_op jit(solution)/shard_map/ppermute | solution.py:466
  4.7 2.6 collective-permute-start.1
  7.3 1.9 constant_dynamic-slice_fusion.7
  10.0 3.5 %collective-permute-start.5 = (bf16[128,1024]{1,0:T(8,128)(2,1)S(1)}, bf16[128,1024]{1,0:T(8,128)(2,1)}, u32[]{:S(2)}, u32[]{:S(2)}) collective-permute-start(bf16[128,1024]{1,0:T(8,128)(2,1)S(1)} %get-tuple-element.28), channel_id=1, source_target_pairs={{0,8},{2,10},{4,12},{6,14},{8,0},{10,2},{12,4},{14,6},{1,9},{3,11}... | collective-permute-start | bytes 786440 | tf_op jit(solution)/shard_map/ppermute | solution.py:466
  13.6 4.8 %constant_dynamic-slice_fusion = bf16[4,512,1024]{2,1,0:T(8,128)(2,1)} fusion(bf16[4,1024,1024]{2,1,0:T(8,128)(2,1)} %bitcast.45, s32[]{:T(128)S(6)} %select_n.73), kind=kLoop, calls=%fused_computation.34 | loop fusion | bytes 8388612 | tf_op jit(solution)/shard_map/dynamic_slice | solution.py:517
  20.8 3.8 %collective-permute-start.13 = (bf16[1024,256]{1,0:T(8,128)(2,1)}, bf16[1024,256]{1,0:T(8,128)(2,1)S(1)}, u32[]{:S(2)}, u32[]{:S(2)}) collective-permute-start(bf16[1024,256]{1,0:T(8,128)(2,1)} %get-tuple-element.21), channel_id=1, source_target_pairs={{0,12},{2,14},{4,8},{6,10},{8,4},{10,6},{12,0},{14,2},{1,13},{3,15... | collective-permute-start | bytes 1572872 | tf_op jit(solution)/shard_map/ppermute | solution.py:466
  28.5 11.1 %collective-permute-done.5 = bf16[128,1024]{1,0:T(8,128)(2,1)} collective-permute-done((bf16[128,1024]{1,0:T(8,128)(2,1)S(1)}, bf16[128,1024]{1,0:T(8,128)(2,1)}, u32[]{:S(2)}, u32[]{:S(2)}) %collective-permute-start.5) | collective-permute-done | bytes 262176 | tf_op jit(solution)/shard_map/ppermute | solution.py:466
  40.7 1.6 dynamic-slice_bitcast_fusion
  49.2 3.2 %collective-permute-done.9 = bf16[1024,256]{1,0:T(8,128)(2,1)S(1)} collective-permute-done((bf16[1024,256]{1,0:T(8,128)(2,1)}, bf16[1024,256]{1,0:T(8,128)(2,1)S(1)}, u32[]{:S(2)}, u32[]{:S(2)}) %collective-permute-start.9) | collective-permute-done | bytes 524320 | tf_op jit(solution)/shard_map/ppermute | solution.py:466
  52.4 28.1 %collective-permute-done.11 = bf16[1024,256]{1,0:T(8,128)(2,1)S(1)} collective-permute-done((bf16[1024,256]{1,0:T(8,128)(2,1)}, bf16[1024,256]{1,0:T(8,128)(2,1)S(1)}, u32[]{:S(2)}, u32[]{:S(2)}) %collective-permute-start.11) | collective-permute-done | bytes 524320 | tf_op jit(solution)/shard_map/ppermute | solution.py:466
  81.1 11.9 %attend.7.refs_10_ = f32[8,520,256]{2,1,0:T(8,128)S(1)} custom-call(s32[4,8,17]{2,1,0:T(8,128)S(1)} %pad_add_fusion.tab, s32[3]{0:T(128)S(1)} %pad_add_fusion.1.pos, bf16[4,128,512]{2,1,0:T(8,128)(2,1)S(1)} %pad_maximum_fusion.refs_0_, bf16[4,128,512]{2,1,0:T(8,128)(2,1)S(1)} %collective-permute-done.7.refs_1_, bf16[8,128,256]{2,1,0:T(8,128)(2,1)S(1)} %bitcast.53, ...), custom_call_target="tpu_custom_call" | custom-call | flops 8589934592 | bytes 524288 | tf_op jit(solution)/shard_map/attend/pallas_call | solution.py:306
  93.0 11.7 %attend.8.refs_11_ = f32[8,520,256]{2,1,0:T(8,128)S(1)} custom-call(s32[4,8,17]{2,1,0:T(8,128)S(1)} %pad_add_fusion.tab, s32[3]{0:T(128)S(1)} %pad_add_fusion.1.pos, bf16[4,128,512]{2,1,0:T(8,128)(2,1)S(1)} %pad_maximum_fusion.refs_0_, bf16[4,128,512]{2,1,0:T(8,128)(2,1)S(1)} %collective-permute-done.7.refs_1_, bf16[8,128,256]{2,1,0:T(8,128)(2,1)S(1)} %bitcast.62, ...), custom_call_target="tpu_custom_call" | custom-call | flops 8589934592 | bytes 524288 | tf_op jit(solution)/shard_map/attend/pallas_call | solution.py:306
  104.7 5.2 %attend.10.refs_12_ = f32[4,520,256]{2,1,0:T(8,128)S(1)} custom-call(s32[4,8,17]{2,1,0:T(8,128)S(1)} %pad_add_fusion.tab, s32[3]{0:T(128)S(1)} %pad_add_fusion.1.pos, bf16[4,128,512]{2,1,0:T(8,128)(2,1)S(1)} %pad_maximum_fusion.refs_0_, bf16[4,128,512]{2,1,0:T(8,128)(2,1)S(1)} %collective-permute-done.7.refs_1_, bf16[8,128,256]{2,1,0:T(8,128)(2,1)S(1)} %bitcast.67, ...), custom_call_target="tpu_custom_call" | custom-call | flops 4294967296 | bytes 262144 | tf_op jit(solution)/shard_map/attend/pallas_call | solution.py:306
  109.9 11.9 %attend.13 = bf16[256,512]{1,0:T(8,128)(2,1)S(1)} custom-call(s32[4,8,17]{2,1,0:T(8,128)S(1)} %pad_add_fusion.tab, s32[3]{0:T(128)S(1)} %pad_add_fusion.1.pos, bf16[4,128,512]{2,1,0:T(8,128)(2,1)S(1)} %pad_maximum_fusion.refs_0_, bf16[4,128,512]{2,1,0:T(8,128)(2,1)S(1)} %collective-permute-done.7.refs_1_, bf16[8,128,256]{2,1,0:T(8,128)(2,1)S(1)} %bitcast.54, ...), custom_call_target="tpu_custom_call" | custom-call | flops 2147483648 | bytes 131072 | tf_op jit(solution)/shard_map/attend/pallas_call | solution.py:306
  122.2 13.1 %attend.12 = bf16[256,512]{1,0:T(8,128)(2,1)S(1)} custom-call(s32[4,8,17]{2,1,0:T(8,128)S(1)} %pad_add_fusion.tab, s32[3]{0:T(128)S(1)} %pad_add_fusion.1.pos, bf16[4,128,512]{2,1,0:T(8,128)(2,1)S(1)} %pad_maximum_fusion.refs_0_, bf16[4,128,512]{2,1,0:T(8,128)(2,1)S(1)} %collective-permute-done.7.refs_1_, bf16[8,128,256]{2,1,0:T(8,128)(2,1)S(1)} %bitcast.55, ...), custom_call_target="tpu_custom_call" | custom-call | flops 4294967296 | bytes 262144 | tf_op jit(solution)/shard_map/attend/pallas_call | solution.py:306
  135.3 1.8 collective-permute-start.25
  137.2 17.1 %attend.11 = bf16[256,512]{1,0:T(8,128)(2,1)S(1)} custom-call(s32[4,8,17]{2,1,0:T(8,128)S(1)} %pad_add_fusion.tab, s32[3]{0:T(128)S(1)} %pad_add_fusion.1.pos, bf16[4,128,512]{2,1,0:T(8,128)(2,1)S(1)} %pad_maximum_fusion.refs_0_, bf16[4,128,512]{2,1,0:T(8,128)(2,1)S(1)} %collective-permute-done.7.refs_1_, bf16[8,128,256]{2,1,0:T(8,128)(2,1)S(1)} %bitcast.56, ...), custom_call_target="tpu_custom_call" | custom-call | flops 2147483648 | bytes 131072 | tf_op jit(solution)/shard_map/attend/pallas_call | solution.py:306
  155.3 29.7 %attend.9 = bf16[256,512]{1,0:T(8,128)(2,1)S(1)} custom-call(s32[4,8,17]{2,1,0:T(8,128)S(1)} %pad_add_fusion.tab, s32[3]{0:T(128)S(1)} %pad_add_fusion.1.pos, bf16[4,128,512]{2,1,0:T(8,128)(2,1)S(1)} %pad_maximum_fusion.refs_0_, bf16[4,128,512]{2,1,0:T(8,128)(2,1)S(1)} %collective-permute-done.7.refs_1_, bf16[8,128,256]{2,1,0:T(8,128)(2,1)S(1)} %bitcast.57, ...), custom_call_target="tpu_custom_call" | custom-call | flops 4294967296 | bytes 262144 | tf_op jit(solution)/shard_map/attend/pallas_call | solution.py:306
  185.0 5.5 %collective-permute-start.15 = (bf16[256,512]{1,0:T(8,128)(2,1)S(1)}, bf16[256,512]{1,0:T(8,128)(2,1)S(1)}, u32[]{:S(2)}, u32[]{:S(2)}) collective-permute-start(bf16[256,512]{1,0:T(8,128)(2,1)S(1)} %attend.9), channel_id=1, source_target_pairs={{0,4},{2,6},{4,0},{6,2},{8,12},{10,14},{12,8},{14,10},{1,5},{3,7},... | collective-permute-start | bytes 786440 | tf_op jit(solution)/shard_map/ppermute | solution.py:466
  192.0 3.8 %collective-permute-done.15 = bf16[256,512]{1,0:T(8,128)(2,1)S(1)} collective-permute-done((bf16[256,512]{1,0:T(8,128)(2,1)S(1)}, bf16[256,512]{1,0:T(8,128)(2,1)S(1)}, u32[]{:S(2)}, u32[]{:S(2)}) %collective-permute-start.15) | collective-permute-done | bytes 262176 | tf_op jit(solution)/shard_map/ppermute | solution.py:466
  201.9 11.8 %collective-permute-done.31.refs_1_ = bf16[2,256,512]{2,1,0:T(8,128)(2,1)S(1)} collective-permute-done((bf16[2,256,512]{2,1,0:T(8,128)(2,1)S(1)}, bf16[2,256,512]{2,1,0:T(8,128)(2,1)S(1)}, u32[]{:S(2)}, u32[]{:S(2)}) %collective-permute-start.31) | collective-permute-done | bytes 524320 | tf_op jit(solution)/shard_map/ppermute | solution.py:466
  213.7 3.5 %project.11 = (bf16[256,1024]{1,0:T(8,128)(2,1)S(1)}, f32[256,1024]{1,0:T(8,128)S(1)}) custom-call(s32[3]{0:T(128)S(1)} %pad_add_fusion.1.pos, bf16[2,256,512]{2,1,0:T(8,128)(2,1)S(1)} %pad_maximum_fusion.5.near, bf16[2,256,512]{2,1,0:T(8,128)(2,1)S(1)} %collective-permute-done.30.refs_0_, bf16[2,256,512]{2,1,0:T(8,128)(2,1)S(1)} %collective-permute-done.31.refs_1_, ...), custom_call_target="tpu_custom_call" | custom-call | flops 2147483648 | bytes 11534336 | tf_op jit(solution)/shard_map/project/pallas_call | solution.py:395
  217.2 7.7 %collective-permute-done.22.refs_1_ = bf16[2,256,512]{2,1,0:T(8,128)(2,1)S(1)} collective-permute-done((bf16[2,256,512]{2,1,0:T(8,128)(2,1)S(1)}, bf16[2,256,512]{2,1,0:T(8,128)(2,1)S(1)}, u32[]{:S(2)}, u32[]{:S(2)}) %collective-permute-start.22) | collective-permute-done | bytes 524320 | tf_op jit(solution)/shard_map/ppermute | solution.py:466
  224.9 3.7 %project.9 = (bf16[256,1024]{1,0:T(8,128)(2,1)S(1)}, f32[256,1024]{1,0:T(8,128)S(1)}) custom-call(s32[3]{0:T(128)S(1)} %pad_add_fusion.1.pos, bf16[2,256,512]{2,1,0:T(8,128)(2,1)S(1)} %pad_maximum_fusion.3.near, bf16[2,256,512]{2,1,0:T(8,128)(2,1)S(1)} %collective-permute-done.21.refs_0_, bf16[2,256,512]{2,1,0:T(8,128)(2,1)S(1)} %collective-permute-done.22.refs_1_, ...), custom_call_target="tpu_custom_call" | custom-call | flops 2147483648 | bytes 11534336 | tf_op jit(solution)/shard_map/project/pallas_call | solution.py:395
  228.7 7.4 %collective-permute-done.27.refs_1_ = bf16[2,256,512]{2,1,0:T(8,128)(2,1)S(1)} collective-permute-done((bf16[2,256,512]{2,1,0:T(8,128)(2,1)S(1)}, bf16[2,256,512]{2,1,0:T(8,128)(2,1)S(1)}, u32[]{:S(2)}, u32[]{:S(2)}) %collective-permute-start.27) | collective-permute-done | bytes 524320 | tf_op jit(solution)/shard_map/ppermute | solution.py:466
  236.1 3.5 %project.10 = (bf16[256,1024]{1,0:T(8,128)(2,1)S(1)}, f32[256,1024]{1,0:T(8,128)S(1)}) custom-call(s32[3]{0:T(128)S(1)} %pad_add_fusion.1.pos, bf16[2,256,512]{2,1,0:T(8,128)(2,1)S(1)} %pad_maximum_fusion.4.near, bf16[2,256,512]{2,1,0:T(8,128)(2,1)S(1)} %collective-permute-done.26.refs_0_, bf16[2,256,512]{2,1,0:T(8,128)(2,1)S(1)} %collective-permute-done.27.refs_1_, ...), custom_call_target="tpu_custom_call" | custom-call | flops 2147483648 | bytes 11534336 | tf_op jit(solution)/shard_map/project/pallas_call | solution.py:395
  239.7 2.2 project.6
  241.9 2.8 %collective-permute-done.17.refs_1_ = bf16[2,256,512]{2,1,0:T(8,128)(2,1)S(1)} collective-permute-done((bf16[2,256,512]{2,1,0:T(8,128)(2,1)S(1)}, bf16[2,256,512]{2,1,0:T(8,128)(2,1)S(1)}, u32[]{:S(2)}, u32[]{:S(2)}) %collective-permute-start.17) | collective-permute-done | bytes 524320 | tf_op jit(solution)/shard_map/ppermute | solution.py:466
  244.7 1.5 project.8
  248.7 1.4 project.7.own
  250.1 11.2 %collective-permute-done.33.theirs = bf16[256,1024]{1,0:T(8,128)(2,1)S(1)} collective-permute-done((bf16[256,1024]{1,0:T(8,128)(2,1)S(1)}, bf16[256,1024]{1,0:T(8,128)(2,1)S(1)}, u32[]{:S(2)}, u32[]{:S(2)}) %collective-permute-start.33) | collective-permute-done | bytes 524320 | tf_op jit(solution)/shard_map/ppermute | solution.py:466
  262.2 9.8 %collective-permute-done.24.theirs = bf16[256,1024]{1,0:T(8,128)(2,1)S(1)} collective-permute-done((bf16[256,1024]{1,0:T(8,128)(2,1)S(1)}, bf16[256,1024]{1,0:T(8,128)(2,1)S(1)}, u32[]{:S(2)}, u32[]{:S(2)}) %collective-permute-start.24) | collective-permute-done | bytes 524320 | tf_op jit(solution)/shard_map/ppermute | solution.py:466
  (98 shorter events, 30.6 us)
Async XLA Ops:
  1.6 19.1 %collective-permute-start = (bf16[16,128]{1,0:T(8,128)(2,1)S(1)}, bf16[16,128]{1,0:T(8,128)(2,1)S(1)}, u32[]{:S(2)}, u32[]{:S(2)}) collective-permute-start(bf16[16,128]{1,0:T(8,128)(2,1)S(1)} %fusion.7), channel_id=1, source_target_pairs={{0,4},{2,6},{4,0},{6,2},{8,12},{10,14},{12,8},{14,10},{1,5},{3,7},... | collective-permute-start | bytes 12296 | tf_op jit(solution)/shard_map/ppermute | solution.py:466
  4.7 16.1 %collective-permute-start.1 = (bf16[16,128]{1,0:T(8,128)(2,1)S(1)}, bf16[16,128]{1,0:T(8,128)(2,1)S(1)}, u32[]{:S(2)}, u32[]{:S(2)}) collective-permute-start(bf16[16,128]{1,0:T(8,128)(2,1)S(1)} %fusion.7), channel_id=1, source_target_pairs={{0,8},{2,10},{4,12},{6,14},{8,0},{10,2},{12,4},{14,6},{1,9},{3,11}... | collective-permute-start | bytes 12296 | tf_op jit(solution)/shard_map/ppermute | solution.py:466
  7.3 17.3 %collective-permute-start.2 = (bf16[16,128]{1,0:T(8,128)(2,1)S(1)}, bf16[16,128]{1,0:T(8,128)(2,1)S(1)}, u32[]{:S(2)}, u32[]{:S(2)}) collective-permute-start(bf16[16,128]{1,0:T(8,128)(2,1)S(1)} %fusion.7), channel_id=1, source_target_pairs={{0,12},{2,14},{4,8},{6,10},{8,4},{10,6},{12,0},{14,2},{1,13},{3,15... | collective-permute-start | bytes 12296 | tf_op jit(solution)/shard_map/ppermute | solution.py:466
  9.1 17.7 %collective-permute-start.4 = (bf16[128,1024]{1,0:T(8,128)(2,1)S(1)}, bf16[128,1024]{1,0:T(8,128)(2,1)}, u32[]{:S(2)}, u32[]{:S(2)}) collective-permute-start(bf16[128,1024]{1,0:T(8,128)(2,1)S(1)} %get-tuple-element.27), channel_id=1, source_target_pairs={{0,4},{2,6},{4,0},{6,2},{8,12},{10,14},{12,8},{14,10},{1,5},{3,7},... | collective-permute-start | bytes 786440 | tf_op jit(solution)/shard_map/ppermute | solution.py:466
  10.0 29.6 %collective-permute-start.5 = (bf16[128,1024]{1,0:T(8,128)(2,1)S(1)}, bf16[128,1024]{1,0:T(8,128)(2,1)}, u32[]{:S(2)}, u32[]{:S(2)}) collective-permute-start(bf16[128,1024]{1,0:T(8,128)(2,1)S(1)} %get-tuple-element.28), channel_id=1, source_target_pairs={{0,8},{2,10},{4,12},{6,14},{8,0},{10,2},{12,4},{14,6},{1,9},{3,11}... | collective-permute-start | bytes 786440 | tf_op jit(solution)/shard_map/ppermute | solution.py:466
  20.8 19.9 %collective-permute-start.6 = (bf16[128,1024]{1,0:T(8,128)(2,1)}, bf16[128,1024]{1,0:T(8,128)(2,1)}, u32[]{:S(2)}, u32[]{:S(2)}) collective-permute-start(bf16[128,1024]{1,0:T(8,128)(2,1)} %get-tuple-element.29), channel_id=1, source_target_pairs={{0,12},{2,14},{4,8},{6,10},{8,4},{10,6},{12,0},{14,2},{1,13},{3,15... | collective-permute-start | bytes 786440 | tf_op jit(solution)/shard_map/ppermute | solution.py:466
  20.8 28.3 %collective-permute-start.13 = (bf16[1024,256]{1,0:T(8,128)(2,1)}, bf16[1024,256]{1,0:T(8,128)(2,1)S(1)}, u32[]{:S(2)}, u32[]{:S(2)}) collective-permute-start(bf16[1024,256]{1,0:T(8,128)(2,1)} %get-tuple-element.21), channel_id=1, source_target_pairs={{0,12},{2,14},{4,8},{6,10},{8,4},{10,6},{12,0},{14,2},{1,13},{3,15... | collective-permute-start | bytes 1572872 | tf_op jit(solution)/shard_map/ppermute | solution.py:466
  25.8 26.6 %collective-permute-start.9 = (bf16[1024,256]{1,0:T(8,128)(2,1)}, bf16[1024,256]{1,0:T(8,128)(2,1)S(1)}, u32[]{:S(2)}, u32[]{:S(2)}) collective-permute-start(bf16[1024,256]{1,0:T(8,128)(2,1)} %get-tuple-element.22), channel_id=1, source_target_pairs={{0,4},{2,6},{4,0},{6,2},{8,12},{10,14},{12,8},{14,10},{1,5},{3,7},... | collective-permute-start | bytes 1572872 | tf_op jit(solution)/shard_map/ppermute | solution.py:466
  26.8 53.7 %collective-permute-start.11 = (bf16[1024,256]{1,0:T(8,128)(2,1)}, bf16[1024,256]{1,0:T(8,128)(2,1)S(1)}, u32[]{:S(2)}, u32[]{:S(2)}) collective-permute-start(bf16[1024,256]{1,0:T(8,128)(2,1)} %get-tuple-element.24), channel_id=1, source_target_pairs={{0,8},{2,10},{4,12},{6,14},{8,0},{10,2},{12,4},{14,6},{1,9},{3,11}... | collective-permute-start | bytes 1572872 | tf_op jit(solution)/shard_map/ppermute | solution.py:466
  39.7 40.9 %collective-permute-start.8 = (bf16[1024,256]{1,0:T(8,128)(2,1)S(1)}, bf16[1024,256]{1,0:T(8,128)(2,1)S(1)}, u32[]{:S(2)}, u32[]{:S(2)}) collective-permute-start(bf16[1024,256]{1,0:T(8,128)(2,1)S(1)} %get-tuple-element.23), channel_id=1, source_target_pairs={{0,2},{2,0},{4,6},{6,4},{8,10},{10,8},{12,14},{14,12},{1,3},{3,1},... | collective-permute-start | bytes 1572872 | tf_op jit(solution)/shard_map/ppermute | solution.py:466
  43.2 37.9 %collective-permute-start.7 = (bf16[4,128,512]{2,1,0:T(8,128)(2,1)}, bf16[4,128,512]{2,1,0:T(8,128)(2,1)S(1)}, u32[]{:S(2)}, u32[]{:S(2)}) collective-permute-start(bf16[4,128,512]{2,1,0:T(8,128)(2,1)} %pad_maximum_fusion.1), channel_id=1, source_target_pairs={{0,2},{2,0},{4,6},{6,4},{8,10},{10,8},{12,14},{14,12},{1,3},{3,1},... | collective-permute-start | bytes 1572872 | tf_op jit(solution)/shard_map/ppermute | solution.py:466
  49.1 164.5 %collective-permute-start.18 = (bf16[4,512,1024]{2,1,0:T(8,128)(2,1)}, bf16[4,512,1024]{2,1,0:T(8,128)(2,1)S(1)}, u32[]{:S(2)}, u32[]{:S(2)}) collective-permute-start(bf16[4,512,1024]{2,1,0:T(8,128)(2,1)} %constant_dynamic-slice_fusion), channel_id=1, source_target_pairs={{0,2},{2,0},{4,6},{6,4},{8,10},{10,8},{12,14},{14,12},{1,3},{3,1},... | collective-permute-start | bytes 12582920 | tf_op jit(solution)/shard_map/ppermute | solution.py:466
  52.4 57.5 %collective-permute-start.14 = (bf16[1024,256]{1,0:T(8,128)(2,1)S(1)}, bf16[1024,256]{1,0:T(8,128)(2,1)S(1)}, u32[]{:S(2)}, u32[]{:S(2)}) collective-permute-start(bf16[1024,256]{1,0:T(8,128)(2,1)S(1)} %collective-permute-done.13), channel_id=1, source_target_pairs={{0,2},{2,0},{4,6},{6,4},{8,10},{10,8},{12,14},{14,12},{1,3},{3,1},... | collective-permute-start | bytes 1572872 | tf_op jit(solution)/shard_map/ppermute | solution.py:466
  80.5 12.4 %collective-permute-start.10 = (bf16[1024,256]{1,0:T(8,128)(2,1)S(1)}, bf16[1024,256]{1,0:T(8,128)(2,1)S(1)}, u32[]{:S(2)}, u32[]{:S(2)}) collective-permute-start(bf16[1024,256]{1,0:T(8,128)(2,1)S(1)} %collective-permute-done.9), channel_id=1, source_target_pairs={{0,2},{2,0},{4,6},{6,4},{8,10},{10,8},{12,14},{14,12},{1,3},{3,1},... | collective-permute-start | bytes 1572872 | tf_op jit(solution)/shard_map/ppermute | solution.py:466
  80.5 24.1 %collective-permute-start.12 = (bf16[1024,256]{1,0:T(8,128)(2,1)S(1)}, bf16[1024,256]{1,0:T(8,128)(2,1)S(1)}, u32[]{:S(2)}, u32[]{:S(2)}) collective-permute-start(bf16[1024,256]{1,0:T(8,128)(2,1)S(1)} %collective-permute-done.11), channel_id=1, source_target_pairs={{0,2},{2,0},{4,6},{6,4},{8,10},{10,8},{12,14},{14,12},{1,3},{3,1},... | collective-permute-start | bytes 1572872 | tf_op jit(solution)/shard_map/ppermute | solution.py:466
  121.9 32.5 %collective-permute-start.29 = (bf16[256,512]{1,0:T(8,128)(2,1)S(1)}, bf16[256,512]{1,0:T(8,128)(2,1)S(1)}, u32[]{:S(2)}, u32[]{:S(2)}) collective-permute-start(bf16[256,512]{1,0:T(8,128)(2,1)S(1)} %attend.13), channel_id=1, source_target_pairs={{0,4},{2,6},{4,0},{6,2},{8,12},{10,14},{12,8},{14,10},{1,5},{3,7},... | collective-permute-start | bytes 786440 | tf_op jit(solution)/shard_map/ppermute | solution.py:466
  135.3 55.9 %collective-permute-start.25 = (bf16[256,512]{1,0:T(8,128)(2,1)S(1)}, bf16[256,512]{1,0:T(8,128)(2,1)S(1)}, u32[]{:S(2)}, u32[]{:S(2)}) collective-permute-start(bf16[256,512]{1,0:T(8,128)(2,1)S(1)} %attend.12), channel_id=1, source_target_pairs={{0,4},{2,6},{4,0},{6,2},{8,12},{10,14},{12,8},{14,10},{1,5},{3,7},... | collective-permute-start | bytes 786440 | tf_op jit(solution)/shard_map/ppermute | solution.py:466
  154.3 36.2 %collective-permute-start.20 = (bf16[256,512]{1,0:T(8,128)(2,1)S(1)}, bf16[256,512]{1,0:T(8,128)(2,1)S(1)}, u32[]{:S(2)}, u32[]{:S(2)}) collective-permute-start(bf16[256,512]{1,0:T(8,128)(2,1)S(1)} %attend.11), channel_id=1, source_target_pairs={{0,4},{2,6},{4,0},{6,2},{8,12},{10,14},{12,8},{14,10},{1,5},{3,7},... | collective-permute-start | bytes 786440 | tf_op jit(solution)/shard_map/ppermute | solution.py:466
  154.5 42.1 %collective-permute-start.30 = (bf16[2,256,512]{2,1,0:T(8,128)(2,1)S(1)}, bf16[2,256,512]{2,1,0:T(8,128)(2,1)S(1)}, u32[]{:S(2)}, u32[]{:S(2)}) collective-permute-start(bf16[2,256,512]{2,1,0:T(8,128)(2,1)S(1)} %pad_maximum_fusion.5.near), channel_id=1, source_target_pairs={{4,8},{6,10},{8,4},{10,6},{5,9},{7,11},{9,5},{11,7},{20,24},{22,26... | collective-permute-start | bytes 1572872 | tf_op jit(solution)/shard_map/ppermute | solution.py:466
  185.0 10.8 %collective-permute-start.15 = (bf16[256,512]{1,0:T(8,128)(2,1)S(1)}, bf16[256,512]{1,0:T(8,128)(2,1)S(1)}, u32[]{:S(2)}, u32[]{:S(2)}) collective-permute-start(bf16[256,512]{1,0:T(8,128)(2,1)S(1)} %attend.9), channel_id=1, source_target_pairs={{0,4},{2,6},{4,0},{6,2},{8,12},{10,14},{12,8},{14,10},{1,5},{3,7},... | collective-permute-start | bytes 786440 | tf_op jit(solution)/shard_map/ppermute | solution.py:466
  190.6 7.4 %collective-permute-start.21 = (bf16[2,256,512]{2,1,0:T(8,128)(2,1)S(1)}, bf16[2,256,512]{2,1,0:T(8,128)(2,1)S(1)}, u32[]{:S(2)}, u32[]{:S(2)}) collective-permute-start(bf16[2,256,512]{2,1,0:T(8,128)(2,1)S(1)} %pad_maximum_fusion.3.near), channel_id=1, source_target_pairs={{4,8},{6,10},{8,4},{10,6},{5,9},{7,11},{9,5},{11,7},{20,24},{22,26... | collective-permute-start | bytes 1572872 | tf_op jit(solution)/shard_map/ppermute | solution.py:466
  191.3 7.9 %collective-permute-start.26 = (bf16[2,256,512]{2,1,0:T(8,128)(2,1)S(1)}, bf16[2,256,512]{2,1,0:T(8,128)(2,1)S(1)}, u32[]{:S(2)}, u32[]{:S(2)}) collective-permute-start(bf16[2,256,512]{2,1,0:T(8,128)(2,1)S(1)} %pad_maximum_fusion.4.near), channel_id=1, source_target_pairs={{4,8},{6,10},{8,4},{10,6},{5,9},{7,11},{9,5},{11,7},{20,24},{22,26... | collective-permute-start | bytes 1572872 | tf_op jit(solution)/shard_map/ppermute | solution.py:466
  196.6 17.0 %collective-permute-start.31 = (bf16[2,256,512]{2,1,0:T(8,128)(2,1)S(1)}, bf16[2,256,512]{2,1,0:T(8,128)(2,1)S(1)}, u32[]{:S(2)}, u32[]{:S(2)}) collective-permute-start(bf16[2,256,512]{2,1,0:T(8,128)(2,1)S(1)} %collective-permute-done.30.refs_0_), channel_id=1, source_target_pairs={{4,0},{6,2},{8,12},{10,14},{5,1},{7,3},{9,13},{11,15},{20,16},{22,... | collective-permute-start | bytes 1572872 | tf_op jit(solution)/shard_map/ppermute | solution.py:466
  197.9 26.9 %collective-permute-start.22 = (bf16[2,256,512]{2,1,0:T(8,128)(2,1)S(1)}, bf16[2,256,512]{2,1,0:T(8,128)(2,1)S(1)}, u32[]{:S(2)}, u32[]{:S(2)}) collective-permute-start(bf16[2,256,512]{2,1,0:T(8,128)(2,1)S(1)} %collective-permute-done.21.refs_0_), channel_id=1, source_target_pairs={{4,0},{6,2},{8,12},{10,14},{5,1},{7,3},{9,13},{11,15},{20,16},{22,... | collective-permute-start | bytes 1572872 | tf_op jit(solution)/shard_map/ppermute | solution.py:466
  199.2 36.9 %collective-permute-start.27 = (bf16[2,256,512]{2,1,0:T(8,128)(2,1)S(1)}, bf16[2,256,512]{2,1,0:T(8,128)(2,1)S(1)}, u32[]{:S(2)}, u32[]{:S(2)}) collective-permute-start(bf16[2,256,512]{2,1,0:T(8,128)(2,1)S(1)} %collective-permute-done.26.refs_0_), channel_id=1, source_target_pairs={{4,0},{6,2},{8,12},{10,14},{5,1},{7,3},{9,13},{11,15},{20,16},{22,... | collective-permute-start | bytes 1572872 | tf_op jit(solution)/shard_map/ppermute | solution.py:466
  200.6 44.1 %collective-permute-start.17 = (bf16[2,256,512]{2,1,0:T(8,128)(2,1)S(1)}, bf16[2,256,512]{2,1,0:T(8,128)(2,1)S(1)}, u32[]{:S(2)}, u32[]{:S(2)}) collective-permute-start(bf16[2,256,512]{2,1,0:T(8,128)(2,1)S(1)} %collective-permute-done.16.refs_0_), channel_id=1, source_target_pairs={{4,0},{6,2},{8,12},{10,14},{5,1},{7,3},{9,13},{11,15},{20,16},{22,... | collective-permute-start | bytes 1572872 | tf_op jit(solution)/shard_map/ppermute | solution.py:466
  217.1 29.1 %collective-permute-start.32 = (bf16[256,1024]{1,0:T(8,128)(2,1)S(1)}, bf16[256,1024]{1,0:T(8,128)(2,1)S(1)}, u32[]{:S(2)}, u32[]{:S(2)}) collective-permute-start(bf16[256,1024]{1,0:T(8,128)(2,1)S(1)} %get-tuple-element.20), channel_id=1, source_target_pairs={{0,2},{2,0},{4,6},{6,4},{8,10},{10,8},{12,14},{14,12},{1,3},{3,1},... | collective-permute-start | bytes 1572872 | tf_op jit(solution)/shard_map/ppermute | solution.py:466
  228.6 19.2 %collective-permute-start.23 = (bf16[256,1024]{1,0:T(8,128)(2,1)S(1)}, bf16[256,1024]{1,0:T(8,128)(2,1)S(1)}, u32[]{:S(2)}, u32[]{:S(2)}) collective-permute-start(bf16[256,1024]{1,0:T(8,128)(2,1)S(1)} %get-tuple-element.16), channel_id=1, source_target_pairs={{0,2},{2,0},{4,6},{6,4},{8,10},{10,8},{12,14},{14,12},{1,3},{3,1},... | collective-permute-start | bytes 1572872 | tf_op jit(solution)/shard_map/ppermute | solution.py:466
  239.6 10.5 %collective-permute-start.28 = (bf16[256,1024]{1,0:T(8,128)(2,1)S(1)}, bf16[256,1024]{1,0:T(8,128)(2,1)S(1)}, u32[]{:S(2)}, u32[]{:S(2)}) collective-permute-start(bf16[256,1024]{1,0:T(8,128)(2,1)S(1)} %get-tuple-element.18), channel_id=1, source_target_pairs={{0,2},{2,0},{4,6},{6,4},{8,10},{10,8},{12,14},{14,12},{1,3},{3,1},... | collective-permute-start | bytes 1572872 | tf_op jit(solution)/shard_map/ppermute | solution.py:466
  246.2 16.1 %collective-permute-start.19 = (bf16[256,1024]{1,0:T(8,128)(2,1)S(1)}, bf16[256,1024]{1,0:T(8,128)(2,1)S(1)}, u32[]{:S(2)}, u32[]{:S(2)}) collective-permute-start(bf16[256,1024]{1,0:T(8,128)(2,1)S(1)} %project.8), channel_id=1, source_target_pairs={{0,2},{2,0},{4,6},{6,4},{8,10},{10,8},{12,14},{14,12},{1,3},{3,1},... | collective-permute-start | bytes 1572872 | tf_op jit(solution)/shard_map/ppermute | solution.py:466
  246.4 14.9 %collective-permute-start.33 = (bf16[256,1024]{1,0:T(8,128)(2,1)S(1)}, bf16[256,1024]{1,0:T(8,128)(2,1)S(1)}, u32[]{:S(2)}, u32[]{:S(2)}) collective-permute-start(bf16[256,1024]{1,0:T(8,128)(2,1)S(1)} %add_convert_fusion), channel_id=1, source_target_pairs={{0,1},{1,0},{2,3},{3,2},{4,5},{5,4},{6,7},{7,6},{8,9},{9,8},{10,11... | collective-permute-start | bytes 1572872 | tf_op jit(solution)/shard_map/ppermute | solution.py:466
  247.9 24.1 %collective-permute-start.24 = (bf16[256,1024]{1,0:T(8,128)(2,1)S(1)}, bf16[256,1024]{1,0:T(8,128)(2,1)S(1)}, u32[]{:S(2)}, u32[]{:S(2)}) collective-permute-start(bf16[256,1024]{1,0:T(8,128)(2,1)S(1)} %add_convert_fusion.1), channel_id=1, source_target_pairs={{0,1},{1,0},{2,3},{3,2},{4,5},{5,4},{6,7},{7,6},{8,9},{9,8},{10,11... | collective-permute-start | bytes 1572872 | tf_op jit(solution)/shard_map/ppermute | solution.py:466
  (5 other events, 130.2 us)
